TPU v7x, 256 devices: a whole 4x4x8 slice. The times are simulated.
256 devices in a mesh: rows: 64 (over x, z, core), cols: 4 (over y).
Axes of the slice: x: 4, y: 4, z: 8, core: 2. Of those that a mesh axis runs over, the one named last changes fastest.
Arguments:
- hidden_acts: bfloat16 [1, 27648, 2560], P(None, 'rows'), may hold values from -17 to 17
- out_grads: bfloat16 [1, 2560, 5120], P(None, None, 'cols'), may hold values from -13 to 13
- row_signs: int32 [27648], P('rows'), may hold values from -1 to 1, as said below
- kept_index: int32 [16384], P('rows'), may hold values from 0 to 32767, as said below
Outputs:
- sketch: float32 [1, 16384, 5120], P(None, 'rows', 'cols')
Inputs may be any that keep to these rules, and one draw needn't show every extreme that they name: `row_signs`: each entry is +1 or -1. `kept_index`: for each b and each s = 0 .. 63, entries b * 256 + s * 4 to b * 256 + (s + 1) * 4 - 1 are distinct padded rows within b * 512 + s * 8 to b * 512 + (s + 1) * 8 - 1.
All inputs are finite; a program needn't handle non-finite values.
Results may differ from a plain program's by a relative error of at most 0.0003.
Values sent between devices are 32-bit elements; how exact they have to be, the bound alone decides.
No kernel may reach another device: no remote copies, remote signals or barrier semaphores. Data moves between devices by JAX's collectives and lax.ppermute only.
A program may use at most 64 MiB of HBM per device.

v0:
```python
import jax
import jax.numpy as jnp
from jax import lax
from jax.sharding import PartitionSpec as P

D = 5120
PADDED = 32768


epsilon = 1e-06


def partner_2(value, axis, bit):
    mask = 2**bit
    pairs = [(source, source ^ mask) for source in range(lax.axis_size(axis))]
    return lax.ppermute(value, axis, pairs)


def sylvester(length):
    indices = jnp.arange(length, dtype=jnp.int32)
    intersection = indices[:, None] & indices[None, :]
    parity = jnp.zeros_like(intersection)
    for bit_level in range(length.bit_length() - 1):
        parity = parity ^ intersection >> bit_level & 1
    return 1 - 2 * parity


def mix_kept(block_mixed, kept_index, pad_rows):
    row_devices = lax.axis_size("rows")
    position = lax.axis_index("rows")
    mixed_rows = block_mixed
    for bit_level in range(row_devices.bit_length() - 1):
        partner = partner_2(mixed_rows, "rows", bit_level)
        upper_half = position >> bit_level & 1 == 1
        mixed_rows = jnp.where(upper_half, partner - mixed_rows, mixed_rows + partner)
    return jnp.take(mixed_rows, kept_index - position * pad_rows, axis=1)


def local(hidden_acts, out_grads, row_signs, kept_index):
    row_devices = lax.axis_size("rows")
    pad_rows = PADDED // row_devices
    own_rows = hidden_acts.shape[1]
    gradient = jnp.einsum(
        "erl,elc->erc", hidden_acts, out_grads, preferred_element_type=jnp.float32
    )
    local_squares = jnp.sum(gradient * gradient, axis=(1, 2))
    squares_all = lax.psum(local_squares, ("rows", "cols"))
    signed = gradient * row_signs.astype(jnp.float32)[None, :, None]
    padded = jnp.pad(signed, ((0, 0), (0, pad_rows - own_rows), (0, 0)))
    inner_table = sylvester(pad_rows).astype(jnp.float32)
    block_mixed = jnp.einsum("ij,ejc->eic", inner_table, padded, precision=lax.Precision.HIGHEST)
    picked = mix_kept(block_mixed, kept_index, pad_rows)
    inv_norm = lax.rsqrt(squares_all / D + epsilon)
    return picked * inv_norm[:, None, None]


def solution(mesh):
    return jax.shard_map(
        local,
        mesh=mesh,
        in_specs=(P(None, "rows", None), P(None, None, "cols"), P("rows"), P("rows")),
        out_specs=P(None, "rows", "cols"),
        check_vma=False,
    )
```

profile of v0, /device:TPU:1, one launch (start us, length us, event | category | flops | bytes accessed | tf_op | source)
XLA Modules:
  0.0 544.0 jit_solution(14460359535064570303)
XLA Ops:
  0.0 0.8 convert_element_type.8
  0.8 0.8 copy-done
  1.6 6.6 %multiply_reduce_fusion = (f32[]{:T(128)}, f32[1,432,1280]{2,1,0:T(8,128)S(1)}) fusion(f32[432]{0:T(512)S(1)} %convert_element_type.8, bf16[1,2560,1280]{2,1,0:T(8,128)(2,1)} %param.5, bf16[1,432,2560]{2,1,0:T(8,128)(2,1)S(1)} %copy-done), kind=kOutput, calls=%fused_computation.13 | convolution fusion | flops 2832814080 | bytes 10979012 | tf_op jit(solution)/shard_map/erl,elc->erc/dot_general | solution.py:43
  8.2 10.9 %convolution_bitcast_fusion = f32[1,512,1280]{1,2,0:T(8,128)} fusion(f32[1,432,1280]{2,1,0:T(8,128)S(1)} %get-tuple-element.8), kind=kOutput, calls=%fused_computation.3 | convolution fusion | flops 4034396160 | bytes 4833280 | tf_op jit(solution)/shard_map/ij,ejc->eic/dot_general | solution.py:51
  19.1 3.2 collective-permute-start
  22.3 4.9 collective-permute-done
  27.2 4.7 add_select_fusion.4
  31.9 58.4 %collective-permute-done.1 = f32[1,512,1280]{1,2,0:T(8,128)} collective-permute-done((f32[1,512,1280]{1,2,0:T(8,128)}, f32[1,512,1280]{1,2,0:T(8,128)}, u32[]{:S(2)}, u32[]{:S(2)}) %collective-permute-start.1) | collective-permute-done | bytes 2621472 | tf_op jit(solution)/shard_map/ppermute | solution.py:16
  90.2 4.7 add_select_fusion.3
  94.9 1.6 collective-permute-start.2
  96.5 114.3 %collective-permute-done.2 = f32[1,512,1280]{1,2,0:T(8,128)} collective-permute-done((f32[1,512,1280]{1,2,0:T(8,128)}, f32[1,512,1280]{1,2,0:T(8,128)}, u32[]{:S(2)}, u32[]{:S(2)}) %collective-permute-start.2) | collective-permute-done | bytes 2621472 | tf_op jit(solution)/shard_map/ppermute | solution.py:16
  210.8 4.7 add_select_fusion.2
  215.5 5.0 collective-permute-start.3
  220.5 113.5 %collective-permute-done.3 = f32[1,512,1280]{1,2,0:T(8,128)} collective-permute-done((f32[1,512,1280]{1,2,0:T(8,128)}, f32[1,512,1280]{1,2,0:T(8,128)}, u32[]{:S(2)}, u32[]{:S(2)}) %collective-permute-start.3) | collective-permute-done | bytes 2621472 | tf_op jit(solution)/shard_map/ppermute | solution.py:16
  334.0 4.7 add_select_fusion.1
  338.7 1.1 collective-permute-start.4
  339.8 56.0 %collective-permute-done.4 = f32[1,512,1280]{1,2,0:T(8,128)} collective-permute-done((f32[1,512,1280]{1,2,0:T(8,128)}, f32[1,512,1280]{1,2,0:T(8,128)}, u32[]{:S(2)}, u32[]{:S(2)}) %collective-permute-start.4) | collective-permute-done | bytes 2621472 | tf_op jit(solution)/shard_map/ppermute | solution.py:16
  395.8 4.7 add_select_fusion
  400.5 2.7 collective-permute-start.5
  403.2 127.5 %psum.7 = f32[1]{0:T(128)} all-reduce(f32[1]{0:T(128)} %bitcast.9), channel_id=1, replica_groups=mesh['rows'=64,'cols'=4] {'rows','cols'}, use_global_device_ids=true, to_apply=%region_1.0 | all-reduce | flops 1 | bytes 8 | tf_op jit(solution)/shard_map/psum | solution.py:47
  531.4 4.7 select_bitcast_fusion
  536.1 3.2 copy.5
  539.3 3.5 gather_fusion
  542.8 1.2 fusion.5
  (7 shorter events, 0.0 us)
Async XLA Ops:
  0.0 1.6 copy-start
  19.1 8.1 %collective-permute-start = (f32[1,512,1280]{1,2,0:T(8,128)}, f32[1,512,1280]{1,2,0:T(8,128)}, u32[]{:S(2)}, u32[]{:S(2)}) collective-permute-start(f32[1,512,1280]{1,2,0:T(8,128)} %convolution_bitcast_fusion), channel_id=1, source_target_pairs={{0,4},{4,0},{8,12},{12,8},{16,20},{20,16},{24,28},{28,24},{32,36},... | collective-permute-start | bytes 7864328 | tf_op jit(solution)/shard_map/ppermute | solution.py:16
  31.9 58.4 %collective-permute-start.1 = (f32[1,512,1280]{1,2,0:T(8,128)}, f32[1,512,1280]{1,2,0:T(8,128)}, u32[]{:S(2)}, u32[]{:S(2)}) collective-permute-start(f32[1,512,1280]{1,2,0:T(8,128)} %add_select_fusion.4), channel_id=1, source_target_pairs={{0,8},{4,12},{8,0},{12,4},{16,24},{20,28},{24,16},{28,20},{32,40},... | collective-permute-start | bytes 7864328 | tf_op jit(solution)/shard_map/ppermute | solution.py:16
  94.9 115.9 %collective-permute-start.2 = (f32[1,512,1280]{1,2,0:T(8,128)}, f32[1,512,1280]{1,2,0:T(8,128)}, u32[]{:S(2)}, u32[]{:S(2)}) collective-permute-start(f32[1,512,1280]{1,2,0:T(8,128)} %add_select_fusion.3), channel_id=1, source_target_pairs={{0,16},{4,20},{8,24},{12,28},{16,0},{20,4},{24,8},{28,12},{32,48},... | collective-permute-start | bytes 7864328 | tf_op jit(solution)/shard_map/ppermute | solution.py:16
  215.5 118.6 %collective-permute-start.3 = (f32[1,512,1280]{1,2,0:T(8,128)}, f32[1,512,1280]{1,2,0:T(8,128)}, u32[]{:S(2)}, u32[]{:S(2)}) collective-permute-start(f32[1,512,1280]{1,2,0:T(8,128)} %add_select_fusion.2), channel_id=1, source_target_pairs={{0,32},{4,36},{8,40},{12,44},{16,48},{20,52},{24,56},{28,60},{32,0... | collective-permute-start | bytes 7864328 | tf_op jit(solution)/shard_map/ppermute | solution.py:16
  338.7 57.1 %collective-permute-start.4 = (f32[1,512,1280]{1,2,0:T(8,128)}, f32[1,512,1280]{1,2,0:T(8,128)}, u32[]{:S(2)}, u32[]{:S(2)}) collective-permute-start(f32[1,512,1280]{1,2,0:T(8,128)} %add_select_fusion.1), channel_id=1, source_target_pairs={{0,64},{4,68},{8,72},{12,76},{16,80},{20,84},{24,88},{28,92},{32,9... | collective-permute-start | bytes 7864328 | tf_op jit(solution)/shard_map/ppermute | solution.py:16
  339.8 191.5 %copy-start.1 = (s32[256]{0:T(256)S(1)}, s32[256]{0:T(256)}, u32[]{:S(2)}) copy-start(s32[256]{0:T(256)} %param.7) | copy-start | bytes 3076
  400.5 130.9 %collective-permute-start.5 = (f32[1,512,1280]{1,2,0:T(8,128)}, f32[1,512,1280]{1,2,0:T(8,128)}, u32[]{:S(2)}, u32[]{:S(2)}) collective-permute-start(f32[1,512,1280]{1,2,0:T(8,128)} %add_select_fusion), channel_id=1, source_target_pairs={{0,128},{4,132},{8,136},{12,140},{16,144},{20,148},{24,152},{28,15... | collective-permute-start | bytes 7864328 | tf_op jit(solution)/shard_map/ppermute | solution.py:16
where the time goes:
time: 544 us
  waiting for transfers between devices  347 us (64%)
  blocking collectives  127 us (23%)
  other arithmetic  30.1 us (6%)
  matrix products  17.5 us (3%)
  starting transfers between devices  13.7 us (3%)
  local copies, waits for them, and re-layouts  7.56 us (1%)
    ppermute x6, waiting for transfers between devices, partner_2(): return lax.ppermute(value, axis, pairs)  347 us
    psum x1, blocking collectives, local(): squares_all = lax.psum(local_squares, ('rows', 'cols'))  127 us
    select_n x6, other arithmetic, mix_kept(): jnp.where(upper_half, partner - mixed_rows, mixed_rows + partner)  28 us
    ppermute x6, starting transfers between devices, partner_2(): return lax.ppermute(value, axis, pairs)  13.7 us
    dot_general x1, matrix products, local(): jnp.einsum('ij,ejc->eic', inner_table, padded, precision=lax.Precision.HI...  10.9 us
  transfers between devices with their start and end apart: 6, of which 5 were waited for; matrix products, arithmetic and copies ran while one was open for 0% of the time, Pallas kernels for 0%

commit v1 on v0

v1 whole, which is shorter than its diff:
```python
import functools

import jax
import jax.numpy as jnp
import numpy as np
from jax import lax
from jax.experimental import pallas as pl
from jax.experimental.pallas import tpu as pltpu
from jax.sharding import PartitionSpec as P

D = 5120
PADDED = 32768

epsilon = 1e-06


def sylvester(length):
    i = np.arange(length)
    common = i[:, None] & i[None, :]
    parity = np.zeros_like(common)
    for bit in range(length.bit_length() - 1):
        parity ^= common >> bit & 1
    return 1 - 2 * parity


def mix_kernel(segments_ref, position_ref, kept_ref, work_ref):
    blocks = segments_ref.shape[0]
    share = kept_ref.shape[1]
    half = blocks // 8
    for high in range(8):
        rows = [segments_ref[high * half + low] for low in range(half)]
        for bit in (1, 2, 4):
            rows = [
                rows[i ^ bit] - rows[i] if i & bit else rows[i] + rows[i ^ bit]
                for i in range(half)
            ]
        for low in range(half):
            work_ref[high * half + low] = rows[low]
    for low in range(half):
        rows = [work_ref[high * half + low] for high in range(8)]
        for bit in (1, 2, 4):
            rows = [
                rows[i ^ bit] - rows[i] if i & bit else rows[i] + rows[i ^ bit]
                for i in range(8)
            ]
        for high in range(8):
            block = high * half + low
            picked = jnp.take_along_axis(
                rows[high], position_ref[block], axis=0, mode="promise_in_bounds"
            )
            kept_ref[block] = picked[:share]


def mix(segments, position, share):
    blocks, segment, width = segments.shape
    return pl.pallas_call(
        mix_kernel,
        grid=(width // 128,),
        in_specs=[
            pl.BlockSpec((blocks, segment, 128), lambda i: (0, 0, i)),
            pl.BlockSpec((blocks, segment, 128), lambda i: (0, 0, 0)),
        ],
        out_specs=pl.BlockSpec((blocks, share, 128), lambda i: (0, 0, i)),
        out_shape=jax.ShapeDtypeStruct((blocks, share, width), jnp.float32),
        scratch_shapes=[pltpu.VMEM((blocks, segment, 128), jnp.float32)],
    )(segments, position)


def sketch_kernel(col_ref, scale_ref, *refs):
    parts = refs[:-3]
    grads_ref, out_ref, terms_ref = refs[-3:]
    count = len(parts)
    rows, width = parts[0].shape

    @pl.when(pl.program_id(0) == 0)
    def _():
        for shift in range(count):
            source = lax.rem(col_ref[0] + count - shift, count)
            at = pl.ds(pl.multiple_of(source * width, 128), width)
            value = parts[shift][...]
            coarse = value.astype(jnp.bfloat16)
            terms_ref[:rows, at] = coarse
            terms_ref[rows:, at] = (value - coarse.astype(jnp.float32)).astype(jnp.bfloat16)

    both = jnp.dot(terms_ref[...], grads_ref[...], preferred_element_type=jnp.float32)
    out_ref[...] = (both[:rows] + both[rows:]) * scale_ref[0]


def sketch(col, scale, parts, grads):
    rows, width = parts[0].shape
    tokens, columns = grads.shape
    tile = 256
    return pl.pallas_call(
        sketch_kernel,
        grid=(columns // tile,),
        in_specs=[
            pl.BlockSpec(memory_space=pltpu.SMEM),
            pl.BlockSpec(memory_space=pltpu.SMEM),
            *[pl.BlockSpec((rows, width), lambda i: (0, 0))] * len(parts),
            pl.BlockSpec((tokens, tile), lambda i: (0, i)),
        ],
        out_specs=pl.BlockSpec((rows, tile), lambda i: (0, i)),
        out_shape=jax.ShapeDtypeStruct((rows, columns), jnp.float32),
        scratch_shapes=[pltpu.VMEM((2 * rows, tokens), jnp.bfloat16)],
    )(col, scale, *parts, grads)


def col_shift(value, shift):
    cols = lax.axis_size("cols")
    return lax.ppermute(value, "cols", [(c, (c + shift) % cols) for c in range(cols)])


def local(hidden_acts, out_grads, row_signs, kept_index):
    row_devices = lax.axis_size("rows")
    cols = lax.axis_size("cols")
    block = lax.axis_index("rows")
    col = lax.axis_index("cols")
    pad_rows = PADDED // row_devices
    own_rows, tokens = hidden_acts.shape[1:]
    segment = pad_rows // row_devices
    share = kept_index.shape[0] // row_devices
    width = tokens // cols
    acts, grads = hidden_acts[0], out_grads[0]

    table = jnp.asarray(sylvester(pad_rows)[:, :own_rows], dtype=jnp.bfloat16)
    table = table * row_signs.astype(jnp.bfloat16)[None, :]
    own = lax.dynamic_slice(acts, (0, col * width), (own_rows, width))
    inner = jnp.dot(table, own, preferred_element_type=jnp.float32)
    segments = lax.all_to_all(
        inner.reshape(row_devices, segment, width), "rows", 0, 0, tiled=True
    )

    gradient = jnp.dot(acts, grads, preferred_element_type=jnp.float32)
    squares = jnp.sum(gradient * gradient)
    first = block * pad_rows + segment * jnp.arange(row_devices, dtype=jnp.int32)
    position = kept_index.reshape(row_devices, share) - first[:, None]
    notes = jnp.concatenate(
        [
            position.astype(jnp.float32),
            jnp.broadcast_to(squares, (row_devices, 128 - share)),
        ],
        axis=1,
    )
    notes = lax.all_to_all(notes[:, None, :], "rows", 0, 0, tiled=True)
    squares = jnp.broadcast_to(jnp.sum(notes[:, 0, share]), (8, 128))
    squares = squares + lax.ppermute(squares, "cols", [(c, c ^ 1) for c in range(cols)])
    squares = squares + lax.ppermute(squares, "cols", [(c, c ^ 2) for c in range(cols)])
    scale = lax.rsqrt(squares[0, :1] / D + epsilon)
    position = notes[:, 0, :share].astype(jnp.int32)
    position = jnp.pad(position, ((0, 0), (0, segment - share)))
    position = jnp.broadcast_to(position[:, :, None], (row_devices, segment, 128))

    kept = mix(segments, position, share)
    kept = lax.all_to_all(kept, "rows", 0, 0, tiled=True)
    kept = kept.reshape(row_devices * share, width)
    parts = [kept] + [col_shift(kept, shift) for shift in range(1, cols)]
    return sketch(col[None], scale, parts, grads)[None]


def solution(mesh):
    return jax.shard_map(
        local,
        mesh=mesh,
        in_specs=(P(None, "rows", None), P(None, None, "cols"), P("rows"), P("rows")),
        out_specs=P(None, "rows", "cols"),
        check_vma=False,
    )
```

time: 544 us -> 154 us (0.28)
  waiting for transfers between devices: 347 us -> 66.5 us
  blocking collectives: 127 us -> 26.3 us
  other arithmetic: 30.1 us -> 2.14 us
  Pallas kernels: 0 us -> 12.7 us
  starting transfers between devices: 13.7 us -> 26 us
  matrix products: 17.5 us -> 8.28 us
    ppermute x6 -> x5, waiting for transfers between devices: 347 us -> 25.3 us  [the longest x1 24 us: local(): lax.ppermute(squares, 'cols', [(c, c ^ 1) for c in range(cols)])]
    psum x1 -> x0, blocking collectives: 127 us -> none  [local(): squares_all = lax.psum(local_squares, ('rows', 'cols'))]
    all_to_all x0 -> x2, waiting for transfers between devices: none -> 41.2 us  [the longest x1 33.5 us: local(): lax.all_to_all(inner.reshape(row_devices, segment, width), 'rows', 0, 0,...]
    select_n x6 -> x0, other arithmetic: 28 us -> none  [mix_kept(): jnp.where(upper_half, partner - mixed_rows, mixed_rows + partner)]
    all_to_all x0 -> x1, blocking collectives: none -> 26.3 us  [local(): kept = lax.all_to_all(kept, 'rows', 0, 0, tiled=True)]
    all_to_all x0 -> x2, starting transfers between devices: none -> 17.7 us  [the longest x1 13 us: local(): notes = lax.all_to_all(notes[:, None, :], 'rows', 0, 0, tiled=True)]
    pallas_call x0 -> x2, Pallas kernels: none -> 12.7 us  [the longest x1 8.63 us: sketch(): pl.pallas_call(sketch_kernel, grid=(columns // tile,), in_specs=[pl.Block...]
    dot_general x2, matrix products: 17.5 us -> 8.28 us  [the longest x1 6.65 us: local(): gradient = jnp.dot(acts, grads, preferred_element_type=jnp.float32)]
  transfers between devices with their start and end apart: 6 -> 7, of which waited for: 5 -> 4; matrix products, arithmetic and copies ran while one was open for 0% -> 4% of each run, Pallas kernels for 0% -> 0%
where the time goes in v1:
time: 154 us; the launch traced here: 151 us
  waiting for transfers between devices  66.5 us (43%)
  blocking collectives  26.3 us (17%)
  starting transfers between devices  26 us (17%)
  Pallas kernels  12.7 us (8%)
  matrix products  8.28 us (5%)
  local copies, waits for them, and re-layouts  8.17 us (5%)
  other arithmetic  2.14 us (1%)
    all_to_all x1, waiting for transfers between devices, local(): lax.all_to_all(inner.reshape(row_devices, segment, width), 'rows', 0, 0,...  33.5 us
    all_to_all x1, blocking collectives, local(): kept = lax.all_to_all(kept, 'rows', 0, 0, tiled=True)  26.3 us
    ppermute x1, waiting for transfers between devices, local(): lax.ppermute(squares, 'cols', [(c, c ^ 1) for c in range(cols)])  24 us
    all_to_all x1, starting transfers between devices, local(): notes = lax.all_to_all(notes[:, None, :], 'rows', 0, 0, tiled=True)  13 us
    pallas_call x1, Pallas kernels, sketch(): pl.pallas_call(sketch_kernel, grid=(columns // tile,), in_specs=[pl.Block...  8.63 us
    all_to_all x1, waiting for transfers between devices, local(): notes = lax.all_to_all(notes[:, None, :], 'rows', 0, 0, tiled=True)  7.64 us
    dot_general x1, matrix products, local(): gradient = jnp.dot(acts, grads, preferred_element_type=jnp.float32)  6.65 us
    all_to_all x1, starting transfers between devices, local(): lax.all_to_all(inner.reshape(row_devices, segment, width), 'rows', 0, 0,...  4.76 us
  transfers between devices with their start and end apart: 7, of which 4 were waited for; matrix products, arithmetic and copies ran while one was open for 4% of the time, Pallas kernels for 0%

profile of v1, /device:TPU:1, one launch (start us, length us, event | category | flops | bytes accessed | tf_op | source)
XLA Modules:
  0.0 151.0 jit_solution(5219439342240956294)
XLA Ops:
  0.0 0.9 reshape.22
  0.9 0.7 copy-done
  1.6 6.6 %fusion.1 = f32[]{:T(128)} fusion(bf16[1,432,2560]{2,1,0:T(8,128)(2,1)S(1)} %copy-done, bf16[1,2560,1280]{2,1,0:T(8,128)(2,1)} %param.6), kind=kOutput, calls=%fused_computation.2 | convolution fusion | flops 2832261120 | bytes 8765444 | tf_op jit(solution)/shard_map/dot_general | solution.py:133
  8.4 1.3 concatenate.3
  9.6 13.0 %all-to-all-start = ((f32[64,1,128]{2,1,0:T(1,128)}), f32[64,1,128]{2,1,0:T(1,128)S(1)}, u32[]{:S(2)}, u32[]{:S(2)}) async-start(f32[64,1,128]{2,1,0:T(1,128)} %bitcast.4), calls=%async_computation | async-start | bytes 65536 | tf_op jit(solution)/shard_map/all_to_all | solution.py:144
  22.6 1.6 %fusion.4 = f32[64,8,640]{2,1,0:T(8,128)} fusion(bf16[1,432,2560]{2,1,0:T(8,128)(2,1)S(1)} %copy-done, s32[]{:T(128)S(6)} %select_n.3, bf16[512,432]{1,0:T(8,128)(2,1)S(1)} %copy-done.6, bf16[432]{0:T(512)(128)(2,1)S(1)} %convert_element_type.13), kind=kOutput, calls=%fused_computation.3 | convolution fusion | flops 283336704 | bytes 2388996 | tf_op jit(solution)/shard_map/dot_general | solution.py:128
  24.3 7.6 %all-to-all-done = f32[64,1,128]{2,1,0:T(1,128)S(1)} async-done(((f32[64,1,128]{2,1,0:T(1,128)}), f32[64,1,128]{2,1,0:T(1,128)S(1)}, u32[]{:S(2)}, u32[]{:S(2)}) %all-to-all-start) | async-done | bytes 32800 | tf_op jit(solution)/shard_map/all_to_all | solution.py:144
  31.9 4.8 %all-to-all-start.1 = ((f32[64,8,640]{2,1,0:T(8,128)}), f32[64,8,640]{2,1,0:T(8,128)S(1)}, u32[]{:S(2)}, u32[]{:S(2)}) async-start(f32[64,8,640]{2,1,0:T(8,128)} %fusion.4), calls=%async_computation.1 | async-start | bytes 2621440 | tf_op jit(solution)/shard_map/all_to_all | solution.py:129
  37.3 33.5 %all-to-all-done.1.segments_ref = f32[64,8,640]{2,1,0:T(8,128)S(1)} async-done(((f32[64,8,640]{2,1,0:T(8,128)}), f32[64,8,640]{2,1,0:T(8,128)S(1)}, u32[]{:S(2)}, u32[]{:S(2)}) %all-to-all-start.1) | async-done | bytes 1310752 | tf_op jit(solution)/shard_map/all_to_all | solution.py:129
  70.9 1.6 %broadcast_in_dim.24.position_ref = s32[64,8,128]{2,1,0:T(8,128)} broadcast(s32[64,8]{1,0:T(8,128)} %pad.5), dimensions={0,1} | broadcast | bytes 264192 | tf_op jit(solution)/shard_map/broadcast_in_dim | solution.py:151
  72.5 4.1 %shard_map.55 = f32[64,4,640]{2,1,0:T(4,128)} custom-call(f32[64,8,640]{2,1,0:T(8,128)} %copy-done.1, s32[64,8,128]{2,1,0:T(8,128)} %broadcast_in_dim.24.position_ref), custom_call_target="tpu_custom_call" | custom-call | tf_op jit(solution)/shard_map/pallas_call | solution.py:56
  76.5 26.3 %all_to_all.15 = f32[64,4,640]{2,1,0:T(4,128)S(1)} all-to-all(f32[64,4,640]{2,1,0:T(4,128)} %shard_map.55), channel_id=1, replica_groups=mesh['rows'=64,'cols'=4] {'rows'}, dimensions={0} | all-to-all | bytes 1310720 | tf_op jit(solution)/shard_map/all_to_all | solution.py:154
  103.1 2.8 %collective-permute-start.4 = (f32[256,640]{1,0:T(8,128)S(1)}, f32[256,640]{1,0:T(8,128)S(1)}, u32[]{:S(2)}, u32[]{:S(2)}) collective-permute-start(f32[256,640]{1,0:T(8,128)S(1)} %reshape.23.refs_0_), channel_id=1, source_target_pairs={{0,3},{1,0},{2,1},{3,2},{4,7},{5,4},{6,5},{7,6},{8,11},{9,8},{10,9... | collective-permute-start | bytes 1966088 | tf_op jit(solution)/shard_map/ppermute | solution.py:110
  106.3 0.7 collective-permute-start.2
  107.0 0.7 slice_reduce_fusion
  108.4 1.7 %collective-permute-start = (f32[8,128]{1,0:T(8,128)S(1)}, f32[8,128]{1,0:T(8,128)S(1)}, u32[]{:S(2)}, u32[]{:S(2)}) collective-permute-start(f32[8,128]{1,0:T(8,128)S(1)} %broadcast_in_dim.23), channel_id=1, source_target_pairs={{0,1},{1,0},{2,3},{3,2},{4,5},{5,4},{6,7},{7,6},{8,9},{9,8},{10,11... | collective-permute-start | bytes 12296 | tf_op jit(solution)/shard_map/ppermute | solution.py:146
  110.0 24.0 %collective-permute-done = f32[8,128]{1,0:T(8,128)S(1)} collective-permute-done((f32[8,128]{1,0:T(8,128)S(1)}, f32[8,128]{1,0:T(8,128)S(1)}, u32[]{:S(2)}, u32[]{:S(2)}) %collective-permute-start) | collective-permute-done | bytes 4128 | tf_op jit(solution)/shard_map/ppermute | solution.py:146
  134.0 0.6 broadcast_add_fusion
  134.7 2.7 %collective-permute-start.1 = (f32[8,128]{1,0:T(8,128)S(1)}, f32[8,128]{1,0:T(8,128)S(1)}, u32[]{:S(2)}, u32[]{:S(2)}) collective-permute-start(f32[8,128]{1,0:T(8,128)S(1)} %broadcast_add_fusion), channel_id=1, source_target_pairs={{0,2},{1,3},{2,0},{3,1},{4,6},{5,7},{6,4},{7,5},{8,10},{9,11},{10,... | collective-permute-start | bytes 12296 | tf_op jit(solution)/shard_map/ppermute | solution.py:147
  137.4 1.3 collective-permute-done.1
  138.7 0.6 fusion.12
  140.6 0.8 copy-done.4
  141.5 0.8 copy-done.5
  142.3 8.6 %shard_map.56 = f32[256,1280]{1,0:T(8,128)} custom-call(s32[1]{0:T(128)} %bitcast.col_ref, f32[1]{0:T(128)} %bitcast.5.scale_ref, f32[256,640]{1,0:T(8,128)} %copy-done.2, f32[256,640]{1,0:T(8,128)} %copy-done.5, f32[256,640]{1,0:T(8,128)} %copy-done.4, f32[256,640]{1,0:T(8,128)} %copy-done.3, bf16[2560,1280]{1,0:T(8,128)(2,1)} %bitcast.22), custom_call_target="tpu_custom_call" | custom-call | tf_op jit(solution)/shard_map/pallas_call | solution.py:93
  (25 shorter events, 2.5 us)
Async XLA Ops:
  0.0 1.6 %copy-start = (bf16[1,432,2560]{2,1,0:T(8,128)(2,1)S(1)}, bf16[1,432,2560]{2,1,0:T(8,128)(2,1)}, u32[]{:S(2)}) copy-start(bf16[1,432,2560]{2,1,0:T(8,128)(2,1)} %param.5) | copy-start | bytes 6635524
  1.6 21.0 %copy-start.7 = (s32[432]{0:T(512)S(1)}, s32[432]{0:T(512)}, u32[]{:S(2)}) copy-start(s32[432]{0:T(512)} %param.7) | copy-start | bytes 5188
  1.6 21.0 %copy-start.6 = (bf16[512,432]{1,0:T(8,128)(2,1)S(1)}, bf16[512,432]{1,0:T(8,128)(2,1)}, u32[]{:S(2)}) copy-start(bf16[512,432]{1,0:T(8,128)(2,1)} %constant.31.clone) | copy-start | bytes 1327108
  9.6 22.3 %all-to-all-start = ((f32[64,1,128]{2,1,0:T(1,128)}), f32[64,1,128]{2,1,0:T(1,128)S(1)}, u32[]{:S(2)}, u32[]{:S(2)}) async-start(f32[64,1,128]{2,1,0:T(1,128)} %bitcast.4), calls=%async_computation | async-start | bytes 65536 | tf_op jit(solution)/shard_map/all_to_all | solution.py:144
  31.9 39.0 %all-to-all-start.1 = ((f32[64,8,640]{2,1,0:T(8,128)}), f32[64,8,640]{2,1,0:T(8,128)S(1)}, u32[]{:S(2)}, u32[]{:S(2)}) async-start(f32[64,8,640]{2,1,0:T(8,128)} %fusion.4), calls=%async_computation.1 | async-start | bytes 2621440 | tf_op jit(solution)/shard_map/all_to_all | solution.py:129
  70.9 1.6 %copy-start.1 = (f32[64,8,640]{2,1,0:T(8,128)}, f32[64,8,640]{2,1,0:T(8,128)S(1)}, u32[]{:S(2)}) copy-start(f32[64,8,640]{2,1,0:T(8,128)S(1)} %all-to-all-done.1.segments_ref) | copy-start | bytes 3932164
  103.1 39.2 %copy-start.2 = (f32[256,640]{1,0:T(8,128)}, f32[256,640]{1,0:T(8,128)S(1)}, u32[]{:S(2)}) copy-start(f32[256,640]{1,0:T(8,128)S(1)} %reshape.23.refs_0_) | copy-start | bytes 1966084
  103.1 37.5 %collective-permute-start.4 = (f32[256,640]{1,0:T(8,128)S(1)}, f32[256,640]{1,0:T(8,128)S(1)}, u32[]{:S(2)}, u32[]{:S(2)}) collective-permute-start(f32[256,640]{1,0:T(8,128)S(1)} %reshape.23.refs_0_), channel_id=1, source_target_pairs={{0,3},{1,0},{2,1},{3,2},{4,7},{5,4},{6,5},{7,6},{8,11},{9,8},{10,9... | collective-permute-start | bytes 1966088 | tf_op jit(solution)/shard_map/ppermute | solution.py:110
  105.9 34.7 %collective-permute-start.3 = (f32[256,640]{1,0:T(8,128)S(1)}, f32[256,640]{1,0:T(8,128)S(1)}, u32[]{:S(2)}, u32[]{:S(2)}) collective-permute-start(f32[256,640]{1,0:T(8,128)S(1)} %reshape.23.refs_0_), channel_id=1, source_target_pairs={{0,2},{1,3},{2,0},{3,1},{4,6},{5,7},{6,4},{7,5},{8,10},{9,11},{10,... | collective-permute-start | bytes 1966088 | tf_op jit(solution)/shard_map/ppermute | solution.py:110
  106.3 34.4 %collective-permute-start.2 = (f32[256,640]{1,0:T(8,128)S(1)}, f32[256,640]{1,0:T(8,128)S(1)}, u32[]{:S(2)}, u32[]{:S(2)}) collective-permute-start(f32[256,640]{1,0:T(8,128)S(1)} %reshape.23.refs_0_), channel_id=1, source_target_pairs={{0,1},{1,2},{2,3},{3,0},{4,5},{5,6},{6,7},{7,4},{8,9},{9,10},{10,1... | collective-permute-start | bytes 1966088 | tf_op jit(solution)/shard_map/ppermute | solution.py:110
  108.4 25.7 %collective-permute-start = (f32[8,128]{1,0:T(8,128)S(1)}, f32[8,128]{1,0:T(8,128)S(1)}, u32[]{:S(2)}, u32[]{:S(2)}) collective-permute-start(f32[8,128]{1,0:T(8,128)S(1)} %broadcast_in_dim.23), channel_id=1, source_target_pairs={{0,1},{1,0},{2,3},{3,2},{4,5},{5,4},{6,7},{7,6},{8,9},{9,8},{10,11... | collective-permute-start | bytes 12296 | tf_op jit(solution)/shard_map/ppermute | solution.py:146
  134.7 4.0 %collective-permute-start.1 = (f32[8,128]{1,0:T(8,128)S(1)}, f32[8,128]{1,0:T(8,128)S(1)}, u32[]{:S(2)}, u32[]{:S(2)}) collective-permute-start(f32[8,128]{1,0:T(8,128)S(1)} %broadcast_add_fusion), channel_id=1, source_target_pairs={{0,2},{1,3},{2,0},{3,1},{4,6},{5,7},{6,4},{7,5},{8,10},{9,11},{10,... | collective-permute-start | bytes 12296 | tf_op jit(solution)/shard_map/ppermute | solution.py:147
  140.6 1.7 %copy-start.3 = (f32[256,640]{1,0:T(8,128)}, f32[256,640]{1,0:T(8,128)S(1)}, u32[]{:S(2)}) copy-start(f32[256,640]{1,0:T(8,128)S(1)} %collective-permute-done.4.refs_3_) | copy-start | bytes 1966084
  140.6 0.9 copy-start.4
  141.5 0.8 copy-start.5

commit v2 on v0

v2 whole, which is shorter than its diff:
```python
import functools

import jax
import jax.numpy as jnp
import numpy as np
from jax import lax
from jax.experimental import pallas as pl
from jax.experimental.pallas import tpu as pltpu
from jax.sharding import PartitionSpec as P


D = 5120
PADDED = 32768

epsilon = 1e-06


def sylvester(length):
    i = np.arange(length)
    common = i[:, None] & i[None, :]
    parity = np.zeros_like(common)
    for bit in range(length.bit_length() - 1):
        parity ^= common >> bit & 1
    return 1 - 2 * parity


LANES = 128
SUBLANES = 8
CHUNKS = (640,)

WHOLE = pl.BlockSpec(memory_space=pltpu.VMEM)
SCALAR = pl.BlockSpec(memory_space=pltpu.SMEM)


def butterfly(rows):
    count = len(rows)
    bit = 1
    while bit < count:
        rows = [
            rows[i ^ bit] - rows[i] if i & bit else rows[i] + rows[i ^ bit]
            for i in range(count)
        ]
        bit *= 2
    return rows


def inner_kernel(blocks, col_ref, table_ref, signs_ref, kept_ref, acts_ref, out_ref):
    tiles = acts_ref.shape[2] // LANES
    stride = tiles * SUBLANES + 1
    table = table_ref[...] * signs_ref[...].astype(jnp.float32).astype(jnp.bfloat16)
    mixed = jnp.dot(table, acts_ref[0], preferred_element_type=jnp.float32)
    kept = kept_ref[...].astype(jnp.float32)
    share = kept.size // blocks
    for block in range(blocks):
        rows = slice(block * SUBLANES, (block + 1) * SUBLANES)
        for tile in range(tiles):
            out_ref[pl.ds(block * stride + tile * SUBLANES, SUBLANES), :] = mixed[
                rows, tile * LANES:(tile + 1) * LANES
            ]
        row = block * share // LANES
        out_ref[pl.ds((block + 1) * stride - 1, 1), :] = kept[row:row + 1]


def inner(col, table, signs, kept, acts, blocks, width):
    own_rows = acts.shape[1]
    rows = blocks * (width // LANES * SUBLANES + 1)
    return pl.pallas_call(
        functools.partial(inner_kernel, blocks),
        grid_spec=pltpu.PrefetchScalarGridSpec(
            num_scalar_prefetch=1,
            grid=(1,),
            in_specs=[
                pl.BlockSpec(table.shape, lambda i, c: (0, 0)),
                pl.BlockSpec(signs.shape, lambda i, c: (0, 0)),
                pl.BlockSpec(kept.shape, lambda i, c: (0, 0)),
                pl.BlockSpec((1, own_rows, width), lambda i, c: (0, 0, c[0])),
            ],
            out_specs=pl.BlockSpec((rows, LANES), lambda i, c: (0, 0)),
        ),
        out_shape=jax.ShapeDtypeStruct((rows, LANES), jnp.float32),
    )(col, table, signs, kept, acts)


def mix_kernel(first, tiles, block_ref, segments_ref, kept_ref, position_ref, work_ref):
    blocks, share, width = kept_ref.shape
    low_count = blocks // 8
    stride = tiles * SUBLANES + 1

    sublane = lax.broadcasted_iota(jnp.int32, (SUBLANES, LANES), 0)
    lane = lax.rem(block_ref[0], LANES // share) * share + jnp.minimum(sublane, share - 1)
    for block in range(blocks):
        row = segments_ref[pl.ds((block + 1) * stride - 1, 1), :]
        row = jnp.broadcast_to(row, (SUBLANES, LANES)).astype(jnp.int32) & (SUBLANES - 1)
        position_ref[block] = jnp.take_along_axis(
            row, lane, axis=1, mode="promise_in_bounds"
        )

    for tile in range(width // LANES):
        at = slice(tile * LANES, (tile + 1) * LANES)
        for high in range(8):
            rows = butterfly(
                [
                    segments_ref[
                        pl.ds(
                            (high * low_count + low) * stride + (first + tile) * SUBLANES,
                            SUBLANES,
                        ),
                        :,
                    ]
                    for low in range(low_count)
                ]
            )
            for low in range(low_count):
                work_ref[high * low_count + low] = rows[low]
        for low in range(low_count):
            rows = butterfly([work_ref[high * low_count + low] for high in range(8)])
            for high in range(8):
                block = high * low_count + low
                picked = jnp.take_along_axis(
                    rows[high], position_ref[block], axis=0, mode="promise_in_bounds"
                )
                kept_ref[block, :, at] = picked[:share]


def mix(block, segments, blocks, share, tiles, start, width):
    return pl.pallas_call(
        functools.partial(mix_kernel, start // LANES, tiles),
        in_specs=[SCALAR, WHOLE],
        out_specs=WHOLE,
        out_shape=jax.ShapeDtypeStruct((blocks, share, width), jnp.float32),
        scratch_shapes=[
            pltpu.VMEM((blocks, SUBLANES, LANES), jnp.int32),
            pltpu.VMEM((blocks, SUBLANES, LANES), jnp.float32),
        ],
    )(block, segments)


def product_kernel(group, offset, count, col_ref, *refs):
    parts = refs[:count]
    total_ref = refs[count] if offset else None
    last = offset + parts[0].shape[1] == group
    squares_ref = refs[-4] if last else None
    grads_ref, out_ref, terms_ref = refs[-3:]
    rows, width = parts[0].shape

    @pl.when(pl.program_id(0) == 0)
    def _():
        for shift in range(count):
            value = parts[shift][...]
            coarse = value.astype(jnp.bfloat16)
            at = slice(shift * width, (shift + 1) * width)
            terms_ref[:rows, at] = coarse
            terms_ref[rows:, at] = (value - coarse.astype(jnp.float32)).astype(jnp.bfloat16)

    both = None
    for shift in range(count):
        source = lax.rem(col_ref[0] + count - shift, count)
        at = pl.ds(pl.multiple_of(source * group + offset, LANES), width)
        step = jnp.dot(
            terms_ref[:, shift * width:(shift + 1) * width],
            grads_ref[at, :],
            preferred_element_type=jnp.float32,
        )
        both = step if both is None else both + step
    value = both[:rows] + both[rows:]
    if offset:
        value = value + total_ref[...]
    if last:
        squares = jnp.sum(squares_ref[...], axis=0)
        scale = lax.rsqrt(squares / D + epsilon)
        value = value * jnp.tile(scale, (1, value.shape[1] // LANES))
    out_ref[...] = value


def product(group, offset, col, parts, total, squares, grads):
    rows, width = parts[0].shape
    tokens, columns = grads.shape
    tile = 256
    column_tile = pl.BlockSpec((rows, tile), lambda i: (0, i))
    totals = [total] if offset else []
    norms = [squares] if offset + width == group else []
    return pl.pallas_call(
        functools.partial(product_kernel, group, offset, len(parts)),
        grid=(columns // tile,),
        in_specs=[
            SCALAR,
            *[WHOLE] * len(parts),
            *[column_tile] * len(totals),
            *[WHOLE] * len(norms),
            pl.BlockSpec((tokens, tile), lambda i: (0, i)),
        ],
        out_specs=column_tile,
        out_shape=jax.ShapeDtypeStruct((rows, columns), jnp.float32),
        scratch_shapes=[pltpu.VMEM((2 * rows, len(parts) * width), jnp.bfloat16)],
    )(col, *parts, *totals, *norms, grads)


def col_shift(value, shift):
    cols = lax.axis_size("cols")
    return lax.ppermute(value, "cols", [(c, (c + shift) % cols) for c in range(cols)])


def exchange(value):
    return lax.all_to_all(value, "rows", 0, 0, tiled=True)


def staged(hidden_acts, out_grads, row_signs, kept_index):
    row_devices = lax.axis_size("rows")
    cols = lax.axis_size("cols")
    block = lax.axis_index("rows")
    col = lax.axis_index("cols")[None]
    pad_rows = PADDED // row_devices
    own_rows, tokens = hidden_acts.shape[1:]
    share = kept_index.shape[0] // row_devices
    group = tokens // cols
    tiles = group // LANES
    grads = out_grads[0]

    table = jnp.asarray(sylvester(pad_rows)[:, :own_rows], dtype=jnp.bfloat16)
    segments = inner(
        col,
        table,
        row_signs[None],
        kept_index.reshape(-1, LANES),
        hidden_acts,
        row_devices,
        group,
    )
    segments = exchange(segments.reshape(row_devices, 1, -1)).reshape(-1, LANES)

    gradient = jnp.dot(hidden_acts[0], grads, preferred_element_type=jnp.float32)
    squares = jnp.sum(gradient * gradient)
    squares = jnp.broadcast_to(squares, (SUBLANES, LANES))
    for bit in (1, 2):
        squares = squares + lax.ppermute(
            squares, "cols", [(c, c ^ bit) for c in range(cols)]
        )
    squares = jnp.broadcast_to(squares[:1], (row_devices, 1, LANES))
    squares = exchange(squares)

    total, start = None, 0
    for width in CHUNKS:
        kept = mix(block[None], segments, row_devices, share, tiles, start, width)
        kept = exchange(kept)
        kept = kept.reshape(row_devices * share, width)
        parts = [kept]
        for shift in range(1, cols):
            parts.append(col_shift(kept, shift))
        total = product(group, start, col, parts, total, squares, grads)
        start += width
    return total[None]


def solution(mesh):
    return jax.shard_map(
        staged,
        mesh=mesh,
        in_specs=(P(None, "rows", None), P(None, None, "cols"), P("rows"), P("rows")),
        out_specs=P(None, "rows", "cols"),
        check_vma=False,
    )
```

time: 544 us -> 143 us (0.26)
  waiting for transfers between devices: 347 us -> 73.7 us
  blocking collectives: 127 us -> 16.4 us
  other arithmetic: 30.1 us -> 1.24 us
  Pallas kernels: 0 us -> 14.7 us
  starting transfers between devices: 13.7 us -> 26.4 us
  matrix products: 17.5 us -> 6.65 us
    ppermute x6 -> x5, waiting for transfers between devices: 347 us -> 27.5 us  [the longest x2 27.5 us: staged(): lax.ppermute(squares, 'cols', [(c, c ^ bit) for c in range(cols)])]
    psum x1 -> x0, blocking collectives: 127 us -> none  [local(): squares_all = lax.psum(local_squares, ('rows', 'cols'))]
    all_to_all x0 -> x2, waiting for transfers between devices: none -> 46.3 us  [exchange(): return lax.all_to_all(value, 'rows', 0, 0, tiled=True)]
    select_n x6 -> x0, other arithmetic: 28 us -> none  [mix_kept(): jnp.where(upper_half, partner - mixed_rows, mixed_rows + partner)]
    all_to_all x0 -> x2, starting transfers between devices: none -> 19.1 us  [exchange(): return lax.all_to_all(value, 'rows', 0, 0, tiled=True)]
    all_to_all x0 -> x1, blocking collectives: none -> 16.4 us  [exchange(): return lax.all_to_all(value, 'rows', 0, 0, tiled=True)]
    pallas_call x0 -> x3, Pallas kernels: none -> 14.7 us  [the longest x1 9.05 us: product(): pl.pallas_call(functools.partial(product_kernel, group, offset, len(parts...]
    dot_general x2 -> x1, matrix products: 17.5 us -> 6.65 us  [staged(): jnp.dot(hidden_acts[0], grads, preferred_element_type=jnp.float32)]
  transfers between devices with their start and end apart: 6 -> 7, of which waited for: 5 -> 3; matrix products, arithmetic and copies ran while one was open for 0% -> 6% of each run, Pallas kernels for 0% -> 0%
where the time goes in v2:
time: 143 us; the launch traced here: 142 us
  waiting for transfers between devices  73.7 us (52%)
  starting transfers between devices  26.4 us (18%)
  blocking collectives  16.4 us (11%)
  Pallas kernels  14.7 us (10%)
  matrix products  6.65 us (5%)
  local copies, waits for them, and re-layouts  3.22 us (2%)
    all_to_all x2, waiting for transfers between devices, exchange(): return lax.all_to_all(value, 'rows', 0, 0, tiled=True)  46.3 us
    ppermute x2, waiting for transfers between devices, staged(): lax.ppermute(squares, 'cols', [(c, c ^ bit) for c in range(cols)])  27.5 us
    all_to_all x2, starting transfers between devices, exchange(): return lax.all_to_all(value, 'rows', 0, 0, tiled=True)  19.1 us
    all_to_all x1, blocking collectives, exchange(): return lax.all_to_all(value, 'rows', 0, 0, tiled=True)  16.4 us
    pallas_call x1, Pallas kernels, product(): pl.pallas_call(functools.partial(product_kernel, group, offset, len(parts...  9.05 us
    dot_general x1, matrix products, staged(): jnp.dot(hidden_acts[0], grads, preferred_element_type=jnp.float32)  6.65 us
    ppermute x3, starting transfers between devices, col_shift(): lax.ppermute(value, 'cols', [(c, (c + shift) % cols) for c in range(cols)])  3.85 us
    ppermute x2, starting transfers between devices, staged(): lax.ppermute(squares, 'cols', [(c, c ^ bit) for c in range(cols)])  3.4 us
  transfers between devices with their start and end apart: 7, of which 3 were waited for; matrix products, arithmetic and copies ran while one was open for 6% of the time, Pallas kernels for 0%

profile of v2, /device:TPU:1, one launch (start us, length us, event | category | flops | bytes accessed | tf_op | source)
XLA Modules:
  0.0 142.4 jit_solution(2805383457901504583)
XLA Ops:
  0.0 2.9 %shard_map.55 = f32[2624,128]{1,0:T(8,128)} custom-call(s32[1]{0:T(128)} %bitcast.col_ref, bf16[512,432]{1,0:T(8,128)(2,1)} %constant.13.clone.table_ref, s32[1,432]{1,0:T(1,128)} %bitcast.20, s32[2,128]{1,0:T(2,128)} %bitcast.21, bf16[1,432,2560]{2,1,0:T(8,128)(2,1)} %acts_ref.1), custom_call_target="tpu_custom_call" | custom-call | tf_op jit(solution)/shard_map/pallas_call | solution.py:67
  2.9 13.0 %all-to-all-start = ((f32[64,1,5248]{2,1,0:T(1,128)}), f32[64,1,5248]{2,1,0:T(1,128)S(1)}, u32[]{:S(2)}, u32[]{:S(2)}) async-start(f32[64,1,5248]{2,1,0:T(1,128)} %bitcast.19), calls=%async_computation | async-start | bytes 2686976 | tf_op jit(solution)/shard_map/all_to_all | solution.py:204
  15.9 0.0 copy-start.2
  15.9 34.8 %all-to-all-done = f32[64,1,5248]{2,1,0:T(1,128)S(1)} async-done(((f32[64,1,5248]{2,1,0:T(1,128)}), f32[64,1,5248]{2,1,0:T(1,128)S(1)}, u32[]{:S(2)}, u32[]{:S(2)}) %all-to-all-start) | async-done | bytes 1343520 | tf_op jit(solution)/shard_map/all_to_all | solution.py:204
  50.7 1.1 copy-done
  51.8 2.7 %shard_map.56 = f32[64,4,640]{2,1,0:T(4,128)} custom-call(s32[1]{0:T(128)} %bitcast.1.block_ref, f32[2624,128]{1,0:T(8,128)} %bitcast.18), custom_call_target="tpu_custom_call" | custom-call | tf_op jit(solution)/shard_map/pallas_call | solution.py:126
  54.5 6.2 %all-to-all-start.1 = ((f32[64,4,640]{2,1,0:T(4,128)}), f32[64,4,640]{2,1,0:T(4,128)S(1)}, u32[]{:S(2)}, u32[]{:S(2)}) async-start(f32[64,4,640]{2,1,0:T(4,128)} %shard_map.56), calls=%async_computation.1 | async-start | bytes 1310720 | tf_op jit(solution)/shard_map/all_to_all | solution.py:204
  60.7 6.6 %fusion.1 = f32[]{:T(128)} fusion(bf16[1,432,2560]{2,1,0:T(8,128)(2,1)S(1)} %copy-done.2, bf16[1,2560,1280]{2,1,0:T(8,128)(2,1)} %param.6), kind=kOutput, calls=%fused_computation.2 | convolution fusion | flops 2832261120 | bytes 8765444 | tf_op jit(solution)/shard_map/dot_general | solution.py:231
  67.4 0.6 broadcast_in_dim.21
  68.0 1.4 collective-permute-start.3
  69.4 11.4 %all-to-all-done.1 = f32[64,4,640]{2,1,0:T(4,128)S(1)} async-done(((f32[64,4,640]{2,1,0:T(4,128)}), f32[64,4,640]{2,1,0:T(4,128)S(1)}, u32[]{:S(2)}, u32[]{:S(2)}) %all-to-all-start.1) | async-done | bytes 655392 | tf_op jit(solution)/shard_map/all_to_all | solution.py:204
  80.8 0.2 reshape.16.refs_0_
  81.0 2.8 %collective-permute-start.2 = (f32[256,640]{1,0:T(8,128)S(1)}, f32[256,640]{1,0:T(8,128)S(1)}, u32[]{:S(2)}, u32[]{:S(2)}) collective-permute-start(f32[256,640]{1,0:T(8,128)S(1)} %reshape.16.refs_0_), channel_id=1, source_target_pairs={{0,3},{1,0},{2,1},{3,2},{4,7},{5,4},{6,5},{7,6},{8,11},{9,8},{10,9... | collective-permute-start | bytes 1966088 | tf_op jit(solution)/shard_map/ppermute | solution.py:200
  83.8 0.3 collective-permute-start.1
  84.2 0.7 collective-permute-start
  84.9 0.6 broadcast_add_fusion
  85.5 2.0 %collective-permute-start.4 = (f32[8,128]{1,0:T(8,128)S(1)}, f32[8,128]{1,0:T(8,128)S(1)}, u32[]{:S(2)}, u32[]{:S(2)}) collective-permute-start(f32[8,128]{1,0:T(8,128)S(1)} %broadcast_add_fusion), channel_id=1, source_target_pairs={{0,2},{1,3},{2,0},{3,1},{4,6},{5,7},{6,4},{7,5},{8,10},{9,11},{10,... | collective-permute-start | bytes 12296 | tf_op jit(solution)/shard_map/ppermute | solution.py:235
  87.5 27.5 %collective-permute-done.4 = f32[8,128]{1,0:T(8,128)S(1)} collective-permute-done((f32[8,128]{1,0:T(8,128)S(1)}, f32[8,128]{1,0:T(8,128)S(1)}, u32[]{:S(2)}, u32[]{:S(2)}) %collective-permute-start.4) | collective-permute-done | bytes 4128 | tf_op jit(solution)/shard_map/ppermute | solution.py:235
  115.0 0.6 fusion.5
  115.7 16.4 %all_to_all.15.refs_4_ = f32[64,1,128]{2,1,0:T(1,128)} all-to-all(f32[64,1,128]{2,1,0:T(1,128)S(1)} %broadcast_in_dim.22), channel_id=1, replica_groups=mesh['rows'=64,'cols'=4] {'rows'}, dimensions={0} | all-to-all | bytes 65536 | tf_op jit(solution)/shard_map/all_to_all | solution.py:204
  132.1 0.8 copy-done.3
  132.9 0.2 copy-done.4
  133.1 0.2 copy-done.5
  133.4 9.1 %shard_map.57 = f32[256,1280]{1,0:T(8,128)} custom-call(s32[1]{0:T(128)} %bitcast.col_ref, f32[256,640]{1,0:T(8,128)} %copy-done.1, f32[256,640]{1,0:T(8,128)} %copy-done.5, f32[256,640]{1,0:T(8,128)} %copy-done.4, f32[256,640]{1,0:T(8,128)} %copy-done.3, f32[64,1,128]{2,1,0:T(1,128)} %all_to_all.15.refs_4_, bf16[2560,1280]{1,0:T(8,128)(2,1)} %bitcast.17), custom_call_target="tpu_custom_call" | custom-call | tf_op jit(solution)/shard_map/pallas_call | solution.py:182
  (13 shorter events, 0.0 us)
Async XLA Ops:
  2.9 47.8 %all-to-all-start = ((f32[64,1,5248]{2,1,0:T(1,128)}), f32[64,1,5248]{2,1,0:T(1,128)S(1)}, u32[]{:S(2)}, u32[]{:S(2)}) async-start(f32[64,1,5248]{2,1,0:T(1,128)} %bitcast.19), calls=%async_computation | async-start | bytes 2686976 | tf_op jit(solution)/shard_map/all_to_all | solution.py:204
  15.9 44.8 %copy-start.2 = (bf16[1,432,2560]{2,1,0:T(8,128)(2,1)S(1)}, bf16[1,432,2560]{2,1,0:T(8,128)(2,1)}, u32[]{:S(2)}) copy-start(bf16[1,432,2560]{2,1,0:T(8,128)(2,1)} %acts_ref.1) | copy-start | bytes 6635524
  50.7 1.1 copy-start
  54.5 26.3 %all-to-all-start.1 = ((f32[64,4,640]{2,1,0:T(4,128)}), f32[64,4,640]{2,1,0:T(4,128)S(1)}, u32[]{:S(2)}, u32[]{:S(2)}) async-start(f32[64,4,640]{2,1,0:T(4,128)} %shard_map.56), calls=%async_computation.1 | async-start | bytes 1310720 | tf_op jit(solution)/shard_map/all_to_all | solution.py:204
  68.0 16.9 %collective-permute-start.3 = (f32[8,128]{1,0:T(8,128)S(1)}, f32[8,128]{1,0:T(8,128)S(1)}, u32[]{:S(2)}, u32[]{:S(2)}) collective-permute-start(f32[8,128]{1,0:T(8,128)S(1)} %broadcast_in_dim.21), channel_id=1, source_target_pairs={{0,1},{1,0},{2,3},{3,2},{4,5},{5,4},{6,7},{7,6},{8,9},{9,8},{10,11... | collective-permute-start | bytes 12296 | tf_op jit(solution)/shard_map/ppermute | solution.py:235
  81.0 51.1 %copy-start.1 = (f32[256,640]{1,0:T(8,128)}, f32[256,640]{1,0:T(8,128)S(1)}, u32[]{:S(2)}) copy-start(f32[256,640]{1,0:T(8,128)S(1)} %reshape.16.refs_0_) | copy-start | bytes 1966084
  81.0 51.0 %collective-permute-start.2 = (f32[256,640]{1,0:T(8,128)S(1)}, f32[256,640]{1,0:T(8,128)S(1)}, u32[]{:S(2)}, u32[]{:S(2)}) collective-permute-start(f32[256,640]{1,0:T(8,128)S(1)} %reshape.16.refs_0_), channel_id=1, source_target_pairs={{0,3},{1,0},{2,1},{3,2},{4,7},{5,4},{6,5},{7,6},{8,11},{9,8},{10,9... | collective-permute-start | bytes 1966088 | tf_op jit(solution)/shard_map/ppermute | solution.py:200
  83.8 48.2 %collective-permute-start.1 = (f32[256,640]{1,0:T(8,128)S(1)}, f32[256,640]{1,0:T(8,128)S(1)}, u32[]{:S(2)}, u32[]{:S(2)}) collective-permute-start(f32[256,640]{1,0:T(8,128)S(1)} %reshape.16.refs_0_), channel_id=1, source_target_pairs={{0,2},{1,3},{2,0},{3,1},{4,6},{5,7},{6,4},{7,5},{8,10},{9,11},{10,... | collective-permute-start | bytes 1966088 | tf_op jit(solution)/shard_map/ppermute | solution.py:200
  84.2 47.9 %collective-permute-start = (f32[256,640]{1,0:T(8,128)S(1)}, f32[256,640]{1,0:T(8,128)S(1)}, u32[]{:S(2)}, u32[]{:S(2)}) collective-permute-start(f32[256,640]{1,0:T(8,128)S(1)} %reshape.16.refs_0_), channel_id=1, source_target_pairs={{0,1},{1,2},{2,3},{3,0},{4,5},{5,6},{6,7},{7,4},{8,9},{9,10},{10,1... | collective-permute-start | bytes 1966088 | tf_op jit(solution)/shard_map/ppermute | solution.py:200
  85.5 29.5 %collective-permute-start.4 = (f32[8,128]{1,0:T(8,128)S(1)}, f32[8,128]{1,0:T(8,128)S(1)}, u32[]{:S(2)}, u32[]{:S(2)}) collective-permute-start(f32[8,128]{1,0:T(8,128)S(1)} %broadcast_add_fusion), channel_id=1, source_target_pairs={{0,2},{1,3},{2,0},{3,1},{4,6},{5,7},{6,4},{7,5},{8,10},{9,11},{10,... | collective-permute-start | bytes 12296 | tf_op jit(solution)/shard_map/ppermute | solution.py:235
  132.1 0.9 copy-start.3
  132.1 1.0 copy-start.4
  132.1 1.3 copy-start.5

commit v3 on v2

--- a/solution.py
+++ b/solution.py
@@ -26,10 +26,14 @@
 
 LANES = 128
 SUBLANES = 8
-CHUNKS = (640,)
+CHUNKS = (384, 256)
 
 WHOLE = pl.BlockSpec(memory_space=pltpu.VMEM)
 SCALAR = pl.BlockSpec(memory_space=pltpu.SMEM)
+
+
+def resident(value):
+    return pltpu.with_memory_space_constraint(value, pltpu.VMEM)
 
 
 def butterfly(rows):
@@ -132,7 +136,7 @@
             pltpu.VMEM((blocks, SUBLANES, LANES), jnp.int32),
             pltpu.VMEM((blocks, SUBLANES, LANES), jnp.float32),
         ],
-    )(block, segments)
+    )(block, resident(segments))
 
 
 def product_kernel(group, offset, count, col_ref, *refs):
@@ -192,7 +196,7 @@
         out_specs=column_tile,
         out_shape=jax.ShapeDtypeStruct((rows, columns), jnp.float32),
         scratch_shapes=[pltpu.VMEM((2 * rows, len(parts) * width), jnp.bfloat16)],
-    )(col, *parts, *totals, *norms, grads)
+    )(col, *map(resident, parts), *totals, *map(resident, norms), grads)
 
 
 def col_shift(value, shift):

time: 143 us -> 137 us (0.958); the launches traced: 142 us -> 135 us
  starting transfers between devices: 26.4 us -> 49.5 us
  waiting for transfers between devices: 73.7 us -> 55 us
  blocking collectives: 16.4 us -> 0 us
  Pallas kernels: 14.7 us -> 19 us
    ppermute x2, waiting for transfers between devices: 27.5 us -> 4.66 us  [staged(): lax.ppermute(squares, 'cols', [(c, c ^ bit) for c in range(cols)])]
    all_to_all x2 -> x4, starting transfers between devices: 19.1 us -> 39.3 us  [exchange(): return lax.all_to_all(value, 'rows', 0, 0, tiled=True)]
    all_to_all x1 -> x0, blocking collectives: 16.4 us -> none  [exchange(): return lax.all_to_all(value, 'rows', 0, 0, tiled=True)]
    pallas_call x1 -> x2, Pallas kernels: 9.05 us -> 14.1 us  [product(): pl.pallas_call(functools.partial(product_kernel, group, offset, len(parts...]
    all_to_all x2 -> x4, waiting for transfers between devices: 46.3 us -> 50.3 us  [exchange(): return lax.all_to_all(value, 'rows', 0, 0, tiled=True)]
    unnamed x12 -> x2, local copies, waits for them, and re-layouts: 2.35 us -> 0.01 us
    reshape x1 -> x2, local copies, waits for them, and re-layouts: 0.23 us -> 2.17 us  [staged(): kept = kept.reshape(row_devices * share, width)]
    ppermute x3 -> x6, starting transfers between devices: 3.85 us -> 5.79 us  [col_shift(): lax.ppermute(value, 'cols', [(c, (c + shift) % cols) for c in range(cols)])]
  transfers between devices with their start and end apart: 7 -> 12, of which waited for: 3 -> 5; matrix products, arithmetic and copies ran while one was open for 6% -> 8% of each run, Pallas kernels for 0% -> 6%
where the time goes in v3:
time: 137 us; the launch traced here: 135 us
  waiting for transfers between devices  55 us (40%)
  starting transfers between devices  49.5 us (36%)
  Pallas kernels  19 us (14%)
  matrix products  6.59 us (5%)
  local copies, waits for them, and re-layouts  3.46 us (3%)
    all_to_all x4, waiting for transfers between devices, exchange(): return lax.all_to_all(value, 'rows', 0, 0, tiled=True)  50.3 us
    all_to_all x4, starting transfers between devices, exchange(): return lax.all_to_all(value, 'rows', 0, 0, tiled=True)  39.3 us
    pallas_call x2, Pallas kernels, product(): pl.pallas_call(functools.partial(product_kernel, group, offset, len(parts...  14.1 us
    dot_general x1, matrix products, staged(): jnp.dot(hidden_acts[0], grads, preferred_element_type=jnp.float32)  6.59 us
    ppermute x6, starting transfers between devices, col_shift(): lax.ppermute(value, 'cols', [(c, (c + shift) % cols) for c in range(cols)])  5.79 us
    ppermute x2, waiting for transfers between devices, staged(): lax.ppermute(squares, 'cols', [(c, c ^ bit) for c in range(cols)])  4.66 us
    ppermute x2, starting transfers between devices, staged(): lax.ppermute(squares, 'cols', [(c, c ^ bit) for c in range(cols)])  4.39 us
    pallas_call x1, Pallas kernels, inner(): pl.pallas_call(functools.partial(inner_kernel, blocks), grid_spec=pltpu.P...  2.89 us
  transfers between devices with their start and end apart: 12, of which 5 were waited for; matrix products, arithmetic and copies ran while one was open for 8% of the time, Pallas kernels for 6%

profile of v3, /device:TPU:1, one launch (start us, length us, event | category | flops | bytes accessed | tf_op | source)
XLA Modules:
  0.0 135.0 jit_solution(15241350892759136339)
XLA Ops:
  0.0 2.9 %shard_map.55 = f32[2624,128]{1,0:T(8,128)} custom-call(s32[1]{0:T(128)} %bitcast.col_ref, bf16[512,432]{1,0:T(8,128)(2,1)} %constant.13.clone.table_ref, s32[1,432]{1,0:T(1,128)} %bitcast.22, s32[2,128]{1,0:T(2,128)} %bitcast.23, bf16[1,432,2560]{2,1,0:T(8,128)(2,1)} %acts_ref.1), custom_call_target="tpu_custom_call" | custom-call | tf_op jit(solution)/shard_map/pallas_call | solution.py:71
  2.9 13.0 %all-to-all-start = ((f32[64,1,5248]{2,1,0:T(1,128)}), f32[64,1,5248]{2,1,0:T(1,128)S(1)}, u32[]{:S(2)}, u32[]{:S(2)}) async-start(f32[64,1,5248]{2,1,0:T(1,128)} %bitcast.21), calls=%async_computation | async-start | bytes 2686976 | tf_op jit(solution)/shard_map/all_to_all | solution.py:208
  15.9 34.8 %all-to-all-done = f32[64,1,5248]{2,1,0:T(1,128)S(1)} async-done(((f32[64,1,5248]{2,1,0:T(1,128)}), f32[64,1,5248]{2,1,0:T(1,128)S(1)}, u32[]{:S(2)}, u32[]{:S(2)}) %all-to-all-start) | async-done | bytes 1343520 | tf_op jit(solution)/shard_map/all_to_all | solution.py:208
  50.7 1.1 shard_map.57
  51.8 6.3 %all-to-all-start.2 = ((f32[64,4,384]{2,1,0:T(4,128)}), f32[64,4,384]{2,1,0:T(4,128)}, u32[]{:S(2)}, u32[]{:S(2)}) async-start(f32[64,4,384]{2,1,0:T(4,128)} %shard_map.57), calls=%async_computation.2 | async-start | bytes 786432 | tf_op jit(solution)/shard_map/all_to_all | solution.py:208
  58.2 0.9 shard_map.56
  59.1 13.5 %all-to-all-done.2 = f32[64,4,384]{2,1,0:T(4,128)} async-done(((f32[64,4,384]{2,1,0:T(4,128)}), f32[64,4,384]{2,1,0:T(4,128)}, u32[]{:S(2)}, u32[]{:S(2)}) %all-to-all-start.2) | async-done | bytes 393248 | tf_op jit(solution)/shard_map/all_to_all | solution.py:208
  72.6 6.4 %all-to-all-start.1 = ((f32[64,4,256]{2,1,0:T(4,128)}), f32[64,4,256]{2,1,0:T(4,128)}, u32[]{:S(2)}, u32[]{:S(2)}) async-start(f32[64,4,256]{2,1,0:T(4,128)} %shard_map.56), calls=%async_computation.1 | async-start | bytes 524288 | tf_op jit(solution)/shard_map/all_to_all | solution.py:208
  79.1 6.6 %fusion.1 = f32[]{:T(128)} fusion(bf16[1,432,2560]{2,1,0:T(8,128)(2,1)S(1)} %copy-done, bf16[1,2560,1280]{2,1,0:T(8,128)(2,1)} %param.6), kind=kOutput, calls=%fused_computation.2 | convolution fusion | flops 2832261120 | bytes 8765444 | tf_op jit(solution)/shard_map/dot_general | solution.py:235
  85.7 0.6 broadcast_in_dim.22
  86.3 1.4 %collective-permute-start.6 = (f32[8,128]{1,0:T(8,128)S(1)}, f32[8,128]{1,0:T(8,128)S(1)}, u32[]{:S(2)}, u32[]{:S(2)}) collective-permute-start(f32[8,128]{1,0:T(8,128)S(1)} %broadcast_in_dim.22), channel_id=1, source_target_pairs={{0,1},{1,0},{2,3},{3,2},{4,5},{5,4},{6,7},{7,6},{8,9},{9,8},{10,11... | collective-permute-start | bytes 12296 | tf_op jit(solution)/shard_map/ppermute | solution.py:239
  87.7 1.1 reshape.20.refs_0_
  89.3 0.6 broadcast_add_fusion
  89.9 3.0 %collective-permute-start.7 = (f32[8,128]{1,0:T(8,128)S(1)}, f32[8,128]{1,0:T(8,128)S(1)}, u32[]{:S(2)}, u32[]{:S(2)}) collective-permute-start(f32[8,128]{1,0:T(8,128)S(1)} %broadcast_add_fusion), channel_id=1, source_target_pairs={{0,2},{1,3},{2,0},{3,1},{4,6},{5,7},{6,4},{7,5},{8,10},{9,11},{10,... | collective-permute-start | bytes 12296 | tf_op jit(solution)/shard_map/ppermute | solution.py:239
  93.0 2.7 %collective-permute-start.5 = (f32[256,384]{1,0:T(8,128)S(1)}, f32[256,384]{1,0:T(8,128)S(1)}, u32[]{:S(2)}, u32[]{:S(2)}) collective-permute-start(f32[256,384]{1,0:T(8,128)S(1)} %reshape.20.refs_0_), channel_id=1, source_target_pairs={{0,3},{1,0},{2,1},{3,2},{4,7},{5,4},{6,5},{7,6},{8,11},{9,8},{10,9... | collective-permute-start | bytes 1179656 | tf_op jit(solution)/shard_map/ppermute | solution.py:204
  95.7 4.5 %collective-permute-done.7 = f32[8,128]{1,0:T(8,128)S(1)} collective-permute-done((f32[8,128]{1,0:T(8,128)S(1)}, f32[8,128]{1,0:T(8,128)S(1)}, u32[]{:S(2)}, u32[]{:S(2)}) %collective-permute-start.7) | collective-permute-done | bytes 4128 | tf_op jit(solution)/shard_map/ppermute | solution.py:239
  100.2 0.6 fusion.5
  100.9 1.0 reshape.19.refs_0_
  102.2 2.5 %collective-permute-start.2 = (f32[256,256]{1,0:T(8,128)S(1)}, f32[256,256]{1,0:T(8,128)S(1)}, u32[]{:S(2)}, u32[]{:S(2)}) collective-permute-start(f32[256,256]{1,0:T(8,128)S(1)} %reshape.19.refs_0_), channel_id=1, source_target_pairs={{0,3},{1,0},{2,1},{3,2},{4,7},{5,4},{6,5},{7,6},{8,11},{9,8},{10,9... | collective-permute-start | bytes 786440 | tf_op jit(solution)/shard_map/ppermute | solution.py:204
  104.7 0.6 broadcast_in_dim.23
  105.3 13.6 %all-to-all-start.3 = ((f32[64,1,128]{2,1,0:T(1,128)}), f32[64,1,128]{2,1,0:T(1,128)S(1)}, u32[]{:S(2)}, u32[]{:S(2)}) async-start(f32[64,1,128]{2,1,0:T(1,128)} %broadcast_in_dim.23), calls=%async_computation.3 | async-start | bytes 65536 | tf_op jit(solution)/shard_map/all_to_all | solution.py:208
  118.9 7.3 %shard_map.58.refs_4_ = f32[256,1280]{1,0:T(8,128)} custom-call(s32[1]{0:T(128)} %bitcast.col_ref, f32[256,384]{1,0:T(8,128)S(1)} %reshape.20.refs_0_, f32[256,384]{1,0:T(8,128)S(1)} %collective-permute-done.3.refs_1_, f32[256,384]{1,0:T(8,128)S(1)} %collective-permute-done.4.refs_2_, f32[256,384]{1,0:T(8,128)S(1)} %collective-permute-done.5.refs_3_, ...), custom_call_target="tpu_custom_call" | custom-call | tf_op jit(solution)/shard_map/pallas_call | solution.py:186
  126.2 1.9 %all-to-all-done.3.refs_5_ = f32[64,1,128]{2,1,0:T(1,128)S(1)} async-done(((f32[64,1,128]{2,1,0:T(1,128)}), f32[64,1,128]{2,1,0:T(1,128)S(1)}, u32[]{:S(2)}, u32[]{:S(2)}) %all-to-all-start.3) | async-done | bytes 32800 | tf_op jit(solution)/shard_map/all_to_all | solution.py:208
  128.2 6.8 %shard_map.59 = f32[256,1280]{1,0:T(8,128)} custom-call(s32[1]{0:T(128)} %bitcast.col_ref, f32[256,256]{1,0:T(8,128)S(1)} %reshape.19.refs_0_, f32[256,256]{1,0:T(8,128)S(1)} %collective-permute-done.refs_1_, f32[256,256]{1,0:T(8,128)S(1)} %collective-permute-done.1.refs_2_, f32[256,256]{1,0:T(8,128)S(1)} %collective-permute-done.2.refs_3_, ...), custom_call_target="tpu_custom_call" | custom-call | tf_op jit(solution)/shard_map/pallas_call | solution.py:186
  (15 shorter events, 0.8 us)
Async XLA Ops:
  2.9 47.8 %all-to-all-start = ((f32[64,1,5248]{2,1,0:T(1,128)}), f32[64,1,5248]{2,1,0:T(1,128)S(1)}, u32[]{:S(2)}, u32[]{:S(2)}) async-start(f32[64,1,5248]{2,1,0:T(1,128)} %bitcast.21), calls=%async_computation | async-start | bytes 2686976 | tf_op jit(solution)/shard_map/all_to_all | solution.py:208
  50.7 28.4 %copy-start = (bf16[1,432,2560]{2,1,0:T(8,128)(2,1)S(1)}, bf16[1,432,2560]{2,1,0:T(8,128)(2,1)}, u32[]{:S(2)}) copy-start(bf16[1,432,2560]{2,1,0:T(8,128)(2,1)} %acts_ref.1) | copy-start | bytes 6635524
  51.8 20.8 %all-to-all-start.2 = ((f32[64,4,384]{2,1,0:T(4,128)}), f32[64,4,384]{2,1,0:T(4,128)}, u32[]{:S(2)}, u32[]{:S(2)}) async-start(f32[64,4,384]{2,1,0:T(4,128)} %shard_map.57), calls=%async_computation.2 | async-start | bytes 786432 | tf_op jit(solution)/shard_map/all_to_all | solution.py:208
  72.6 28.2 %all-to-all-start.1 = ((f32[64,4,256]{2,1,0:T(4,128)}), f32[64,4,256]{2,1,0:T(4,128)}, u32[]{:S(2)}, u32[]{:S(2)}) async-start(f32[64,4,256]{2,1,0:T(4,128)} %shard_map.56), calls=%async_computation.1 | async-start | bytes 524288 | tf_op jit(solution)/shard_map/all_to_all | solution.py:208
  86.3 2.9 %collective-permute-start.6 = (f32[8,128]{1,0:T(8,128)S(1)}, f32[8,128]{1,0:T(8,128)S(1)}, u32[]{:S(2)}, u32[]{:S(2)}) collective-permute-start(f32[8,128]{1,0:T(8,128)S(1)} %broadcast_in_dim.22), channel_id=1, source_target_pairs={{0,1},{1,0},{2,3},{3,2},{4,5},{5,4},{6,7},{7,6},{8,9},{9,8},{10,11... | collective-permute-start | bytes 12296 | tf_op jit(solution)/shard_map/ppermute | solution.py:239
  88.9 13.3 %collective-permute-start.3 = (f32[256,384]{1,0:T(8,128)S(1)}, f32[256,384]{1,0:T(8,128)S(1)}, u32[]{:S(2)}, u32[]{:S(2)}) collective-permute-start(f32[256,384]{1,0:T(8,128)S(1)} %reshape.20.refs_0_), channel_id=1, source_target_pairs={{0,1},{1,2},{2,3},{3,0},{4,5},{5,6},{6,7},{7,4},{8,9},{9,10},{10,1... | collective-permute-start | bytes 1179656 | tf_op jit(solution)/shard_map/ppermute | solution.py:204
  89.9 10.3 %collective-permute-start.7 = (f32[8,128]{1,0:T(8,128)S(1)}, f32[8,128]{1,0:T(8,128)S(1)}, u32[]{:S(2)}, u32[]{:S(2)}) collective-permute-start(f32[8,128]{1,0:T(8,128)S(1)} %broadcast_add_fusion), channel_id=1, source_target_pairs={{0,2},{1,3},{2,0},{3,1},{4,6},{5,7},{6,4},{7,5},{8,10},{9,11},{10,... | collective-permute-start | bytes 12296 | tf_op jit(solution)/shard_map/ppermute | solution.py:239
  92.9 26.0 %collective-permute-start.4 = (f32[256,384]{1,0:T(8,128)S(1)}, f32[256,384]{1,0:T(8,128)S(1)}, u32[]{:S(2)}, u32[]{:S(2)}) collective-permute-start(f32[256,384]{1,0:T(8,128)S(1)} %reshape.20.refs_0_), channel_id=1, source_target_pairs={{0,2},{1,3},{2,0},{3,1},{4,6},{5,7},{6,4},{7,5},{8,10},{9,11},{10,... | collective-permute-start | bytes 1179656 | tf_op jit(solution)/shard_map/ppermute | solution.py:204
  93.0 25.9 %collective-permute-start.5 = (f32[256,384]{1,0:T(8,128)S(1)}, f32[256,384]{1,0:T(8,128)S(1)}, u32[]{:S(2)}, u32[]{:S(2)}) collective-permute-start(f32[256,384]{1,0:T(8,128)S(1)} %reshape.20.refs_0_), channel_id=1, source_target_pairs={{0,3},{1,0},{2,1},{3,2},{4,7},{5,4},{6,5},{7,6},{8,11},{9,8},{10,9... | collective-permute-start | bytes 1179656 | tf_op jit(solution)/shard_map/ppermute | solution.py:204
  101.9 26.2 %collective-permute-start = (f32[256,256]{1,0:T(8,128)S(1)}, f32[256,256]{1,0:T(8,128)S(1)}, u32[]{:S(2)}, u32[]{:S(2)}) collective-permute-start(f32[256,256]{1,0:T(8,128)S(1)} %reshape.19.refs_0_), channel_id=1, source_target_pairs={{0,1},{1,2},{2,3},{3,0},{4,5},{5,6},{6,7},{7,4},{8,9},{9,10},{10,1... | collective-permute-start | bytes 786440 | tf_op jit(solution)/shard_map/ppermute | solution.py:204
  102.0 26.1 %collective-permute-start.1 = (f32[256,256]{1,0:T(8,128)S(1)}, f32[256,256]{1,0:T(8,128)S(1)}, u32[]{:S(2)}, u32[]{:S(2)}) collective-permute-start(f32[256,256]{1,0:T(8,128)S(1)} %reshape.19.refs_0_), channel_id=1, source_target_pairs={{0,2},{1,3},{2,0},{3,1},{4,6},{5,7},{6,4},{7,5},{8,10},{9,11},{10,... | collective-permute-start | bytes 786440 | tf_op jit(solution)/shard_map/ppermute | solution.py:204
  102.2 26.0 %collective-permute-start.2 = (f32[256,256]{1,0:T(8,128)S(1)}, f32[256,256]{1,0:T(8,128)S(1)}, u32[]{:S(2)}, u32[]{:S(2)}) collective-permute-start(f32[256,256]{1,0:T(8,128)S(1)} %reshape.19.refs_0_), channel_id=1, source_target_pairs={{0,3},{1,0},{2,1},{3,2},{4,7},{5,4},{6,5},{7,6},{8,11},{9,8},{10,9... | collective-permute-start | bytes 786440 | tf_op jit(solution)/shard_map/ppermute | solution.py:204
  105.3 22.8 %all-to-all-start.3 = ((f32[64,1,128]{2,1,0:T(1,128)}), f32[64,1,128]{2,1,0:T(1,128)S(1)}, u32[]{:S(2)}, u32[]{:S(2)}) async-start(f32[64,1,128]{2,1,0:T(1,128)} %broadcast_in_dim.23), calls=%async_computation.3 | async-start | bytes 65536 | tf_op jit(solution)/shard_map/all_to_all | solution.py:208

commit v4 on v3

--- a/solution.py
+++ b/solution.py
@@ -26,7 +26,6 @@
 
 LANES = 128
 SUBLANES = 8
-CHUNKS = (384, 256)
 
 WHOLE = pl.BlockSpec(memory_space=pltpu.VMEM)
 SCALAR = pl.BlockSpec(memory_space=pltpu.SMEM)
@@ -139,64 +138,78 @@
     )(block, resident(segments))
 
 
-def product_kernel(group, offset, count, col_ref, *refs):
-    parts = refs[:count]
-    total_ref = refs[count] if offset else None
-    last = offset + parts[0].shape[1] == group
-    squares_ref = refs[-4] if last else None
-    grads_ref, out_ref, terms_ref = refs[-3:]
-    rows, width = parts[0].shape
+def product_kernel(shifts, adds, scales, col_ref, *refs):
+    count = len(shifts)
+    parts, refs = refs[:2 * count], refs[2 * count:]
+    total_ref = refs[0] if adds else None
+    squares_ref = refs[adds] if scales else None
+    grads = refs[adds + scales:-2]
+    out_ref, terms_ref = refs[-2:]
+    half, width = parts[0].shape
+    rows = 2 * half
 
     @pl.when(pl.program_id(0) == 0)
     def _():
-        for shift in range(count):
-            value = parts[shift][...]
+        for i, part in enumerate(parts):
+            value = part[...]
             coarse = value.astype(jnp.bfloat16)
-            at = slice(shift * width, (shift + 1) * width)
-            terms_ref[:rows, at] = coarse
-            terms_ref[rows:, at] = (value - coarse.astype(jnp.float32)).astype(jnp.bfloat16)
+            at = slice(i // 2 * width, (i // 2 + 1) * width)
+            first = i % 2 * half
+            terms_ref[first:first + half, at] = coarse
+            terms_ref[rows + first:rows + first + half, at] = (
+                value - coarse.astype(jnp.float32)
+            ).astype(jnp.bfloat16)
 
     both = None
-    for shift in range(count):
-        source = lax.rem(col_ref[0] + count - shift, count)
-        at = pl.ds(pl.multiple_of(source * group + offset, LANES), width)
+    for i in range(count):
         step = jnp.dot(
-            terms_ref[:, shift * width:(shift + 1) * width],
-            grads_ref[at, :],
+            terms_ref[:, i * width:(i + 1) * width],
+            grads[i][...],
             preferred_element_type=jnp.float32,
         )
         both = step if both is None else both + step
     value = both[:rows] + both[rows:]
-    if offset:
+    if adds:
         value = value + total_ref[...]
-    if last:
+    if scales:
         squares = jnp.sum(squares_ref[...], axis=0)
         scale = lax.rsqrt(squares / D + epsilon)
         value = value * jnp.tile(scale, (1, value.shape[1] // LANES))
     out_ref[...] = value
 
 
-def product(group, offset, col, parts, total, squares, grads):
-    rows, width = parts[0].shape
+def product(col, parts, total, squares, grads):
+    shifts = tuple(parts)
+    halves = [resident(half) for shift in shifts for half in parts[shift]]
+    half, width = halves[0].shape
     tokens, columns = grads.shape
+    count = tokens // width
     tile = 256
-    column_tile = pl.BlockSpec((rows, tile), lambda i: (0, i))
-    totals = [total] if offset else []
-    norms = [squares] if offset + width == group else []
+    column_tile = pl.BlockSpec((2 * half, tile), lambda i, c: (0, i))
+    totals = [] if total is None else [total]
+    norms = [] if squares is None else [resident(squares)]
+
+    def rows_of(shift):
+        return pl.BlockSpec(
+            (width, tile), lambda i, c: (lax.rem(c[0] + count - shift, count), i)
+        )
+
     return pl.pallas_call(
-        functools.partial(product_kernel, group, offset, len(parts)),
-        grid=(columns // tile,),
-        in_specs=[
-            SCALAR,
-            *[WHOLE] * len(parts),
-            *[column_tile] * len(totals),
-            *[WHOLE] * len(norms),
-            pl.BlockSpec((tokens, tile), lambda i: (0, i)),
-        ],
-        out_specs=column_tile,
-        out_shape=jax.ShapeDtypeStruct((rows, columns), jnp.float32),
-        scratch_shapes=[pltpu.VMEM((2 * rows, len(parts) * width), jnp.bfloat16)],
-    )(col, *map(resident, parts), *totals, *map(resident, norms), grads)
+        functools.partial(product_kernel, shifts, len(totals), len(norms)),
+        grid_spec=pltpu.PrefetchScalarGridSpec(
+            num_scalar_prefetch=1,
+            grid=(columns // tile,),
+            in_specs=[
+                *[WHOLE] * len(halves),
+                *[column_tile] * len(totals),
+                *[WHOLE] * len(norms),
+                *[rows_of(shift) for shift in shifts],
+            ],
+            out_specs=column_tile,
+            scratch_shapes=[pltpu.VMEM((4 * half, len(shifts) * width), jnp.bfloat16)],
+        ),
+        out_shape=jax.ShapeDtypeStruct((2 * half, columns), jnp.float32),
+    )(col, *halves, *totals, *norms, *[grads] * len(shifts))
 
 
 def col_shift(value, shift):
@@ -242,16 +255,21 @@
     squares = jnp.broadcast_to(squares[:1], (row_devices, 1, LANES))
     squares = exchange(squares)
 
-    total, start = None, 0
-    for width in CHUNKS:
-        kept = mix(block[None], segments, row_devices, share, tiles, start, width)
-        kept = exchange(kept)
-        kept = kept.reshape(row_devices * share, width)
-        parts = [kept]
-        for shift in range(1, cols):
-            parts.append(col_shift(kept, shift))
-        total = product(group, start, col, parts, total, squares, grads)
-        start += width
+    kept = mix(block[None], segments, row_devices, share, tiles, 0, group)
+    kept = exchange(kept)
+
+    half = row_devices // 2
+    top = kept[:half].reshape(half * share, group)
+    low = kept[half:].reshape(half * share, group)
+    up_top = col_shift(top, 1)
+    down_low = col_shift(low, -1)
+    up_low = col_shift(low, 1)
+    down_top = col_shift(top, -1)
+    far_top = col_shift(up_top, 1)
+    far_low = col_shift(down_low, -1)
+    total = product(col, {0: (top, low)}, None, None, grads)
+    total = product(col, {1: (up_top, up_low), cols - 1: (down_top, down_low)}, total, None, grads)
+    total = product(col, {2: (far_top, far_low)}, total, squares, grads)
     return total[None]
 
 

time: 137 us -> 127 us (0.927); the launches traced: 135 us -> 127 us
  blocking collectives: 0 us -> 26.4 us
  waiting for transfers between devices: 55 us -> 37.3 us
  starting transfers between devices: 49.5 us -> 32.3 us
  Pallas kernels: 19 us -> 21.2 us
  local copies, waits for them, and re-layouts: 3.46 us -> 1.55 us
    all_to_all x0 -> x1, blocking collectives: none -> 26.4 us  [exchange(): return lax.all_to_all(value, 'rows', 0, 0, tiled=True)]
    all_to_all x4 -> x2, starting transfers between devices: 39.3 us -> 22.3 us  [exchange(): return lax.all_to_all(value, 'rows', 0, 0, tiled=True)]
    all_to_all x4 -> x2, waiting for transfers between devices: 50.3 us -> 34.8 us  [exchange(): return lax.all_to_all(value, 'rows', 0, 0, tiled=True)]
    pallas_call x2 -> x3, Pallas kernels: 14.1 us -> 17 us  [product(): pl.pallas_call(functools.partial(product_kernel, shifts, len(totals), len...]
    ppermute x2, starting transfers between devices: 4.39 us -> 1.73 us  [staged(): lax.ppermute(squares, 'cols', [(c, c ^ bit) for c in range(cols)])]
    ppermute x6, starting transfers between devices: 5.79 us -> 8.25 us  [col_shift(): lax.ppermute(value, 'cols', [(c, (c + shift) % cols) for c in range(cols)])]
    ppermute x2, waiting for transfers between devices: 4.66 us -> 2.45 us  [staged(): lax.ppermute(squares, 'cols', [(c, c ^ bit) for c in range(cols)])]
    reshape x2, local copies, waits for them, and re-layouts: 2.17 us -> 0.23 us  [the longest x1 0.11 us: staged(): low = kept[half:].reshape(half * share, group)]
  transfers between devices with their start and end apart: 12 -> 10, of which waited for: 5 -> 2; matrix products, arithmetic and copies ran while one was open for 8% -> 7% of each run, Pallas kernels for 6% -> 9%
where the time goes in v4:
time: 127 us
  waiting for transfers between devices  37.3 us (29%)
  starting transfers between devices  32.3 us (25%)
  blocking collectives  26.4 us (21%)
  Pallas kernels  21.2 us (17%)
  matrix products  6.59 us (5%)
  local copies, waits for them, and re-layouts  1.55 us (1%)
  other arithmetic  1.3 us (1%)
    all_to_all x2, waiting for transfers between devices, exchange(): return lax.all_to_all(value, 'rows', 0, 0, tiled=True)  34.8 us
    all_to_all x1, blocking collectives, exchange(): return lax.all_to_all(value, 'rows', 0, 0, tiled=True)  26.4 us
    all_to_all x2, starting transfers between devices, exchange(): return lax.all_to_all(value, 'rows', 0, 0, tiled=True)  22.3 us
    pallas_call x3, Pallas kernels, product(): pl.pallas_call(functools.partial(product_kernel, shifts, len(totals), len...  17 us
    ppermute x6, starting transfers between devices, col_shift(): lax.ppermute(value, 'cols', [(c, (c + shift) % cols) for c in range(cols)])  8.25 us
    dot_general x1, matrix products, staged(): jnp.dot(hidden_acts[0], grads, preferred_element_type=jnp.float32)  6.59 us
    pallas_call x1, Pallas kernels, inner(): pl.pallas_call(functools.partial(inner_kernel, blocks), grid_spec=pltpu.P...  2.9 us
  transfers between devices with their start and end apart: 10, of which 2 were waited for; matrix products, arithmetic and copies ran while one was open for 7% of the time, Pallas kernels for 9%

profile of v4, /device:TPU:1, one launch (start us, length us, event | category | flops | bytes accessed | tf_op | source)
XLA Modules:
  0.0 126.8 jit_solution(12743343270068792769)
XLA Ops:
  0.0 2.9 %shard_map.55 = f32[2624,128]{1,0:T(8,128)} custom-call(s32[1]{0:T(128)} %bitcast.col_ref, bf16[512,432]{1,0:T(8,128)(2,1)} %constant.13.clone.table_ref, s32[1,432]{1,0:T(1,128)} %bitcast.23, s32[2,128]{1,0:T(2,128)} %bitcast.24, bf16[1,432,2560]{2,1,0:T(8,128)(2,1)} %acts_ref.1), custom_call_target="tpu_custom_call" | custom-call | tf_op jit(solution)/shard_map/pallas_call | solution.py:70
  2.9 13.0 %all-to-all-start = ((f32[64,1,5248]{2,1,0:T(1,128)}), f32[64,1,5248]{2,1,0:T(1,128)S(1)}, u32[]{:S(2)}, u32[]{:S(2)}) async-start(f32[64,1,5248]{2,1,0:T(1,128)} %bitcast.22), calls=%async_computation | async-start | bytes 2686976 | tf_op jit(solution)/shard_map/all_to_all | solution.py:221
  15.9 34.8 %all-to-all-done = f32[64,1,5248]{2,1,0:T(1,128)S(1)} async-done(((f32[64,1,5248]{2,1,0:T(1,128)}), f32[64,1,5248]{2,1,0:T(1,128)S(1)}, u32[]{:S(2)}, u32[]{:S(2)}) %all-to-all-start) | async-done | bytes 1343520 | tf_op jit(solution)/shard_map/all_to_all | solution.py:221
  50.7 1.4 %shard_map.56 = f32[64,4,640]{2,1,0:T(4,128)} custom-call(s32[1]{0:T(128)} %bitcast.1.block_ref, f32[2624,128]{1,0:T(8,128)S(1)} %bitcast.17), custom_call_target="tpu_custom_call" | custom-call | tf_op jit(solution)/shard_map/pallas_call | solution.py:129
  52.1 26.4 %all_to_all.15 = f32[64,4,640]{2,1,0:T(4,128)S(1)} all-to-all(f32[64,4,640]{2,1,0:T(4,128)} %shard_map.56), channel_id=1, replica_groups=mesh['rows'=64,'cols'=4] {'rows'}, dimensions={0} | all-to-all | bytes 1310720 | tf_op jit(solution)/shard_map/all_to_all | solution.py:221
  78.6 0.1 reshape.19.refs_0_
  78.7 0.1 reshape.20.refs_1_
  78.8 1.4 %collective-permute-start = (f32[128,640]{1,0:T(8,128)S(1)}, f32[128,640]{1,0:T(8,128)S(1)}, u32[]{:S(2)}, u32[]{:S(2)}) collective-permute-start(f32[128,640]{1,0:T(8,128)S(1)} %reshape.19.refs_0_), channel_id=1, source_target_pairs={{0,1},{1,2},{2,3},{3,0},{4,5},{5,6},{6,7},{7,4},{8,9},{9,10},{10,1... | collective-permute-start | bytes 983048 | tf_op jit(solution)/shard_map/ppermute | solution.py:217
  80.2 1.5 %collective-permute-start.2 = (f32[128,640]{1,0:T(8,128)S(1)}, f32[128,640]{1,0:T(8,128)S(1)}, u32[]{:S(2)}, u32[]{:S(2)}) collective-permute-start(f32[128,640]{1,0:T(8,128)S(1)} %reshape.20.refs_1_), channel_id=1, source_target_pairs={{0,3},{1,0},{2,1},{3,2},{4,7},{5,4},{6,5},{7,6},{8,11},{9,8},{10,9... | collective-permute-start | bytes 983048 | tf_op jit(solution)/shard_map/ppermute | solution.py:217
  81.7 6.6 %fusion.1 = f32[]{:T(128)} fusion(bf16[1,432,2560]{2,1,0:T(8,128)(2,1)S(1)} %copy-done, bf16[1,2560,1280]{2,1,0:T(8,128)(2,1)} %param.6), kind=kOutput, calls=%fused_computation.2 | convolution fusion | flops 2832261120 | bytes 8765444 | tf_op jit(solution)/shard_map/dot_general | solution.py:248
  88.3 0.6 broadcast_in_dim.21
  89.0 0.1 collective-permute-start.6
  89.1 2.4 %collective-permute-done.6 = f32[8,128]{1,0:T(8,128)S(1)} collective-permute-done((f32[8,128]{1,0:T(8,128)S(1)}, f32[8,128]{1,0:T(8,128)S(1)}, u32[]{:S(2)}, u32[]{:S(2)}) %collective-permute-start.6) | collective-permute-done | bytes 4128 | tf_op jit(solution)/shard_map/ppermute | solution.py:252
  91.5 0.6 broadcast_add_fusion
  92.2 1.6 %collective-permute-start.7 = (f32[8,128]{1,0:T(8,128)S(1)}, f32[8,128]{1,0:T(8,128)S(1)}, u32[]{:S(2)}, u32[]{:S(2)}) collective-permute-start(f32[8,128]{1,0:T(8,128)S(1)} %broadcast_add_fusion), channel_id=1, source_target_pairs={{0,2},{1,3},{2,0},{3,1},{4,6},{5,7},{6,4},{7,5},{8,10},{9,11},{10,... | collective-permute-start | bytes 12296 | tf_op jit(solution)/shard_map/ppermute | solution.py:252
  93.8 0.4 collective-permute-start.4
  94.2 2.3 %collective-permute-start.5 = (f32[128,640]{1,0:T(8,128)S(1)}, f32[128,640]{1,0:T(8,128)S(1)}, u32[]{:S(2)}, u32[]{:S(2)}) collective-permute-start(f32[128,640]{1,0:T(8,128)S(1)} %reshape.19.refs_0_), channel_id=1, source_target_pairs={{0,3},{1,0},{2,1},{3,2},{4,7},{5,4},{6,5},{7,6},{8,11},{9,8},{10,9... | collective-permute-start | bytes 983048 | tf_op jit(solution)/shard_map/ppermute | solution.py:217
  96.5 2.7 %collective-permute-start.3 = (f32[128,640]{1,0:T(8,128)S(1)}, f32[128,640]{1,0:T(8,128)S(1)}, u32[]{:S(2)}, u32[]{:S(2)}) collective-permute-start(f32[128,640]{1,0:T(8,128)S(1)} %collective-permute-done.2.refs_3_), channel_id=1, source_target_pairs={{0,3},{1,0},{2,1},{3,2},{4,7},{5,4},{6,5},{7,6},{8,11},{9,8},{10,9... | collective-permute-start | bytes 983048 | tf_op jit(solution)/shard_map/ppermute | solution.py:217
  99.2 0.6 fusion.6
  99.8 0.6 broadcast_in_dim.22
  100.5 9.4 %all-to-all-start.2 = ((f32[64,1,128]{2,1,0:T(1,128)}), f32[64,1,128]{2,1,0:T(1,128)S(1)}, u32[]{:S(2)}, u32[]{:S(2)}) async-start(f32[64,1,128]{2,1,0:T(1,128)} %broadcast_in_dim.22), calls=%async_computation.2 | async-start | bytes 65536 | tf_op jit(solution)/shard_map/all_to_all | solution.py:221
  109.8 5.1 %shard_map.57.refs_4_ = f32[256,1280]{1,0:T(8,128)} custom-call(s32[1]{0:T(128)} %bitcast.col_ref, f32[128,640]{1,0:T(8,128)S(1)} %reshape.19.refs_0_, f32[128,640]{1,0:T(8,128)S(1)} %reshape.20.refs_1_, bf16[2560,1280]{1,0:T(8,128)(2,1)} %bitcast.18), custom_call_target="tpu_custom_call" | custom-call | tf_op jit(solution)/shard_map/pallas_call | solution.py:197
  115.0 6.4 %shard_map.58.refs_2_ = f32[256,1280]{1,0:T(8,128)} custom-call(s32[1]{0:T(128)} %bitcast.col_ref, f32[128,640]{1,0:T(8,128)S(1)} %collective-permute-done.refs_0_, f32[128,640]{1,0:T(8,128)S(1)} %collective-permute-done.4.refs_1_, f32[128,640]{1,0:T(8,128)S(1)} %collective-permute-done.5.refs_2_, f32[128,640]{1,0:T(8,128)S(1)} %collective-permute-done.2.refs_3_, ...), custom_call_target="tpu_custom_call" | custom-call | tf_op jit(solution)/shard_map/pallas_call | solution.py:197
  121.4 5.4 %shard_map.59 = f32[256,1280]{1,0:T(8,128)} custom-call(s32[1]{0:T(128)} %bitcast.col_ref, f32[128,640]{1,0:T(8,128)S(1)} %collective-permute-done.1.refs_0_, f32[128,640]{1,0:T(8,128)S(1)} %collective-permute-done.3.refs_1_, f32[256,1280]{1,0:T(8,128)} %shard_map.58.refs_2_, f32[64,1,128]{2,1,0:T(1,128)S(1)} %all-to-all-done.2.refs_3_, ...), custom_call_target="tpu_custom_call" | custom-call | tf_op jit(solution)/shard_map/pallas_call | solution.py:197
  (13 shorter events, 0.1 us)
Async XLA Ops:
  2.9 47.8 %all-to-all-start = ((f32[64,1,5248]{2,1,0:T(1,128)}), f32[64,1,5248]{2,1,0:T(1,128)S(1)}, u32[]{:S(2)}, u32[]{:S(2)}) async-start(f32[64,1,5248]{2,1,0:T(1,128)} %bitcast.22), calls=%async_computation | async-start | bytes 2686976 | tf_op jit(solution)/shard_map/all_to_all | solution.py:221
  52.1 29.6 %copy-start = (bf16[1,432,2560]{2,1,0:T(8,128)(2,1)S(1)}, bf16[1,432,2560]{2,1,0:T(8,128)(2,1)}, u32[]{:S(2)}) copy-start(bf16[1,432,2560]{2,1,0:T(8,128)(2,1)} %acts_ref.1) | copy-start | bytes 6635524
  78.8 17.7 %collective-permute-start = (f32[128,640]{1,0:T(8,128)S(1)}, f32[128,640]{1,0:T(8,128)S(1)}, u32[]{:S(2)}, u32[]{:S(2)}) collective-permute-start(f32[128,640]{1,0:T(8,128)S(1)} %reshape.19.refs_0_), channel_id=1, source_target_pairs={{0,1},{1,2},{2,3},{3,0},{4,5},{5,6},{6,7},{7,4},{8,9},{9,10},{10,1... | collective-permute-start | bytes 983048 | tf_op jit(solution)/shard_map/ppermute | solution.py:217
  80.2 16.3 %collective-permute-start.2 = (f32[128,640]{1,0:T(8,128)S(1)}, f32[128,640]{1,0:T(8,128)S(1)}, u32[]{:S(2)}, u32[]{:S(2)}) collective-permute-start(f32[128,640]{1,0:T(8,128)S(1)} %reshape.20.refs_1_), channel_id=1, source_target_pairs={{0,3},{1,0},{2,1},{3,2},{4,7},{5,4},{6,5},{7,6},{8,11},{9,8},{10,9... | collective-permute-start | bytes 983048 | tf_op jit(solution)/shard_map/ppermute | solution.py:217
  89.0 2.5 %collective-permute-start.6 = (f32[8,128]{1,0:T(8,128)S(1)}, f32[8,128]{1,0:T(8,128)S(1)}, u32[]{:S(2)}, u32[]{:S(2)}) collective-permute-start(f32[8,128]{1,0:T(8,128)S(1)} %broadcast_in_dim.21), channel_id=1, source_target_pairs={{0,1},{1,0},{2,3},{3,2},{4,5},{5,4},{6,7},{7,6},{8,9},{9,8},{10,11... | collective-permute-start | bytes 12296 | tf_op jit(solution)/shard_map/ppermute | solution.py:252
  92.2 7.0 %collective-permute-start.7 = (f32[8,128]{1,0:T(8,128)S(1)}, f32[8,128]{1,0:T(8,128)S(1)}, u32[]{:S(2)}, u32[]{:S(2)}) collective-permute-start(f32[8,128]{1,0:T(8,128)S(1)} %broadcast_add_fusion), channel_id=1, source_target_pairs={{0,2},{1,3},{2,0},{3,1},{4,6},{5,7},{6,4},{7,5},{8,10},{9,11},{10,... | collective-permute-start | bytes 12296 | tf_op jit(solution)/shard_map/ppermute | solution.py:252
  93.8 21.2 %collective-permute-start.4 = (f32[128,640]{1,0:T(8,128)S(1)}, f32[128,640]{1,0:T(8,128)S(1)}, u32[]{:S(2)}, u32[]{:S(2)}) collective-permute-start(f32[128,640]{1,0:T(8,128)S(1)} %reshape.20.refs_1_), channel_id=1, source_target_pairs={{0,1},{1,2},{2,3},{3,0},{4,5},{5,6},{6,7},{7,4},{8,9},{9,10},{10,1... | collective-permute-start | bytes 983048 | tf_op jit(solution)/shard_map/ppermute | solution.py:217
  94.2 20.8 %collective-permute-start.5 = (f32[128,640]{1,0:T(8,128)S(1)}, f32[128,640]{1,0:T(8,128)S(1)}, u32[]{:S(2)}, u32[]{:S(2)}) collective-permute-start(f32[128,640]{1,0:T(8,128)S(1)} %reshape.19.refs_0_), channel_id=1, source_target_pairs={{0,3},{1,0},{2,1},{3,2},{4,7},{5,4},{6,5},{7,6},{8,11},{9,8},{10,9... | collective-permute-start | bytes 983048 | tf_op jit(solution)/shard_map/ppermute | solution.py:217
  96.5 24.9 %collective-permute-start.1 = (f32[128,640]{1,0:T(8,128)S(1)}, f32[128,640]{1,0:T(8,128)S(1)}, u32[]{:S(2)}, u32[]{:S(2)}) collective-permute-start(f32[128,640]{1,0:T(8,128)S(1)} %collective-permute-done.refs_0_), channel_id=1, source_target_pairs={{0,1},{1,2},{2,3},{3,0},{4,5},{5,6},{6,7},{7,4},{8,9},{9,10},{10,1... | collective-permute-start | bytes 983048 | tf_op jit(solution)/shard_map/ppermute | solution.py:217
  96.5 24.9 %collective-permute-start.3 = (f32[128,640]{1,0:T(8,128)S(1)}, f32[128,640]{1,0:T(8,128)S(1)}, u32[]{:S(2)}, u32[]{:S(2)}) collective-permute-start(f32[128,640]{1,0:T(8,128)S(1)} %collective-permute-done.2.refs_3_), channel_id=1, source_target_pairs={{0,3},{1,0},{2,1},{3,2},{4,7},{5,4},{6,5},{7,6},{8,11},{9,8},{10,9... | collective-permute-start | bytes 983048 | tf_op jit(solution)/shard_map/ppermute | solution.py:217
  100.5 21.0 %all-to-all-start.2 = ((f32[64,1,128]{2,1,0:T(1,128)}), f32[64,1,128]{2,1,0:T(1,128)S(1)}, u32[]{:S(2)}, u32[]{:S(2)}) async-start(f32[64,1,128]{2,1,0:T(1,128)} %broadcast_in_dim.22), calls=%async_computation.2 | async-start | bytes 65536 | tf_op jit(solution)/shard_map/all_to_all | solution.py:221

commit v5 on v4

--- a/solution.py
+++ b/solution.py
@@ -29,6 +29,7 @@
 
 WHOLE = pl.BlockSpec(memory_space=pltpu.VMEM)
 SCALAR = pl.BlockSpec(memory_space=pltpu.SMEM)
+PARAMS = pltpu.CompilerParams(vmem_limit_bytes=24 * 2**20)
 
 
 def resident(value):
@@ -78,10 +79,11 @@
                 pl.BlockSpec(kept.shape, lambda i, c: (0, 0)),
                 pl.BlockSpec((1, own_rows, width), lambda i, c: (0, 0, c[0])),
             ],
-            out_specs=pl.BlockSpec((rows, LANES), lambda i, c: (0, 0)),
+            out_specs=WHOLE,
         ),
-        out_shape=jax.ShapeDtypeStruct((rows, LANES), jnp.float32),
-    )(col, table, signs, kept, acts)
+        out_shape=pltpu.VMEM((rows, LANES), jnp.float32),
+        compiler_params=PARAMS,
+    )(col, *[pltpu.with_memory_space_constraint(v, pltpu.HBM) for v in (table, signs, kept, acts)])
 
 
 def mix_kernel(first, tiles, block_ref, segments_ref, kept_ref, position_ref, work_ref):
@@ -130,7 +132,8 @@
         functools.partial(mix_kernel, start // LANES, tiles),
         in_specs=[SCALAR, WHOLE],
         out_specs=WHOLE,
-        out_shape=jax.ShapeDtypeStruct((blocks, share, width), jnp.float32),
+        out_shape=pltpu.VMEM((blocks, share, width), jnp.float32),
+        compiler_params=PARAMS,
         scratch_shapes=[
             pltpu.VMEM((blocks, SUBLANES, LANES), jnp.int32),
             pltpu.VMEM((blocks, SUBLANES, LANES), jnp.float32),
@@ -143,73 +146,83 @@
     parts, refs = refs[:2 * count], refs[2 * count:]
     total_ref = refs[0] if adds else None
     squares_ref = refs[adds] if scales else None
-    grads = refs[adds + scales:-2]
-    out_ref, terms_ref = refs[-2:]
+    grads_ref, out_ref, terms_ref, rows_ref, rows_sems = refs[adds + scales:adds + scales + 5]
     half, width = parts[0].shape
     rows = 2 * half
-
-    @pl.when(pl.program_id(0) == 0)
-    def _():
-        for i, part in enumerate(parts):
-            value = part[...]
-            coarse = value.astype(jnp.bfloat16)
-            at = slice(i // 2 * width, (i // 2 + 1) * width)
-            first = i % 2 * half
-            terms_ref[first:first + half, at] = coarse
-            terms_ref[rows + first:rows + first + half, at] = (
-                value - coarse.astype(jnp.float32)
-            ).astype(jnp.bfloat16)
-
-    both = None
-    for i in range(count):
-        step = jnp.dot(
-            terms_ref[:, i * width:(i + 1) * width],
-            grads[i][...],
-            preferred_element_type=jnp.float32,
-        )
-        both = step if both is None else both + step
-    value = both[:rows] + both[rows:]
-    if adds:
-        value = value + total_ref[...]
+    columns = grads_ref.shape[1]
+    groups = grads_ref.shape[0] // width
+    tile = 256
+    tiles = [slice(first, first + tile) for first in range(0, columns, tile)]
+
+    fetches = []
+    for index, at in enumerate(tiles):
+        for i, shift in enumerate(shifts):
+            source = lax.rem(col_ref[0] + groups - shift, groups)
+            fetches.append(
+                pltpu.make_async_copy(
+                    grads_ref.at[pl.ds(pl.multiple_of(source * width, LANES), width), at],
+                    rows_ref.at[i * width:(i + 1) * width, at],
+                    rows_sems.at[index * count + i],
+                )
+            )
+            fetches[-1].start()
+
+    for i, part in enumerate(parts):
+        value = part[...]
+        coarse = value.astype(jnp.bfloat16)
+        at = slice(i // 2 * width, (i // 2 + 1) * width)
+        first = i % 2 * half
+        terms_ref[first:first + half, at] = coarse
+        terms_ref[rows + first:rows + first + half, at] = (
+            value - coarse.astype(jnp.float32)
+        ).astype(jnp.bfloat16)
+
     if scales:
+        done_ref, sems = refs[-2:]
         squares = jnp.sum(squares_ref[...], axis=0)
-        scale = lax.rsqrt(squares / D + epsilon)
-        value = value * jnp.tile(scale, (1, value.shape[1] // LANES))
-    out_ref[...] = value
+        scale = jnp.tile(lax.rsqrt(squares / D + epsilon), (1, tile // LANES))
+    copies = []
+    for index, at in enumerate(tiles):
+        for fetch in fetches[index * count:(index + 1) * count]:
+            fetch.wait()
+        both = jnp.dot(terms_ref[...], rows_ref[:, at], preferred_element_type=jnp.float32)
+        value = both[:rows] + both[rows:]
+        if adds:
+            value = value + total_ref[:, at]
+        if not scales:
+            out_ref[:, at] = value
+            continue
+        done_ref[:, at] = value * scale
+        copies.append(pltpu.make_async_copy(done_ref.at[:, at], out_ref.at[:, at], sems.at[index]))
+        copies[-1].start()
+    for copy in copies:
+        copy.wait()
 
 
 def product(col, parts, total, squares, grads):
     shifts = tuple(parts)
-    halves = [resident(half) for shift in shifts for half in parts[shift]]
+    halves = [half for shift in shifts for half in parts[shift]]
     half, width = halves[0].shape
-    tokens, columns = grads.shape
-    count = tokens // width
-    tile = 256
-    column_tile = pl.BlockSpec((2 * half, tile), lambda i, c: (0, i))
-    totals = [] if total is None else [total]
-    norms = [] if squares is None else [resident(squares)]
-
-    def rows_of(shift):
-        return pl.BlockSpec(
-            (width, tile), lambda i, c: (lax.rem(c[0] + count - shift, count), i)
-        )
-
+    columns = grads.shape[1]
+    operands = [*halves, *([] if total is None else [total]), *([] if squares is None else [squares])]
+    last = squares is not None
+    shape = (2 * half, columns)
+    depth = len(shifts) * width
+    scratch = [
+        pltpu.VMEM((4 * half, depth), jnp.bfloat16),
+        pltpu.VMEM((depth, columns), jnp.bfloat16),
+        pltpu.SemaphoreType.DMA((len(shifts) * columns // 256,)),
+    ]
+    if last:
+        scratch += [pltpu.VMEM(shape, jnp.float32), pltpu.SemaphoreType.DMA((columns // 256,))]
     return pl.pallas_call(
-        functools.partial(product_kernel, shifts, len(totals), len(norms)),
-        grid_spec=pltpu.PrefetchScalarGridSpec(
-            num_scalar_prefetch=1,
-            grid=(columns // tile,),
-            in_specs=[
-                *[WHOLE] * len(halves),
-                *[column_tile] * len(totals),
-                *[WHOLE] * len(norms),
-                *[rows_of(shift) for shift in shifts],
-            ],
-            out_specs=column_tile,
-            scratch_shapes=[pltpu.VMEM((4 * half, len(shifts) * width), jnp.bfloat16)],
-        ),
-        out_shape=jax.ShapeDtypeStruct((2 * half, columns), jnp.float32),
-    )(col, *halves, *totals, *norms, *[grads] * len(shifts))
+        functools.partial(product_kernel, shifts, int(total is not None), int(last)),
+        in_specs=[SCALAR, *[WHOLE] * len(operands), pl.BlockSpec(memory_space=pl.ANY)],
+        out_specs=pl.BlockSpec(memory_space=pl.ANY) if last else WHOLE,
+        out_shape=jax.ShapeDtypeStruct(shape, jnp.float32) if last else pltpu.VMEM(shape, jnp.float32),
+        scratch_shapes=scratch,
+        compiler_params=PARAMS,
+    )(col, *map(resident, operands), pltpu.with_memory_space_constraint(grads, pltpu.HBM))
 
 
 def col_shift(value, shift):

time: 127 us -> 123 us (0.969)
  Pallas kernels: 21.2 us -> 16.4 us
    pallas_call x3, Pallas kernels: 17 us -> 13 us  [product(): pl.pallas_call(functools.partial(product_kernel, shifts, int(total is not...]
  transfers between devices with their start and end apart: 10 -> 10, of which waited for: 2 -> 3; matrix products, arithmetic and copies ran while one was open for 7% -> 8% of each run, Pallas kernels for 9% -> 7%
where the time goes in v5:
time: 123 us
  waiting for transfers between devices  37.9 us (31%)
  starting transfers between devices  32.3 us (26%)
  blocking collectives  26.1 us (21%)
  Pallas kernels  16.4 us (13%)
  matrix products  7.26 us (6%)
  local copies, waits for them, and re-layouts  1.57 us (1%)
  other arithmetic  1.3 us (1%)
    all_to_all x2, waiting for transfers between devices, exchange(): return lax.all_to_all(value, 'rows', 0, 0, tiled=True)  35.4 us
    all_to_all x1, blocking collectives, exchange(): return lax.all_to_all(value, 'rows', 0, 0, tiled=True)  26.1 us
    all_to_all x2, starting transfers between devices, exchange(): return lax.all_to_all(value, 'rows', 0, 0, tiled=True)  22.3 us
    pallas_call x3, Pallas kernels, product(): pl.pallas_call(functools.partial(product_kernel, shifts, int(total is not...  13 us
    ppermute x6, starting transfers between devices, col_shift(): lax.ppermute(value, 'cols', [(c, (c + shift) % cols) for c in range(cols)])  8.25 us
    dot_general x1, matrix products, staged(): jnp.dot(hidden_acts[0], grads, preferred_element_type=jnp.float32)  7.26 us
    pallas_call x1, Pallas kernels, inner(): pl.pallas_call(functools.partial(inner_kernel, blocks), grid_spec=pltpu.P...  2.91 us
  transfers between devices with their start and end apart: 10, of which 3 were waited for; matrix products, arithmetic and copies ran while one was open for 8% of the time, Pallas kernels for 7%

profile of v5, /device:TPU:1, one launch (start us, length us, event | category | flops | bytes accessed | tf_op | source)
XLA Modules:
  0.0 123.1 jit_solution(14392967259621349124)
XLA Ops:
  0.0 2.9 %shard_map.55 = f32[2624,128]{1,0:T(8,128)} custom-call(s32[1]{0:T(128)} %bitcast.col_ref, bf16[512,432]{1,0:T(8,128)(2,1)} %constant.13.clone.table_ref, s32[1,432]{1,0:T(1,128)} %bitcast.21, s32[2,128]{1,0:T(2,128)} %bitcast.22, bf16[1,432,2560]{2,1,0:T(8,128)(2,1)} %acts_ref.1), custom_call_target="tpu_custom_call" | custom-call | tf_op jit(solution)/shard_map/pallas_call | solution.py:71
  2.9 13.0 %all-to-all-start = ((f32[64,1,5248]{2,1,0:T(1,128)}), f32[64,1,5248]{2,1,0:T(1,128)S(1)}, u32[]{:S(2)}, u32[]{:S(2)}) async-start(f32[64,1,5248]{2,1,0:T(1,128)} %bitcast.4), calls=%async_computation | async-start | bytes 2686976 | tf_op jit(solution)/shard_map/all_to_all | solution.py:234
  15.9 34.8 %all-to-all-done = f32[64,1,5248]{2,1,0:T(1,128)S(1)} async-done(((f32[64,1,5248]{2,1,0:T(1,128)}), f32[64,1,5248]{2,1,0:T(1,128)S(1)}, u32[]{:S(2)}, u32[]{:S(2)}) %all-to-all-start) | async-done | bytes 1343520 | tf_op jit(solution)/shard_map/all_to_all | solution.py:234
  50.7 0.5 shard_map.56
  51.3 26.1 %all_to_all.15 = f32[64,4,640]{2,1,0:T(4,128)S(1)} all-to-all(f32[64,4,640]{2,1,0:T(4,128)S(1)} %shard_map.56), channel_id=1, replica_groups=mesh['rows'=64,'cols'=4] {'rows'}, dimensions={0} | all-to-all | bytes 1310720 | tf_op jit(solution)/shard_map/all_to_all | solution.py:234
  77.4 0.1 reshape.19.refs_0_
  77.5 0.1 reshape.20.refs_1_
  77.7 1.4 %collective-permute-start = (f32[128,640]{1,0:T(8,128)S(1)}, f32[128,640]{1,0:T(8,128)S(1)}, u32[]{:S(2)}, u32[]{:S(2)}) collective-permute-start(f32[128,640]{1,0:T(8,128)S(1)} %reshape.19.refs_0_), channel_id=1, source_target_pairs={{0,1},{1,2},{2,3},{3,0},{4,5},{5,6},{6,7},{7,4},{8,9},{9,10},{10,1... | collective-permute-start | bytes 983048 | tf_op jit(solution)/shard_map/ppermute | solution.py:230
  79.0 1.5 %collective-permute-start.2 = (f32[128,640]{1,0:T(8,128)S(1)}, f32[128,640]{1,0:T(8,128)S(1)}, u32[]{:S(2)}, u32[]{:S(2)}) collective-permute-start(f32[128,640]{1,0:T(8,128)S(1)} %reshape.20.refs_1_), channel_id=1, source_target_pairs={{0,3},{1,0},{2,1},{3,2},{4,7},{5,4},{6,5},{7,6},{8,11},{9,8},{10,9... | collective-permute-start | bytes 983048 | tf_op jit(solution)/shard_map/ppermute | solution.py:230
  80.6 7.3 %fusion.1 = f32[]{:T(128)} fusion(bf16[1,432,2560]{2,1,0:T(8,128)(2,1)} %acts_ref.1, bf16[1,2560,1280]{2,1,0:T(8,128)(2,1)} %param.6), kind=kOutput, calls=%fused_computation.2 | convolution fusion | flops 2832261120 | bytes 8765444 | tf_op jit(solution)/shard_map/dot_general | solution.py:261
  87.8 0.6 broadcast_in_dim.21
  88.6 2.4 %collective-permute-done.6 = f32[8,128]{1,0:T(8,128)S(1)} collective-permute-done((f32[8,128]{1,0:T(8,128)S(1)}, f32[8,128]{1,0:T(8,128)S(1)}, u32[]{:S(2)}, u32[]{:S(2)}) %collective-permute-start.6) | collective-permute-done | bytes 4128 | tf_op jit(solution)/shard_map/ppermute | solution.py:265
  91.0 0.6 broadcast_add_fusion
  91.7 1.6 %collective-permute-start.7 = (f32[8,128]{1,0:T(8,128)S(1)}, f32[8,128]{1,0:T(8,128)S(1)}, u32[]{:S(2)}, u32[]{:S(2)}) collective-permute-start(f32[8,128]{1,0:T(8,128)S(1)} %broadcast_add_fusion), channel_id=1, source_target_pairs={{0,2},{1,3},{2,0},{3,1},{4,6},{5,7},{6,4},{7,5},{8,10},{9,11},{10,... | collective-permute-start | bytes 12296 | tf_op jit(solution)/shard_map/ppermute | solution.py:265
  93.3 0.4 collective-permute-start.4
  93.7 2.3 %collective-permute-start.5 = (f32[128,640]{1,0:T(8,128)S(1)}, f32[128,640]{1,0:T(8,128)S(1)}, u32[]{:S(2)}, u32[]{:S(2)}) collective-permute-start(f32[128,640]{1,0:T(8,128)S(1)} %reshape.19.refs_0_), channel_id=1, source_target_pairs={{0,3},{1,0},{2,1},{3,2},{4,7},{5,4},{6,5},{7,6},{8,11},{9,8},{10,9... | collective-permute-start | bytes 983048 | tf_op jit(solution)/shard_map/ppermute | solution.py:230
  96.0 2.7 %collective-permute-start.3 = (f32[128,640]{1,0:T(8,128)S(1)}, f32[128,640]{1,0:T(8,128)S(1)}, u32[]{:S(2)}, u32[]{:S(2)}) collective-permute-start(f32[128,640]{1,0:T(8,128)S(1)} %collective-permute-done.2.refs_3_), channel_id=1, source_target_pairs={{0,3},{1,0},{2,1},{3,2},{4,7},{5,4},{6,5},{7,6},{8,11},{9,8},{10,9... | collective-permute-start | bytes 983048 | tf_op jit(solution)/shard_map/ppermute | solution.py:230
  98.7 0.6 fusion.6
  99.3 0.6 broadcast_in_dim.22
  100.0 9.4 %all-to-all-start.2 = ((f32[64,1,128]{2,1,0:T(1,128)}), f32[64,1,128]{2,1,0:T(1,128)S(1)}, u32[]{:S(2)}, u32[]{:S(2)}) async-start(f32[64,1,128]{2,1,0:T(1,128)} %broadcast_in_dim.22), calls=%async_computation.2 | async-start | bytes 65536 | tf_op jit(solution)/shard_map/all_to_all | solution.py:234
  109.4 3.6 %shard_map.57.refs_4_ = f32[256,1280]{1,0:T(8,128)S(1)} custom-call(s32[1]{0:T(128)} %bitcast.col_ref, f32[128,640]{1,0:T(8,128)S(1)} %reshape.19.refs_0_, f32[128,640]{1,0:T(8,128)S(1)} %reshape.20.refs_1_, bf16[2560,1280]{1,0:T(8,128)(2,1)} %bitcast.18), custom_call_target="tpu_custom_call" | custom-call | tf_op jit(solution)/shard_map/pallas_call | solution.py:218
  113.0 5.0 %shard_map.58.refs_2_ = f32[256,1280]{1,0:T(8,128)S(1)} custom-call(s32[1]{0:T(128)} %bitcast.col_ref, f32[128,640]{1,0:T(8,128)S(1)} %collective-permute-done.refs_0_, f32[128,640]{1,0:T(8,128)S(1)} %collective-permute-done.4.refs_1_, f32[128,640]{1,0:T(8,128)S(1)} %collective-permute-done.5.refs_2_, f32[128,640]{1,0:T(8,128)S(1)} %collective-permute-done.2.refs_3_, ...), custom_call_target="tpu_custom_call" | custom-call | tf_op jit(solution)/shard_map/pallas_call | solution.py:218
  118.0 0.6 all-to-all-done.2.refs_3_
  118.6 4.4 %shard_map.59 = f32[256,1280]{1,0:T(8,128)} custom-call(s32[1]{0:T(128)} %bitcast.col_ref, f32[128,640]{1,0:T(8,128)S(1)} %collective-permute-done.1.refs_0_, f32[128,640]{1,0:T(8,128)S(1)} %collective-permute-done.3.refs_1_, f32[256,1280]{1,0:T(8,128)S(1)} %shard_map.58.refs_2_, f32[64,1,128]{2,1,0:T(1,128)S(1)} %all-to-all-done.2.refs_3_, ...), custom_call_target="tpu_custom_call" | custom-call | tf_op jit(solution)/shard_map/pallas_call | solution.py:218
  (11 shorter events, 0.2 us)
Async XLA Ops:
  2.9 47.8 %all-to-all-start = ((f32[64,1,5248]{2,1,0:T(1,128)}), f32[64,1,5248]{2,1,0:T(1,128)S(1)}, u32[]{:S(2)}, u32[]{:S(2)}) async-start(f32[64,1,5248]{2,1,0:T(1,128)} %bitcast.4), calls=%async_computation | async-start | bytes 2686976 | tf_op jit(solution)/shard_map/all_to_all | solution.py:234
  77.7 18.3 %collective-permute-start = (f32[128,640]{1,0:T(8,128)S(1)}, f32[128,640]{1,0:T(8,128)S(1)}, u32[]{:S(2)}, u32[]{:S(2)}) collective-permute-start(f32[128,640]{1,0:T(8,128)S(1)} %reshape.19.refs_0_), channel_id=1, source_target_pairs={{0,1},{1,2},{2,3},{3,0},{4,5},{5,6},{6,7},{7,4},{8,9},{9,10},{10,1... | collective-permute-start | bytes 983048 | tf_op jit(solution)/shard_map/ppermute | solution.py:230
  79.0 17.0 %collective-permute-start.2 = (f32[128,640]{1,0:T(8,128)S(1)}, f32[128,640]{1,0:T(8,128)S(1)}, u32[]{:S(2)}, u32[]{:S(2)}) collective-permute-start(f32[128,640]{1,0:T(8,128)S(1)} %reshape.20.refs_1_), channel_id=1, source_target_pairs={{0,3},{1,0},{2,1},{3,2},{4,7},{5,4},{6,5},{7,6},{8,11},{9,8},{10,9... | collective-permute-start | bytes 983048 | tf_op jit(solution)/shard_map/ppermute | solution.py:230
  88.5 2.5 %collective-permute-start.6 = (f32[8,128]{1,0:T(8,128)S(1)}, f32[8,128]{1,0:T(8,128)S(1)}, u32[]{:S(2)}, u32[]{:S(2)}) collective-permute-start(f32[8,128]{1,0:T(8,128)S(1)} %broadcast_in_dim.21), channel_id=1, source_target_pairs={{0,1},{1,0},{2,3},{3,2},{4,5},{5,4},{6,7},{7,6},{8,9},{9,8},{10,11... | collective-permute-start | bytes 12296 | tf_op jit(solution)/shard_map/ppermute | solution.py:265
  91.7 7.0 %collective-permute-start.7 = (f32[8,128]{1,0:T(8,128)S(1)}, f32[8,128]{1,0:T(8,128)S(1)}, u32[]{:S(2)}, u32[]{:S(2)}) collective-permute-start(f32[8,128]{1,0:T(8,128)S(1)} %broadcast_add_fusion), channel_id=1, source_target_pairs={{0,2},{1,3},{2,0},{3,1},{4,6},{5,7},{6,4},{7,5},{8,10},{9,11},{10,... | collective-permute-start | bytes 12296 | tf_op jit(solution)/shard_map/ppermute | solution.py:265
  93.3 19.7 %collective-permute-start.4 = (f32[128,640]{1,0:T(8,128)S(1)}, f32[128,640]{1,0:T(8,128)S(1)}, u32[]{:S(2)}, u32[]{:S(2)}) collective-permute-start(f32[128,640]{1,0:T(8,128)S(1)} %reshape.20.refs_1_), channel_id=1, source_target_pairs={{0,1},{1,2},{2,3},{3,0},{4,5},{5,6},{6,7},{7,4},{8,9},{9,10},{10,1... | collective-permute-start | bytes 983048 | tf_op jit(solution)/shard_map/ppermute | solution.py:230
  93.7 19.3 %collective-permute-start.5 = (f32[128,640]{1,0:T(8,128)S(1)}, f32[128,640]{1,0:T(8,128)S(1)}, u32[]{:S(2)}, u32[]{:S(2)}) collective-permute-start(f32[128,640]{1,0:T(8,128)S(1)} %reshape.19.refs_0_), channel_id=1, source_target_pairs={{0,3},{1,0},{2,1},{3,2},{4,7},{5,4},{6,5},{7,6},{8,11},{9,8},{10,9... | collective-permute-start | bytes 983048 | tf_op jit(solution)/shard_map/ppermute | solution.py:230
  96.0 22.6 %collective-permute-start.1 = (f32[128,640]{1,0:T(8,128)S(1)}, f32[128,640]{1,0:T(8,128)S(1)}, u32[]{:S(2)}, u32[]{:S(2)}) collective-permute-start(f32[128,640]{1,0:T(8,128)S(1)} %collective-permute-done.refs_0_), channel_id=1, source_target_pairs={{0,1},{1,2},{2,3},{3,0},{4,5},{5,6},{6,7},{7,4},{8,9},{9,10},{10,1... | collective-permute-start | bytes 983048 | tf_op jit(solution)/shard_map/ppermute | solution.py:230
  96.0 22.6 %collective-permute-start.3 = (f32[128,640]{1,0:T(8,128)S(1)}, f32[128,640]{1,0:T(8,128)S(1)}, u32[]{:S(2)}, u32[]{:S(2)}) collective-permute-start(f32[128,640]{1,0:T(8,128)S(1)} %collective-permute-done.2.refs_3_), channel_id=1, source_target_pairs={{0,3},{1,0},{2,1},{3,2},{4,7},{5,4},{6,5},{7,6},{8,11},{9,8},{10,9... | collective-permute-start | bytes 983048 | tf_op jit(solution)/shard_map/ppermute | solution.py:230
  100.0 18.6 %all-to-all-start.2 = ((f32[64,1,128]{2,1,0:T(1,128)}), f32[64,1,128]{2,1,0:T(1,128)S(1)}, u32[]{:S(2)}, u32[]{:S(2)}) async-start(f32[64,1,128]{2,1,0:T(1,128)} %broadcast_in_dim.22), calls=%async_computation.2 | async-start | bytes 65536 | tf_op jit(solution)/shard_map/all_to_all | solution.py:234

commit v6 on v5

--- a/solution.py
+++ b/solution.py
@@ -50,16 +50,27 @@
 
 def inner_kernel(blocks, col_ref, table_ref, signs_ref, kept_ref, acts_ref, out_ref):
     tiles = acts_ref.shape[2] // LANES
+    own_rows = acts_ref.shape[1]
     stride = tiles * SUBLANES + 1
-    table = table_ref[...] * signs_ref[...].astype(jnp.float32).astype(jnp.bfloat16)
-    mixed = jnp.dot(table, acts_ref[0], preferred_element_type=jnp.float32)
+    signs = signs_ref[...].astype(jnp.float32).astype(jnp.bfloat16)
+    size = table_ref.shape[0]
+    halves = butterfly(
+        [
+            jnp.dot(
+                table_ref[:, :min(own_rows - first, size)] * signs[:, first:first + size],
+                acts_ref[0, first:first + size],
+                preferred_element_type=jnp.float32,
+            )
+            for first in (0, size)
+        ]
+    )
     kept = kept_ref[...].astype(jnp.float32)
     share = kept.size // blocks
     for block in range(blocks):
-        rows = slice(block * SUBLANES, (block + 1) * SUBLANES)
+        half, first = divmod(block * SUBLANES, size)
         for tile in range(tiles):
-            out_ref[pl.ds(block * stride + tile * SUBLANES, SUBLANES), :] = mixed[
-                rows, tile * LANES:(tile + 1) * LANES
+            out_ref[pl.ds(block * stride + tile * SUBLANES, SUBLANES), :] = halves[half][
+                first:first + SUBLANES, tile * LANES:(tile + 1) * LANES
             ]
         row = block * share // LANES
         out_ref[pl.ds((block + 1) * stride - 1, 1), :] = kept[row:row + 1]
@@ -141,31 +152,46 @@
     )(block, resident(segments))
 
 
-def product_kernel(shifts, adds, scales, col_ref, *refs):
+def product_kernel(shifts, adds, scales, ahead, col_ref, *refs):
     count = len(shifts)
     parts, refs = refs[:2 * count], refs[2 * count:]
-    total_ref = refs[0] if adds else None
-    squares_ref = refs[adds] if scales else None
-    grads_ref, out_ref, terms_ref, rows_ref, rows_sems = refs[adds + scales:adds + scales + 5]
+    total_ref, refs = (refs[0], refs[1:]) if adds else (None, refs)
+    squares, refs = (refs[:2], refs[2:]) if scales else (None, refs)
+    grads_ref, refs = refs[0], refs[1:]
+    if scales:
+        out_ref, terms_ref, done_ref, sems = refs
+        rows_ref = grads_ref
+    else:
+        ahead_ref, refs = (refs[1], refs[:1] + refs[2:]) if ahead else (None, refs)
+        out_ref, terms_ref, rows_ref, rows_sems = refs
     half, width = parts[0].shape
     rows = 2 * half
     columns = grads_ref.shape[1]
-    groups = grads_ref.shape[0] // width
     tile = 256
     tiles = [slice(first, first + tile) for first in range(0, columns, tile)]
 
-    fetches = []
-    for index, at in enumerate(tiles):
-        for i, shift in enumerate(shifts):
-            source = lax.rem(col_ref[0] + groups - shift, groups)
-            fetches.append(
-                pltpu.make_async_copy(
-                    grads_ref.at[pl.ds(pl.multiple_of(source * width, LANES), width), at],
-                    rows_ref.at[i * width:(i + 1) * width, at],
-                    rows_sems.at[index * count + i],
-                )
-            )
-            fetches[-1].start()
+    def fetch(shift, at, out, sem):
+        groups = grads_ref.shape[0] // width
+        source = lax.rem(col_ref[0] + groups - shift, groups)
+        copy = pltpu.make_async_copy(
+            grads_ref.at[pl.ds(pl.multiple_of(source * width, LANES), width), at], out, sem
+        )
+        copy.start()
+        return copy
+
+    fetches = [
+        fetch(
+            shift,
+            at,
+            rows_ref.at[i * width:(i + 1) * width, at],
+            rows_sems.at[index * count + i],
+        )
+        for index, at in enumerate(tiles)
+        for i, shift in enumerate(shifts)
+        if not scales
+    ]
+    if ahead:
+        later = fetch(ahead, slice(None), ahead_ref, rows_sems.at[len(fetches)])
 
     for i, part in enumerate(parts):
         value = part[...]
@@ -178,13 +204,12 @@
         ).astype(jnp.bfloat16)
 
     if scales:
-        done_ref, sems = refs[-2:]
-        squares = jnp.sum(squares_ref[...], axis=0)
+        squares = squares[0][:1] + squares[1][:1]
         scale = jnp.tile(lax.rsqrt(squares / D + epsilon), (1, tile // LANES))
     copies = []
     for index, at in enumerate(tiles):
-        for fetch in fetches[index * count:(index + 1) * count]:
-            fetch.wait()
+        for copy in fetches[index * count:(index + 1) * count]:
+            copy.wait()
         both = jnp.dot(terms_ref[...], rows_ref[:, at], preferred_element_type=jnp.float32)
         value = both[:rows] + both[rows:]
         if adds:
@@ -197,32 +222,46 @@
         copies[-1].start()
     for copy in copies:
         copy.wait()
-
-
-def product(col, parts, total, squares, grads):
+    if ahead:
+        later.wait()
+
+
+def product(col, parts, grads, total=None, squares=None, ahead=None):
     shifts = tuple(parts)
+    last = squares is not None
     halves = [half for shift in shifts for half in parts[shift]]
     half, width = halves[0].shape
     columns = grads.shape[1]
-    operands = [*halves, *([] if total is None else [total]), *([] if squares is None else [squares])]
-    last = squares is not None
+    depth = len(shifts) * width
+    operands = [*halves, *([] if total is None else [total]), *(squares or ())]
     shape = (2 * half, columns)
-    depth = len(shifts) * width
-    scratch = [
-        pltpu.VMEM((4 * half, depth), jnp.bfloat16),
-        pltpu.VMEM((depth, columns), jnp.bfloat16),
-        pltpu.SemaphoreType.DMA((len(shifts) * columns // 256,)),
-    ]
+    anywhere = pl.BlockSpec(memory_space=pl.ANY)
+    scratch = [pltpu.VMEM((4 * half, depth), jnp.bfloat16)]
     if last:
-        scratch += [pltpu.VMEM(shape, jnp.float32), pltpu.SemaphoreType.DMA((columns // 256,))]
+        grads = resident(grads)
+        outs, specs = jax.ShapeDtypeStruct(shape, jnp.float32), anywhere
+        scratch += [
+            pltpu.VMEM(shape, jnp.float32),
+            pltpu.SemaphoreType.DMA((columns // 256,)),
+        ]
+    else:
+        grads = pltpu.with_memory_space_constraint(grads, pltpu.HBM)
+        outs, specs = [pltpu.VMEM(shape, jnp.float32)], [WHOLE]
+        if ahead:
+            outs.append(pltpu.VMEM((width, columns), grads.dtype))
+            specs.append(WHOLE)
+        scratch += [
+            pltpu.VMEM((depth, columns), jnp.bfloat16),
+            pltpu.SemaphoreType.DMA((len(shifts) * columns // 256 + 1,)),
+        ]
     return pl.pallas_call(
-        functools.partial(product_kernel, shifts, int(total is not None), int(last)),
-        in_specs=[SCALAR, *[WHOLE] * len(operands), pl.BlockSpec(memory_space=pl.ANY)],
-        out_specs=pl.BlockSpec(memory_space=pl.ANY) if last else WHOLE,
-        out_shape=jax.ShapeDtypeStruct(shape, jnp.float32) if last else pltpu.VMEM(shape, jnp.float32),
+        functools.partial(product_kernel, shifts, total is not None, last, ahead),
+        in_specs=[SCALAR, *[WHOLE] * len(operands), WHOLE if last else anywhere],
+        out_specs=specs,
+        out_shape=outs,
         scratch_shapes=scratch,
         compiler_params=PARAMS,
-    )(col, *map(resident, operands), pltpu.with_memory_space_constraint(grads, pltpu.HBM))
+    )(col, *map(resident, operands), grads)
 
 
 def col_shift(value, shift):
@@ -240,13 +279,13 @@
     block = lax.axis_index("rows")
     col = lax.axis_index("cols")[None]
     pad_rows = PADDED // row_devices
-    own_rows, tokens = hidden_acts.shape[1:]
+    _, tokens = hidden_acts.shape[1:]
     share = kept_index.shape[0] // row_devices
     group = tokens // cols
     tiles = group // LANES
     grads = out_grads[0]
 
-    table = jnp.asarray(sylvester(pad_rows)[:, :own_rows], dtype=jnp.bfloat16)
+    table = jnp.asarray(sylvester(pad_rows // 2), dtype=jnp.bfloat16)
     segments = inner(
         col,
         table,
@@ -261,12 +300,14 @@
     gradient = jnp.dot(hidden_acts[0], grads, preferred_element_type=jnp.float32)
     squares = jnp.sum(gradient * gradient)
     squares = jnp.broadcast_to(squares, (SUBLANES, LANES))
-    for bit in (1, 2):
-        squares = squares + lax.ppermute(
-            squares, "cols", [(c, c ^ bit) for c in range(cols)]
+    steps = [("y", 1, "cols"), ("y", 2, "cols"), ("c", 1, "rows"), ("x", 16, "rows")]
+    steps += [("x", 32, "rows"), ("z", 2, "rows"), ("z", 4, "rows"), ("z", 8, "rows")]
+    for name, mask, axis in steps:
+        other = lax.ppermute(
+            squares, axis, [(i, i ^ mask) for i in range(lax.axis_size(axis))]
         )
-    squares = jnp.broadcast_to(squares[:1], (row_devices, 1, LANES))
-    squares = exchange(squares)
+        if (name, mask) != steps[-1][:2]:
+            squares = squares + other
 
     kept = mix(block[None], segments, row_devices, share, tiles, 0, group)
     kept = exchange(kept)
@@ -280,9 +321,10 @@
     down_top = col_shift(top, -1)
     far_top = col_shift(up_top, 1)
     far_low = col_shift(down_low, -1)
-    total = product(col, {0: (top, low)}, None, None, grads)
-    total = product(col, {1: (up_top, up_low), cols - 1: (down_top, down_low)}, total, None, grads)
-    total = product(col, {2: (far_top, far_low)}, total, squares, grads)
+    (total,) = product(col, {0: (top, low)}, grads)
+    parts = {1: (up_top, up_low), cols - 1: (down_top, down_low)}
+    total, rows = product(col, parts, grads, total, ahead=2)
+    total = product(col, {2: (far_top, far_low)}, rows, total, (squares, other))
     return total[None]
 
 

time: 123 us -> 138 us (1.12)
  the two profiles are of different devices: /device:TPU:1 before, /device:TPU:24 now
where the time goes in v6:
time: 138 us; the launch traced here: 137 us
  waiting for transfers between devices  56.7 us (41%)
  starting transfers between devices  31.2 us (23%)
  blocking collectives  26.6 us (19%)
  Pallas kernels  13.9 us (10%)
  matrix products  6.59 us (5%)
    all_to_all x1, waiting for transfers between devices, exchange(): return lax.all_to_all(value, 'rows', 0, 0, tiled=True)  34.2 us
    all_to_all x1, blocking collectives, exchange(): return lax.all_to_all(value, 'rows', 0, 0, tiled=True)  26.6 us
    ppermute x8, waiting for transfers between devices, staged(): lax.ppermute(squares, axis, [(i, i ^ mask) for i in range(lax.axis_size(a...  22.4 us
    ppermute x8, starting transfers between devices, staged(): lax.ppermute(squares, axis, [(i, i ^ mask) for i in range(lax.axis_size(a...  12.8 us
    all_to_all x1, starting transfers between devices, exchange(): return lax.all_to_all(value, 'rows', 0, 0, tiled=True)  11.9 us
    pallas_call x3, Pallas kernels, product(): pl.pallas_call(functools.partial(product_kernel, shifts, total is not Non...  10.7 us
    dot_general x1, matrix products, staged(): jnp.dot(hidden_acts[0], grads, preferred_element_type=jnp.float32)  6.59 us
    ppermute x6, starting transfers between devices, col_shift(): lax.ppermute(value, 'cols', [(c, (c + shift) % cols) for c in range(cols)])  6.4 us
  transfers between devices with their start and end apart: 15, of which 7 were waited for; matrix products, arithmetic and copies ran while one was open for 6% of the time, Pallas kernels for 6%

profile of v6, /device:TPU:24, one launch (start us, length us, event | category | flops | bytes accessed | tf_op | source)
XLA Modules:
  0.0 137.5 jit_solution(4870317314153905337)
XLA Ops:
  0.0 2.6 %shard_map.55 = f32[2624,128]{1,0:T(8,128)} custom-call(s32[1]{0:T(128)} %bitcast.col_ref, bf16[256,256]{1,0:T(8,128)(2,1)} %constant.13.clone.table_ref, s32[1,432]{1,0:T(1,128)} %bitcast.18, s32[2,128]{1,0:T(2,128)} %bitcast.19, bf16[1,432,2560]{2,1,0:T(8,128)(2,1)} %acts_ref.1), custom_call_target="tpu_custom_call" | custom-call | tf_op jit(solution)/shard_map/pallas_call | solution.py:82
  2.6 11.9 %all-to-all-start = ((f32[64,1,5248]{2,1,0:T(1,128)}), f32[64,1,5248]{2,1,0:T(1,128)S(1)}, u32[]{:S(2)}, u32[]{:S(2)}) async-start(f32[64,1,5248]{2,1,0:T(1,128)} %bitcast.4), calls=%async_computation | async-start | bytes 2686976 | tf_op jit(solution)/shard_map/all_to_all | solution.py:273
  14.6 34.2 %all-to-all-done = f32[64,1,5248]{2,1,0:T(1,128)S(1)} async-done(((f32[64,1,5248]{2,1,0:T(1,128)}), f32[64,1,5248]{2,1,0:T(1,128)S(1)}, u32[]{:S(2)}, u32[]{:S(2)}) %all-to-all-start) | async-done | bytes 1343520 | tf_op jit(solution)/shard_map/all_to_all | solution.py:273
  49.3 26.6 %all_to_all.10 = f32[64,4,640]{2,1,0:T(4,128)S(1)} all-to-all(f32[64,4,640]{2,1,0:T(4,128)S(1)} %shard_map.56), channel_id=1, replica_groups=mesh['rows'=64,'cols'=4] {'rows'}, dimensions={0} | all-to-all | bytes 1310720 | tf_op jit(solution)/shard_map/all_to_all | solution.py:273
  76.6 1.8 %collective-permute-start.2 = (f32[128,640]{1,0:T(8,128)S(1)}, f32[128,640]{1,0:T(8,128)S(1)}, u32[]{:S(2)}, u32[]{:S(2)}) collective-permute-start(f32[128,640]{1,0:T(8,128)S(1)} %reshape.19.refs_1_), channel_id=1, source_target_pairs={{0,3},{1,0},{2,1},{3,2},{4,7},{5,4},{6,5},{7,6},{8,11},{9,8},{10,9... | collective-permute-start | bytes 983048 | tf_op jit(solution)/shard_map/ppermute | solution.py:269
  78.4 6.6 %fusion.1 = f32[]{:T(128)} fusion(bf16[1,432,2560]{2,1,0:T(8,128)(2,1)S(1)} %copy-done, bf16[1,2560,1280]{2,1,0:T(8,128)(2,1)} %param.6), kind=kOutput, calls=%fused_computation.2 | convolution fusion | flops 2832261120 | bytes 8765444 | tf_op jit(solution)/shard_map/dot_general | solution.py:300
  86.4 1.1 collective-permute-start.4
  87.5 1.0 collective-permute-start.5
  88.5 2.3 %collective-permute-start.1 = (f32[128,640]{1,0:T(8,128)S(1)}, f32[128,640]{1,0:T(8,128)S(1)}, u32[]{:S(2)}, u32[]{:S(2)}) collective-permute-start(f32[128,640]{1,0:T(8,128)S(1)} %collective-permute-done.refs_0_), channel_id=1, source_target_pairs={{0,1},{1,2},{2,3},{3,0},{4,5},{5,6},{6,7},{7,4},{8,9},{9,10},{10,1... | collective-permute-start | bytes 983048 | tf_op jit(solution)/shard_map/ppermute | solution.py:269
  91.4 2.0 %collective-permute-start.7 = (f32[8,128]{1,0:T(8,128)S(1)}, f32[8,128]{1,0:T(8,128)S(1)}, u32[]{:S(2)}, u32[]{:S(2)}) collective-permute-start(f32[8,128]{1,0:T(8,128)S(1)} %broadcast_add_fusion), channel_id=1, source_target_pairs={{0,2},{1,3},{2,0},{3,1},{4,6},{5,7},{6,4},{7,5},{8,10},{9,11},{10,... | collective-permute-start | bytes 12296 | tf_op jit(solution)/shard_map/ppermute | solution.py:306
  93.4 11.3 %collective-permute-done.7 = f32[8,128]{1,0:T(8,128)S(1)} collective-permute-done((f32[8,128]{1,0:T(8,128)S(1)}, f32[8,128]{1,0:T(8,128)S(1)}, u32[]{:S(2)}, u32[]{:S(2)}) %collective-permute-start.7) | collective-permute-done | bytes 4128 | tf_op jit(solution)/shard_map/ppermute | solution.py:306
  105.5 1.2 collective-permute-done.8
  106.6 1.5 %collective-permute-start.9 = (f32[8,128]{1,0:T(8,128)S(1)}, f32[8,128]{1,0:T(8,128)S(1)}, u32[]{:S(2)}, u32[]{:S(2)}) collective-permute-start(f32[8,128]{1,0:T(8,128)S(1)} %add.23), channel_id=1, source_target_pairs={{0,64},{4,68},{8,72},{12,76},{16,80},{20,84},{24,88},{28,92},{32,9... | collective-permute-start | bytes 12296 | tf_op jit(solution)/shard_map/ppermute | solution.py:306
  108.2 2.1 %collective-permute-done.9 = f32[8,128]{1,0:T(8,128)S(1)} collective-permute-done((f32[8,128]{1,0:T(8,128)S(1)}, f32[8,128]{1,0:T(8,128)S(1)}, u32[]{:S(2)}, u32[]{:S(2)}) %collective-permute-start.9) | collective-permute-done | bytes 4128 | tf_op jit(solution)/shard_map/ppermute | solution.py:306
  110.2 3.1 %collective-permute-start.10 = (f32[8,128]{1,0:T(8,128)S(1)}, f32[8,128]{1,0:T(8,128)S(1)}, u32[]{:S(2)}, u32[]{:S(2)}) collective-permute-start(f32[8,128]{1,0:T(8,128)S(1)} %add.24), channel_id=1, source_target_pairs={{0,128},{4,132},{8,136},{12,140},{16,144},{20,148},{24,152},{28,15... | collective-permute-start | bytes 12296 | tf_op jit(solution)/shard_map/ppermute | solution.py:306
  113.4 2.0 %collective-permute-done.10 = f32[8,128]{1,0:T(8,128)S(1)} collective-permute-done((f32[8,128]{1,0:T(8,128)S(1)}, f32[8,128]{1,0:T(8,128)S(1)}, u32[]{:S(2)}, u32[]{:S(2)}) %collective-permute-start.10) | collective-permute-done | bytes 4128 | tf_op jit(solution)/shard_map/ppermute | solution.py:306
  115.4 0.9 collective-permute-start.11
  116.2 2.7 %collective-permute-done.11 = f32[8,128]{1,0:T(8,128)S(1)} collective-permute-done((f32[8,128]{1,0:T(8,128)S(1)}, f32[8,128]{1,0:T(8,128)S(1)}, u32[]{:S(2)}, u32[]{:S(2)}) %collective-permute-start.11) | collective-permute-done | bytes 4128 | tf_op jit(solution)/shard_map/ppermute | solution.py:306
  119.0 1.3 collective-permute-start.12
  120.3 3.2 %collective-permute-done.12 = f32[8,128]{1,0:T(8,128)S(1)} collective-permute-done((f32[8,128]{1,0:T(8,128)S(1)}, f32[8,128]{1,0:T(8,128)S(1)}, u32[]{:S(2)}, u32[]{:S(2)}) %collective-permute-start.12) | collective-permute-done | bytes 4128 | tf_op jit(solution)/shard_map/ppermute | solution.py:306
  123.5 3.0 %collective-permute-start.13 = (f32[8,128]{1,0:T(8,128)S(1)}, f32[8,128]{1,0:T(8,128)S(1)}, u32[]{:S(2)}, u32[]{:S(2)}) collective-permute-start(f32[8,128]{1,0:T(8,128)S(1)} %add.27.refs_3_), channel_id=1, source_target_pairs={{0,32},{4,36},{8,40},{12,44},{16,48},{20,52},{24,56},{28,60},{32,0... | collective-permute-start | bytes 12296 | tf_op jit(solution)/shard_map/ppermute | solution.py:306
  126.5 3.6 %shard_map.57.refs_4_ = f32[256,1280]{1,0:T(8,128)S(1)} custom-call(s32[1]{0:T(128)} %bitcast.col_ref, f32[128,640]{1,0:T(8,128)S(1)} %reshape.18.refs_0_, f32[128,640]{1,0:T(8,128)S(1)} %reshape.19.refs_1_, bf16[2560,1280]{1,0:T(8,128)(2,1)} %bitcast.16), custom_call_target="tpu_custom_call" | custom-call | tf_op jit(solution)/shard_map/pallas_call | solution.py:257
  130.2 5.0 %shard_map.58 = (f32[256,1280]{1,0:T(8,128)S(1)}, bf16[640,1280]{1,0:T(8,128)(2,1)S(1)}) custom-call(s32[1]{0:T(128)} %bitcast.col_ref, f32[128,640]{1,0:T(8,128)S(1)} %collective-permute-done.refs_0_, f32[128,640]{1,0:T(8,128)S(1)} %collective-permute-done.4.refs_1_, f32[128,640]{1,0:T(8,128)S(1)} %collective-permute-done.5.refs_2_, ...), custom_call_target="tpu_custom_call" | custom-call | tf_op jit(solution)/shard_map/pallas_call | solution.py:257
  135.2 2.1 %shard_map.59 = f32[256,1280]{1,0:T(8,128)} custom-call(s32[1]{0:T(128)} %bitcast.col_ref, f32[128,640]{1,0:T(8,128)S(1)} %collective-permute-done.1.refs_0_, f32[128,640]{1,0:T(8,128)S(1)} %collective-permute-done.3.refs_1_, f32[256,1280]{1,0:T(8,128)S(1)} %get-tuple-element.7.refs_2_, f32[8,128]{1,0:T(8,128)S(1)} %add.27.refs_3_, ...), custom_call_target="tpu_custom_call" | custom-call | tf_op jit(solution)/shard_map/pallas_call | solution.py:257
  (26 shorter events, 4.1 us)
Async XLA Ops:
  2.6 46.1 %all-to-all-start = ((f32[64,1,5248]{2,1,0:T(1,128)}), f32[64,1,5248]{2,1,0:T(1,128)S(1)}, u32[]{:S(2)}, u32[]{:S(2)}) async-start(f32[64,1,5248]{2,1,0:T(1,128)} %bitcast.4), calls=%async_computation | async-start | bytes 2686976 | tf_op jit(solution)/shard_map/all_to_all | solution.py:273
  49.3 29.0 %copy-start = (bf16[1,432,2560]{2,1,0:T(8,128)(2,1)S(1)}, bf16[1,432,2560]{2,1,0:T(8,128)(2,1)}, u32[]{:S(2)}) copy-start(bf16[1,432,2560]{2,1,0:T(8,128)(2,1)} %acts_ref.1) | copy-start | bytes 6635524
  76.3 12.2 %collective-permute-start = (f32[128,640]{1,0:T(8,128)S(1)}, f32[128,640]{1,0:T(8,128)S(1)}, u32[]{:S(2)}, u32[]{:S(2)}) collective-permute-start(f32[128,640]{1,0:T(8,128)S(1)} %reshape.18.refs_0_), channel_id=1, source_target_pairs={{0,1},{1,2},{2,3},{3,0},{4,5},{5,6},{6,7},{7,4},{8,9},{9,10},{10,1... | collective-permute-start | bytes 983048 | tf_op jit(solution)/shard_map/ppermute | solution.py:269
  76.6 14.2 %collective-permute-start.2 = (f32[128,640]{1,0:T(8,128)S(1)}, f32[128,640]{1,0:T(8,128)S(1)}, u32[]{:S(2)}, u32[]{:S(2)}) collective-permute-start(f32[128,640]{1,0:T(8,128)S(1)} %reshape.19.refs_1_), channel_id=1, source_target_pairs={{0,3},{1,0},{2,1},{3,2},{4,7},{5,4},{6,5},{7,6},{8,11},{9,8},{10,9... | collective-permute-start | bytes 983048 | tf_op jit(solution)/shard_map/ppermute | solution.py:269
  85.6 5.1 %collective-permute-start.6 = (f32[8,128]{1,0:T(8,128)S(1)}, f32[8,128]{1,0:T(8,128)S(1)}, u32[]{:S(2)}, u32[]{:S(2)}) collective-permute-start(f32[8,128]{1,0:T(8,128)S(1)} %broadcast_in_dim.18), channel_id=1, source_target_pairs={{0,1},{1,0},{2,3},{3,2},{4,5},{5,4},{6,7},{7,6},{8,9},{9,8},{10,11... | collective-permute-start | bytes 12296 | tf_op jit(solution)/shard_map/ppermute | solution.py:306
  86.4 43.7 %collective-permute-start.4 = (f32[128,640]{1,0:T(8,128)S(1)}, f32[128,640]{1,0:T(8,128)S(1)}, u32[]{:S(2)}, u32[]{:S(2)}) collective-permute-start(f32[128,640]{1,0:T(8,128)S(1)} %reshape.19.refs_1_), channel_id=1, source_target_pairs={{0,1},{1,2},{2,3},{3,0},{4,5},{5,6},{6,7},{7,4},{8,9},{9,10},{10,1... | collective-permute-start | bytes 983048 | tf_op jit(solution)/shard_map/ppermute | solution.py:269
  87.5 42.7 %collective-permute-start.5 = (f32[128,640]{1,0:T(8,128)S(1)}, f32[128,640]{1,0:T(8,128)S(1)}, u32[]{:S(2)}, u32[]{:S(2)}) collective-permute-start(f32[128,640]{1,0:T(8,128)S(1)} %reshape.18.refs_0_), channel_id=1, source_target_pairs={{0,3},{1,0},{2,1},{3,2},{4,7},{5,4},{6,5},{7,6},{8,11},{9,8},{10,9... | collective-permute-start | bytes 983048 | tf_op jit(solution)/shard_map/ppermute | solution.py:269
  88.5 46.7 %collective-permute-start.1 = (f32[128,640]{1,0:T(8,128)S(1)}, f32[128,640]{1,0:T(8,128)S(1)}, u32[]{:S(2)}, u32[]{:S(2)}) collective-permute-start(f32[128,640]{1,0:T(8,128)S(1)} %collective-permute-done.refs_0_), channel_id=1, source_target_pairs={{0,1},{1,2},{2,3},{3,0},{4,5},{5,6},{6,7},{7,4},{8,9},{9,10},{10,1... | collective-permute-start | bytes 983048 | tf_op jit(solution)/shard_map/ppermute | solution.py:269
  90.7 44.5 %collective-permute-start.3 = (f32[128,640]{1,0:T(8,128)S(1)}, f32[128,640]{1,0:T(8,128)S(1)}, u32[]{:S(2)}, u32[]{:S(2)}) collective-permute-start(f32[128,640]{1,0:T(8,128)S(1)} %collective-permute-done.2.refs_3_), channel_id=1, source_target_pairs={{0,3},{1,0},{2,1},{3,2},{4,7},{5,4},{6,5},{7,6},{8,11},{9,8},{10,9... | collective-permute-start | bytes 983048 | tf_op jit(solution)/shard_map/ppermute | solution.py:269
  91.4 13.3 %collective-permute-start.7 = (f32[8,128]{1,0:T(8,128)S(1)}, f32[8,128]{1,0:T(8,128)S(1)}, u32[]{:S(2)}, u32[]{:S(2)}) collective-permute-start(f32[8,128]{1,0:T(8,128)S(1)} %broadcast_add_fusion), channel_id=1, source_target_pairs={{0,2},{1,3},{2,0},{3,1},{4,6},{5,7},{6,4},{7,5},{8,10},{9,11},{10,... | collective-permute-start | bytes 12296 | tf_op jit(solution)/shard_map/ppermute | solution.py:306
  105.4 1.3 collective-permute-start.8
  106.6 3.6 %collective-permute-start.9 = (f32[8,128]{1,0:T(8,128)S(1)}, f32[8,128]{1,0:T(8,128)S(1)}, u32[]{:S(2)}, u32[]{:S(2)}) collective-permute-start(f32[8,128]{1,0:T(8,128)S(1)} %add.23), channel_id=1, source_target_pairs={{0,64},{4,68},{8,72},{12,76},{16,80},{20,84},{24,88},{28,92},{32,9... | collective-permute-start | bytes 12296 | tf_op jit(solution)/shard_map/ppermute | solution.py:306
  110.2 5.1 %collective-permute-start.10 = (f32[8,128]{1,0:T(8,128)S(1)}, f32[8,128]{1,0:T(8,128)S(1)}, u32[]{:S(2)}, u32[]{:S(2)}) collective-permute-start(f32[8,128]{1,0:T(8,128)S(1)} %add.24), channel_id=1, source_target_pairs={{0,128},{4,132},{8,136},{12,140},{16,144},{20,148},{24,152},{28,15... | collective-permute-start | bytes 12296 | tf_op jit(solution)/shard_map/ppermute | solution.py:306
  115.4 3.6 %collective-permute-start.11 = (f32[8,128]{1,0:T(8,128)S(1)}, f32[8,128]{1,0:T(8,128)S(1)}, u32[]{:S(2)}, u32[]{:S(2)}) collective-permute-start(f32[8,128]{1,0:T(8,128)S(1)} %add.25), channel_id=1, source_target_pairs={{0,8},{4,12},{8,0},{12,4},{16,24},{20,28},{24,16},{28,20},{32,40},... | collective-permute-start | bytes 12296 | tf_op jit(solution)/shard_map/ppermute | solution.py:306
  119.0 4.5 %collective-permute-start.12 = (f32[8,128]{1,0:T(8,128)S(1)}, f32[8,128]{1,0:T(8,128)S(1)}, u32[]{:S(2)}, u32[]{:S(2)}) collective-permute-start(f32[8,128]{1,0:T(8,128)S(1)} %add.26), channel_id=1, source_target_pairs={{0,16},{4,20},{8,24},{12,28},{16,0},{20,4},{24,8},{28,12},{32,48},... | collective-permute-start | bytes 12296 | tf_op jit(solution)/shard_map/ppermute | solution.py:306
  123.5 11.7 %collective-permute-start.13 = (f32[8,128]{1,0:T(8,128)S(1)}, f32[8,128]{1,0:T(8,128)S(1)}, u32[]{:S(2)}, u32[]{:S(2)}) collective-permute-start(f32[8,128]{1,0:T(8,128)S(1)} %add.27.refs_3_), channel_id=1, source_target_pairs={{0,32},{4,36},{8,40},{12,44},{16,48},{20,52},{24,56},{28,60},{32,0... | collective-permute-start | bytes 12296 | tf_op jit(solution)/shard_map/ppermute | solution.py:306

commit v7 on v6

--- a/solution.py
+++ b/solution.py
@@ -67,12 +67,13 @@
     kept = kept_ref[...].astype(jnp.float32)
     share = kept.size // blocks
     for block in range(blocks):
-        half, first = divmod(block * SUBLANES, size)
+        segment = block % 2 * (blocks // 2) + block // 2
+        half, first = divmod(segment * SUBLANES, size)
         for tile in range(tiles):
             out_ref[pl.ds(block * stride + tile * SUBLANES, SUBLANES), :] = halves[half][
                 first:first + SUBLANES, tile * LANES:(tile + 1) * LANES
             ]
-        row = block * share // LANES
+        row = segment * share // LANES
         out_ref[pl.ds((block + 1) * stride - 1, 1), :] = kept[row:row + 1]
 
 
@@ -98,12 +99,14 @@
 
 
 def mix_kernel(first, tiles, block_ref, segments_ref, kept_ref, position_ref, work_ref):
-    blocks, share, width = kept_ref.shape
+    pairs, _, width = kept_ref.shape
+    blocks, share = 2 * pairs, SUBLANES // 2
     low_count = blocks // 8
     stride = tiles * SUBLANES + 1
 
     sublane = lax.broadcasted_iota(jnp.int32, (SUBLANES, LANES), 0)
-    lane = lax.rem(block_ref[0], LANES // share) * share + jnp.minimum(sublane, share - 1)
+    lane = block_ref[0] // 2 * share + lax.rem(sublane, share)
+    even = (sublane < share) == (lax.rem(block_ref[0], 2) == 0)
     for block in range(blocks):
         row = segments_ref[pl.ds((block + 1) * stride - 1, 1), :]
         row = jnp.broadcast_to(row, (SUBLANES, LANES)).astype(jnp.int32) & (SUBLANES - 1)
@@ -131,11 +134,15 @@
         for low in range(low_count):
             rows = butterfly([work_ref[high * low_count + low] for high in range(8)])
             for high in range(8):
-                block = high * low_count + low
-                picked = jnp.take_along_axis(
-                    rows[high], position_ref[block], axis=0, mode="promise_in_bounds"
+                work_ref[high * low_count + low] = rows[high]
+        for pair in range(pairs):
+            low_block, high_block = [
+                jnp.take_along_axis(
+                    work_ref[block], position_ref[block], axis=0, mode="promise_in_bounds"
                 )
-                kept_ref[block, :, at] = picked[:share]
+                for block in (2 * pair, 2 * pair + 1)
+            ]
+            kept_ref[pair, :, at] = jnp.where(even, low_block, high_block)
 
 
 def mix(block, segments, blocks, share, tiles, start, width):
@@ -143,7 +150,7 @@
         functools.partial(mix_kernel, start // LANES, tiles),
         in_specs=[SCALAR, WHOLE],
         out_specs=WHOLE,
-        out_shape=pltpu.VMEM((blocks, share, width), jnp.float32),
+        out_shape=pltpu.VMEM((blocks // 2, 2 * share, width), jnp.float32),
         compiler_params=PARAMS,
         scratch_shapes=[
             pltpu.VMEM((blocks, SUBLANES, LANES), jnp.int32),
@@ -152,9 +159,9 @@
     )(block, resident(segments))
 
 
-def product_kernel(shifts, adds, scales, ahead, col_ref, *refs):
+def product_kernel(shifts, pieces, adds, scales, ahead, col_ref, core_ref, *refs):
     count = len(shifts)
-    parts, refs = refs[:2 * count], refs[2 * count:]
+    parts, refs = refs[:pieces * count], refs[pieces * count:]
     total_ref, refs = (refs[0], refs[1:]) if adds else (None, refs)
     squares, refs = (refs[:2], refs[2:]) if scales else (None, refs)
     grads_ref, refs = refs[0], refs[1:]
@@ -164,10 +171,11 @@
     else:
         ahead_ref, refs = (refs[1], refs[:1] + refs[2:]) if ahead else (None, refs)
         out_ref, terms_ref, rows_ref, rows_sems = refs
-    half, width = parts[0].shape
-    rows = 2 * half
+    piece, width = parts[0].shape
+    rows = pieces * piece
+    half = rows // 2
     columns = grads_ref.shape[1]
-    tile = 256
+    tile = 256 if scales else columns
     tiles = [slice(first, first + tile) for first in range(0, columns, tile)]
 
     def fetch(shift, at, out, sem):
@@ -196,10 +204,10 @@
     for i, part in enumerate(parts):
         value = part[...]
         coarse = value.astype(jnp.bfloat16)
-        at = slice(i // 2 * width, (i // 2 + 1) * width)
-        first = i % 2 * half
-        terms_ref[first:first + half, at] = coarse
-        terms_ref[rows + first:rows + first + half, at] = (
+        at = slice(i // pieces * width, (i // pieces + 1) * width)
+        first = i % pieces * piece
+        terms_ref[first:first + piece, at] = coarse
+        terms_ref[rows + first:rows + first + piece, at] = (
             value - coarse.astype(jnp.float32)
         ).astype(jnp.bfloat16)
 
@@ -218,31 +226,41 @@
             out_ref[:, at] = value
             continue
         done_ref[:, at] = value * scale
-        copies.append(pltpu.make_async_copy(done_ref.at[:, at], out_ref.at[:, at], sems.at[index]))
-        copies[-1].start()
+        for i in range(2):
+            first = pl.multiple_of(lax.rem(core_ref[0] + i, 2) * half, half)
+            copies.append(
+                pltpu.make_async_copy(
+                    done_ref.at[i * half:(i + 1) * half, at],
+                    out_ref.at[pl.ds(first, half), at],
+                    sems.at[index, i],
+                )
+            )
+            copies[-1].start()
     for copy in copies:
         copy.wait()
     if ahead:
         later.wait()
 
 
-def product(col, parts, grads, total=None, squares=None, ahead=None):
+def product(col, core, parts, grads, total=None, squares=None, ahead=None):
     shifts = tuple(parts)
     last = squares is not None
     halves = [half for shift in shifts for half in parts[shift]]
-    half, width = halves[0].shape
+    piece, width = halves[0].shape
+    pieces = len(halves) // len(shifts)
+    rows = pieces * piece
     columns = grads.shape[1]
     depth = len(shifts) * width
     operands = [*halves, *([] if total is None else [total]), *(squares or ())]
-    shape = (2 * half, columns)
+    shape = (rows, columns)
     anywhere = pl.BlockSpec(memory_space=pl.ANY)
-    scratch = [pltpu.VMEM((4 * half, depth), jnp.bfloat16)]
+    scratch = [pltpu.VMEM((2 * rows, depth), jnp.bfloat16)]
     if last:
         grads = resident(grads)
         outs, specs = jax.ShapeDtypeStruct(shape, jnp.float32), anywhere
         scratch += [
             pltpu.VMEM(shape, jnp.float32),
-            pltpu.SemaphoreType.DMA((columns // 256,)),
+            pltpu.SemaphoreType.DMA((columns // 256, 2)),
         ]
     else:
         grads = pltpu.with_memory_space_constraint(grads, pltpu.HBM)
@@ -255,13 +273,13 @@
             pltpu.SemaphoreType.DMA((len(shifts) * columns // 256 + 1,)),
         ]
     return pl.pallas_call(
-        functools.partial(product_kernel, shifts, total is not None, last, ahead),
-        in_specs=[SCALAR, *[WHOLE] * len(operands), WHOLE if last else anywhere],
+        functools.partial(product_kernel, shifts, pieces, total is not None, last, ahead),
+        in_specs=[SCALAR, SCALAR, *[WHOLE] * len(operands), WHOLE if last else anywhere],
         out_specs=specs,
         out_shape=outs,
         scratch_shapes=scratch,
         compiler_params=PARAMS,
-    )(col, *map(resident, operands), grads)
+    )(col, core, *map(resident, operands), grads)
 
 
 def col_shift(value, shift):
@@ -278,6 +296,7 @@
     cols = lax.axis_size("cols")
     block = lax.axis_index("rows")
     col = lax.axis_index("cols")[None]
+    core = (block & 1)[None]
     pad_rows = PADDED // row_devices
     _, tokens = hidden_acts.shape[1:]
     share = kept_index.shape[0] // row_devices
@@ -309,22 +328,27 @@
         if (name, mask) != steps[-1][:2]:
             squares = squares + other
 
+    cores = [list(range(core, row_devices, 2)) for core in range(2)]
     kept = mix(block[None], segments, row_devices, share, tiles, 0, group)
-    kept = exchange(kept)
-
-    half = row_devices // 2
-    top = kept[:half].reshape(half * share, group)
-    low = kept[half:].reshape(half * share, group)
+    kept = lax.all_to_all(kept, "rows", 0, 0, axis_index_groups=cores, tiled=True)
+
+    half = row_devices // 2 * share
+    top = kept[:, :share].reshape(half, group)
+    low = kept[:, share:].reshape(half, group)
+    low = lax.ppermute(low, "rows", [(i, i ^ 1) for i in range(row_devices)])
     up_top = col_shift(top, 1)
     down_low = col_shift(low, -1)
     up_low = col_shift(low, 1)
     down_top = col_shift(top, -1)
-    far_top = col_shift(up_top, 1)
-    far_low = col_shift(down_low, -1)
-    (total,) = product(col, {0: (top, low)}, grads)
+    part = half // 2
+    far = [col_shift(up_top[:part], 1)]
+    far.append(col_shift(down_top[part:], -1))
+    far.append(col_shift(up_low[:part], 1))
+    far.append(col_shift(down_low[part:], -1))
+    (total,) = product(col, core, {0: (top, low)}, grads)
     parts = {1: (up_top, up_low), cols - 1: (down_top, down_low)}
-    total, rows = product(col, parts, grads, total, ahead=2)
-    total = product(col, {2: (far_top, far_low)}, rows, total, (squares, other))
+    total, rows = product(col, core, parts, grads, total, ahead=2)
+    total = product(col, core, {2: far}, rows, total, (squares, other))
     return total[None]
 
 

time: 138 us -> 134 us (0.971)
  the two profiles are of different devices: /device:TPU:24 before, /device:TPU:2 now
where the time goes in v7:
time: 134 us
  waiting for transfers between devices  47.7 us (36%)
  starting transfers between devices  39.2 us (29%)
  blocking collectives  25.3 us (19%)
  Pallas kernels  11.8 us (9%)
  matrix products  7.34 us (5%)
  other arithmetic  1.39 us (1%)
    all_to_all x1, waiting for transfers between devices, exchange(): return lax.all_to_all(value, 'rows', 0, 0, tiled=True)  33.3 us
    all_to_all x1, blocking collectives, staged(): lax.all_to_all(kept, 'rows', 0, 0, axis_index_groups=cores, tiled=True)  25.3 us
    ppermute x8, waiting for transfers between devices, staged(): lax.ppermute(squares, axis, [(i, i ^ mask) for i in range(lax.axis_size(a...  14.4 us
    ppermute x8, starting transfers between devices, staged(): lax.ppermute(squares, axis, [(i, i ^ mask) for i in range(lax.axis_size(a...  13.6 us
    ppermute x8, starting transfers between devices, col_shift(): lax.ppermute(value, 'cols', [(c, (c + shift) % cols) for c in range(cols)])  13.5 us
    all_to_all x1, starting transfers between devices, exchange(): return lax.all_to_all(value, 'rows', 0, 0, tiled=True)  12 us
    pallas_call x3, Pallas kernels, product(): pl.pallas_call(functools.partial(product_kernel, shifts, pieces, total is...  8.64 us
    dot_general x1, matrix products, staged(): jnp.dot(hidden_acts[0], grads, preferred_element_type=jnp.float32)  7.34 us
  transfers between devices with their start and end apart: 18, of which 7 were waited for; matrix products, arithmetic and copies ran while one was open for 7% of the time, Pallas kernels for 5%

profile of v7, /device:TPU:2, one launch (start us, length us, event | category | flops | bytes accessed | tf_op | source)
XLA Modules:
  0.0 134.1 jit_solution(9275098821410162906)
XLA Ops:
  0.0 2.6 %shard_map.55 = f32[2624,128]{1,0:T(8,128)} custom-call(s32[1]{0:T(128)} %bitcast.col_ref, bf16[256,256]{1,0:T(8,128)(2,1)} %constant.15.clone.table_ref, s32[1,432]{1,0:T(1,128)} %bitcast.19, s32[2,128]{1,0:T(2,128)} %bitcast.20, bf16[1,432,2560]{2,1,0:T(8,128)(2,1)} %acts_ref.1), custom_call_target="tpu_custom_call" | custom-call | tf_op jit(solution)/shard_map/pallas_call | solution.py:83
  2.6 12.0 %all-to-all-start = ((f32[64,1,5248]{2,1,0:T(1,128)}), f32[64,1,5248]{2,1,0:T(1,128)S(1)}, u32[]{:S(2)}, u32[]{:S(2)}) async-start(f32[64,1,5248]{2,1,0:T(1,128)} %bitcast.5), calls=%async_computation | async-start | bytes 2686976 | tf_op jit(solution)/shard_map/all_to_all | solution.py:291
  14.7 33.3 %all-to-all-done = f32[64,1,5248]{2,1,0:T(1,128)S(1)} async-done(((f32[64,1,5248]{2,1,0:T(1,128)}), f32[64,1,5248]{2,1,0:T(1,128)S(1)}, u32[]{:S(2)}, u32[]{:S(2)}) %all-to-all-start) | async-done | bytes 1343520 | tf_op jit(solution)/shard_map/all_to_all | solution.py:291
  48.5 25.3 %all_to_all.10 = f32[32,8,640]{2,1,0:T(8,128)S(1)} all-to-all(f32[32,8,640]{2,1,0:T(8,128)S(1)} %shard_map.56), channel_id=1, replica_groups={{0,8,16,24,32,40,48,56,64,72,80,88,96,104,112,120,128,136,144,152,160,1..., dimensions={0} | all-to-all | bytes 1310720 | tf_op jit(solution)/shard_map/all_to_all | solution.py:333
  74.2 1.6 %collective-permute-start = (f32[128,640]{1,0:T(8,128)S(1)}, f32[128,640]{1,0:T(8,128)S(1)}, u32[]{:S(2)}, u32[]{:S(2)}) collective-permute-start(f32[128,640]{1,0:T(8,128)S(1)} %reshape.18.refs_0_), channel_id=1, source_target_pairs={{0,1},{1,2},{2,3},{3,0},{4,5},{5,6},{6,7},{7,4},{8,9},{9,10},{10,1... | collective-permute-start | bytes 983048 | tf_op jit(solution)/shard_map/ppermute | solution.py:287
  75.9 1.7 %collective-permute-start.2 = (f32[128,640]{1,0:T(8,128)S(1)}, f32[128,640]{1,0:T(8,128)S(1)}, u32[]{:S(2)}, u32[]{:S(2)}) collective-permute-start(f32[128,640]{1,0:T(8,128)S(1)} %reshape.18.refs_0_), channel_id=1, source_target_pairs={{0,3},{1,0},{2,1},{3,2},{4,7},{5,4},{6,5},{7,6},{8,11},{9,8},{10,9... | collective-permute-start | bytes 983048 | tf_op jit(solution)/shard_map/ppermute | solution.py:287
  77.9 2.9 %collective-permute-start.7 = (f32[128,640]{1,0:T(8,128)S(1)}, f32[128,640]{1,0:T(8,128)S(1)}, u32[]{:S(2)}, u32[]{:S(2)}) collective-permute-start(f32[128,640]{1,0:T(8,128)S(1)} %collective-permute-done.4.refs_1_), channel_id=1, source_target_pairs={{0,3},{1,0},{2,1},{3,2},{4,7},{5,4},{6,5},{7,6},{8,11},{9,8},{10,9... | collective-permute-start | bytes 983048 | tf_op jit(solution)/shard_map/ppermute | solution.py:287
  80.8 7.3 %fusion.1 = f32[]{:T(128)} fusion(bf16[1,432,2560]{2,1,0:T(8,128)(2,1)} %acts_ref.1, bf16[1,2560,1280]{2,1,0:T(8,128)(2,1)} %param.6), kind=kOutput, calls=%fused_computation.2 | convolution fusion | flops 2832261120 | bytes 8765444 | tf_op jit(solution)/shard_map/dot_general | solution.py:319
  88.9 3.9 %collective-permute-done.9 = f32[8,128]{1,0:T(8,128)S(1)} collective-permute-done((f32[8,128]{1,0:T(8,128)S(1)}, f32[8,128]{1,0:T(8,128)S(1)}, u32[]{:S(2)}, u32[]{:S(2)}) %collective-permute-start.9) | collective-permute-done | bytes 4128 | tf_op jit(solution)/shard_map/ppermute | solution.py:325
  93.5 3.0 %collective-permute-start.10 = (f32[8,128]{1,0:T(8,128)S(1)}, f32[8,128]{1,0:T(8,128)S(1)}, u32[]{:S(2)}, u32[]{:S(2)}) collective-permute-start(f32[8,128]{1,0:T(8,128)S(1)} %broadcast_add_fusion), channel_id=1, source_target_pairs={{0,2},{1,3},{2,0},{3,1},{4,6},{5,7},{6,4},{7,5},{8,10},{9,11},{10,... | collective-permute-start | bytes 12296 | tf_op jit(solution)/shard_map/ppermute | solution.py:325
  96.6 3.3 %collective-permute-start.3 = (f32[64,640]{1,0:T(8,128)S(1)}, f32[64,640]{1,0:T(8,128)S(1)}, u32[]{:S(2)}, u32[]{:S(2)}) collective-permute-start(f32[64,640]{1,0:T(8,128)S(1)} %slice.26), channel_id=1, source_target_pairs={{0,3},{1,0},{2,1},{3,2},{4,7},{5,4},{6,5},{7,6},{8,11},{9,8},{10,9... | collective-permute-start | bytes 491528 | tf_op jit(solution)/shard_map/ppermute | solution.py:287
  100.2 3.3 %collective-permute-start.8 = (f32[64,640]{1,0:T(8,128)S(1)}, f32[64,640]{1,0:T(8,128)S(1)}, u32[]{:S(2)}, u32[]{:S(2)}) collective-permute-start(f32[64,640]{1,0:T(8,128)S(1)} %slice.29), channel_id=1, source_target_pairs={{0,3},{1,0},{2,1},{3,2},{4,7},{5,4},{6,5},{7,6},{8,11},{9,8},{10,9... | collective-permute-start | bytes 491528 | tf_op jit(solution)/shard_map/ppermute | solution.py:287
  105.5 2.0 %collective-permute-start.12 = (f32[8,128]{1,0:T(8,128)S(1)}, f32[8,128]{1,0:T(8,128)S(1)}, u32[]{:S(2)}, u32[]{:S(2)}) collective-permute-start(f32[8,128]{1,0:T(8,128)S(1)} %add.23), channel_id=1, source_target_pairs={{0,64},{4,68},{8,72},{12,76},{16,80},{20,84},{24,88},{28,92},{32,9... | collective-permute-start | bytes 12296 | tf_op jit(solution)/shard_map/ppermute | solution.py:325
  107.5 1.6 %collective-permute-done.12 = f32[8,128]{1,0:T(8,128)S(1)} collective-permute-done((f32[8,128]{1,0:T(8,128)S(1)}, f32[8,128]{1,0:T(8,128)S(1)}, u32[]{:S(2)}, u32[]{:S(2)}) %collective-permute-start.12) | collective-permute-done | bytes 4128 | tf_op jit(solution)/shard_map/ppermute | solution.py:325
  109.1 1.6 %collective-permute-start.13 = (f32[8,128]{1,0:T(8,128)S(1)}, f32[8,128]{1,0:T(8,128)S(1)}, u32[]{:S(2)}, u32[]{:S(2)}) collective-permute-start(f32[8,128]{1,0:T(8,128)S(1)} %add.24), channel_id=1, source_target_pairs={{0,128},{4,132},{8,136},{12,140},{16,144},{20,148},{24,152},{28,15... | collective-permute-start | bytes 12296 | tf_op jit(solution)/shard_map/ppermute | solution.py:325
  110.7 3.5 %collective-permute-done.13 = f32[8,128]{1,0:T(8,128)S(1)} collective-permute-done((f32[8,128]{1,0:T(8,128)S(1)}, f32[8,128]{1,0:T(8,128)S(1)}, u32[]{:S(2)}, u32[]{:S(2)}) %collective-permute-start.13) | collective-permute-done | bytes 4128 | tf_op jit(solution)/shard_map/ppermute | solution.py:325
  114.2 2.9 %collective-permute-start.14 = (f32[8,128]{1,0:T(8,128)S(1)}, f32[8,128]{1,0:T(8,128)S(1)}, u32[]{:S(2)}, u32[]{:S(2)}) collective-permute-start(f32[8,128]{1,0:T(8,128)S(1)} %add.25), channel_id=1, source_target_pairs={{0,8},{4,12},{8,0},{12,4},{16,24},{20,28},{24,16},{28,20},{32,40},... | collective-permute-start | bytes 12296 | tf_op jit(solution)/shard_map/ppermute | solution.py:325
  117.1 1.6 %collective-permute-done.14 = f32[8,128]{1,0:T(8,128)S(1)} collective-permute-done((f32[8,128]{1,0:T(8,128)S(1)}, f32[8,128]{1,0:T(8,128)S(1)}, u32[]{:S(2)}, u32[]{:S(2)}) %collective-permute-start.14) | collective-permute-done | bytes 4128 | tf_op jit(solution)/shard_map/ppermute | solution.py:325
  118.7 1.8 %collective-permute-start.15 = (f32[8,128]{1,0:T(8,128)S(1)}, f32[8,128]{1,0:T(8,128)S(1)}, u32[]{:S(2)}, u32[]{:S(2)}) collective-permute-start(f32[8,128]{1,0:T(8,128)S(1)} %add.26), channel_id=1, source_target_pairs={{0,16},{4,20},{8,24},{12,28},{16,0},{20,4},{24,8},{28,12},{32,48},... | collective-permute-start | bytes 12296 | tf_op jit(solution)/shard_map/ppermute | solution.py:325
  120.5 2.7 %collective-permute-done.15 = f32[8,128]{1,0:T(8,128)S(1)} collective-permute-done((f32[8,128]{1,0:T(8,128)S(1)}, f32[8,128]{1,0:T(8,128)S(1)}, u32[]{:S(2)}, u32[]{:S(2)}) %collective-permute-start.15) | collective-permute-done | bytes 4128 | tf_op jit(solution)/shard_map/ppermute | solution.py:325
  123.2 2.1 %collective-permute-start.16 = (f32[8,128]{1,0:T(8,128)S(1)}, f32[8,128]{1,0:T(8,128)S(1)}, u32[]{:S(2)}, u32[]{:S(2)}) collective-permute-start(f32[8,128]{1,0:T(8,128)S(1)} %add.27.refs_5_), channel_id=1, source_target_pairs={{0,32},{4,36},{8,40},{12,44},{16,48},{20,52},{24,56},{28,60},{32,0... | collective-permute-start | bytes 12296 | tf_op jit(solution)/shard_map/ppermute | solution.py:325
  125.3 2.7 %shard_map.57.refs_4_ = f32[256,1280]{1,0:T(8,128)S(1)} custom-call(s32[1]{0:T(128)} %bitcast.col_ref, s32[1]{0:T(128)} %bitcast.1.core_ref, f32[128,640]{1,0:T(8,128)S(1)} %reshape.18.refs_0_, f32[128,640]{1,0:T(8,128)S(1)} %collective-permute-done.4.refs_1_, bf16[2560,1280]{1,0:T(8,128)(2,1)} %bitcast.17), custom_call_target="tpu_custom_call" | custom-call | tf_op jit(solution)/shard_map/pallas_call | solution.py:275
  128.0 3.9 %shard_map.58 = (f32[256,1280]{1,0:T(8,128)S(1)}, bf16[640,1280]{1,0:T(8,128)(2,1)S(1)}) custom-call(s32[1]{0:T(128)} %bitcast.col_ref, s32[1]{0:T(128)} %bitcast.1.core_ref, f32[128,640]{1,0:T(8,128)S(1)} %collective-permute-done.refs_0_, f32[128,640]{1,0:T(8,128)S(1)} %collective-permute-done.5.refs_1_, f32[128,640]{1,0:T(8,128)S(1)} %collective-permute-done.2.refs_2_, ...), custom_call_target="tpu_custom_call" | custom-call | tf_op jit(solution)/shard_map/pallas_call | solution.py:275
  131.9 2.1 %shard_map.59 = f32[256,1280]{1,0:T(8,128)} custom-call(s32[1]{0:T(128)} %bitcast.col_ref, s32[1]{0:T(128)} %bitcast.1.core_ref, f32[64,640]{1,0:T(8,128)S(1)} %collective-permute-done.1.refs_0_, f32[64,640]{1,0:T(8,128)S(1)} %collective-permute-done.3.refs_1_, f32[64,640]{1,0:T(8,128)S(1)} %collective-permute-done.6.refs_2_, ...), custom_call_target="tpu_custom_call" | custom-call | tf_op jit(solution)/shard_map/pallas_call | solution.py:275
  (34 shorter events, 5.2 us)
Async XLA Ops:
  2.6 45.3 %all-to-all-start = ((f32[64,1,5248]{2,1,0:T(1,128)}), f32[64,1,5248]{2,1,0:T(1,128)S(1)}, u32[]{:S(2)}, u32[]{:S(2)}) async-start(f32[64,1,5248]{2,1,0:T(1,128)} %bitcast.5), calls=%async_computation | async-start | bytes 2686976 | tf_op jit(solution)/shard_map/all_to_all | solution.py:291
  74.0 3.5 %collective-permute-start.4 = (f32[128,640]{1,0:T(8,128)S(1)}, f32[128,640]{1,0:T(8,128)S(1)}, u32[]{:S(2)}, u32[]{:S(2)}) collective-permute-start(f32[128,640]{1,0:T(8,128)S(1)} %reshape.19), channel_id=1, source_target_pairs={{0,4},{4,0},{8,12},{12,8},{16,20},{20,16},{24,28},{28,24},{32,36},... | collective-permute-start | bytes 983048 | tf_op jit(solution)/shard_map/ppermute | solution.py:338
  74.2 22.3 %collective-permute-start = (f32[128,640]{1,0:T(8,128)S(1)}, f32[128,640]{1,0:T(8,128)S(1)}, u32[]{:S(2)}, u32[]{:S(2)}) collective-permute-start(f32[128,640]{1,0:T(8,128)S(1)} %reshape.18.refs_0_), channel_id=1, source_target_pairs={{0,1},{1,2},{2,3},{3,0},{4,5},{5,6},{6,7},{7,4},{8,9},{9,10},{10,1... | collective-permute-start | bytes 983048 | tf_op jit(solution)/shard_map/ppermute | solution.py:287
  75.9 20.7 %collective-permute-start.2 = (f32[128,640]{1,0:T(8,128)S(1)}, f32[128,640]{1,0:T(8,128)S(1)}, u32[]{:S(2)}, u32[]{:S(2)}) collective-permute-start(f32[128,640]{1,0:T(8,128)S(1)} %reshape.18.refs_0_), channel_id=1, source_target_pairs={{0,3},{1,0},{2,1},{3,2},{4,7},{5,4},{6,5},{7,6},{8,11},{9,8},{10,9... | collective-permute-start | bytes 983048 | tf_op jit(solution)/shard_map/ppermute | solution.py:287
  77.5 22.4 %collective-permute-start.5 = (f32[128,640]{1,0:T(8,128)S(1)}, f32[128,640]{1,0:T(8,128)S(1)}, u32[]{:S(2)}, u32[]{:S(2)}) collective-permute-start(f32[128,640]{1,0:T(8,128)S(1)} %collective-permute-done.4.refs_1_), channel_id=1, source_target_pairs={{0,1},{1,2},{2,3},{3,0},{4,5},{5,6},{6,7},{7,4},{8,9},{9,10},{10,1... | collective-permute-start | bytes 983048 | tf_op jit(solution)/shard_map/ppermute | solution.py:287
  77.9 22.3 %collective-permute-start.7 = (f32[128,640]{1,0:T(8,128)S(1)}, f32[128,640]{1,0:T(8,128)S(1)}, u32[]{:S(2)}, u32[]{:S(2)}) collective-permute-start(f32[128,640]{1,0:T(8,128)S(1)} %collective-permute-done.4.refs_1_), channel_id=1, source_target_pairs={{0,3},{1,0},{2,1},{3,2},{4,7},{5,4},{6,5},{7,6},{8,11},{9,8},{10,9... | collective-permute-start | bytes 983048 | tf_op jit(solution)/shard_map/ppermute | solution.py:287
  88.8 4.0 %collective-permute-start.9 = (f32[8,128]{1,0:T(8,128)S(1)}, f32[8,128]{1,0:T(8,128)S(1)}, u32[]{:S(2)}, u32[]{:S(2)}) collective-permute-start(f32[8,128]{1,0:T(8,128)S(1)} %broadcast_in_dim.22), channel_id=1, source_target_pairs={{0,1},{1,0},{2,3},{3,2},{4,5},{5,4},{6,7},{7,6},{8,9},{9,8},{10,11... | collective-permute-start | bytes 12296 | tf_op jit(solution)/shard_map/ppermute | solution.py:325
  93.5 10.0 %collective-permute-start.10 = (f32[8,128]{1,0:T(8,128)S(1)}, f32[8,128]{1,0:T(8,128)S(1)}, u32[]{:S(2)}, u32[]{:S(2)}) collective-permute-start(f32[8,128]{1,0:T(8,128)S(1)} %broadcast_add_fusion), channel_id=1, source_target_pairs={{0,2},{1,3},{2,0},{3,1},{4,6},{5,7},{6,4},{7,5},{8,10},{9,11},{10,... | collective-permute-start | bytes 12296 | tf_op jit(solution)/shard_map/ppermute | solution.py:325
  96.5 35.4 %collective-permute-start.1 = (f32[64,640]{1,0:T(8,128)S(1)}, f32[64,640]{1,0:T(8,128)S(1)}, u32[]{:S(2)}, u32[]{:S(2)}) collective-permute-start(f32[64,640]{1,0:T(8,128)S(1)} %slice.25), channel_id=1, source_target_pairs={{0,1},{1,2},{2,3},{3,0},{4,5},{5,6},{6,7},{7,4},{8,9},{9,10},{10,1... | collective-permute-start | bytes 491528 | tf_op jit(solution)/shard_map/ppermute | solution.py:287
  96.6 35.3 %collective-permute-start.3 = (f32[64,640]{1,0:T(8,128)S(1)}, f32[64,640]{1,0:T(8,128)S(1)}, u32[]{:S(2)}, u32[]{:S(2)}) collective-permute-start(f32[64,640]{1,0:T(8,128)S(1)} %slice.26), channel_id=1, source_target_pairs={{0,3},{1,0},{2,1},{3,2},{4,7},{5,4},{6,5},{7,6},{8,11},{9,8},{10,9... | collective-permute-start | bytes 491528 | tf_op jit(solution)/shard_map/ppermute | solution.py:287
  99.9 32.0 %collective-permute-start.6 = (f32[64,640]{1,0:T(8,128)S(1)}, f32[64,640]{1,0:T(8,128)S(1)}, u32[]{:S(2)}, u32[]{:S(2)}) collective-permute-start(f32[64,640]{1,0:T(8,128)S(1)} %slice.28), channel_id=1, source_target_pairs={{0,1},{1,2},{2,3},{3,0},{4,5},{5,6},{6,7},{7,4},{8,9},{9,10},{10,1... | collective-permute-start | bytes 491528 | tf_op jit(solution)/shard_map/ppermute | solution.py:287
  100.2 31.7 %collective-permute-start.8 = (f32[64,640]{1,0:T(8,128)S(1)}, f32[64,640]{1,0:T(8,128)S(1)}, u32[]{:S(2)}, u32[]{:S(2)}) collective-permute-start(f32[64,640]{1,0:T(8,128)S(1)} %slice.29), channel_id=1, source_target_pairs={{0,3},{1,0},{2,1},{3,2},{4,7},{5,4},{6,5},{7,6},{8,11},{9,8},{10,9... | collective-permute-start | bytes 491528 | tf_op jit(solution)/shard_map/ppermute | solution.py:287
  104.2 1.3 collective-permute-start.11
  105.5 3.6 %collective-permute-start.12 = (f32[8,128]{1,0:T(8,128)S(1)}, f32[8,128]{1,0:T(8,128)S(1)}, u32[]{:S(2)}, u32[]{:S(2)}) collective-permute-start(f32[8,128]{1,0:T(8,128)S(1)} %add.23), channel_id=1, source_target_pairs={{0,64},{4,68},{8,72},{12,76},{16,80},{20,84},{24,88},{28,92},{32,9... | collective-permute-start | bytes 12296 | tf_op jit(solution)/shard_map/ppermute | solution.py:325
  109.1 5.1 %collective-permute-start.13 = (f32[8,128]{1,0:T(8,128)S(1)}, f32[8,128]{1,0:T(8,128)S(1)}, u32[]{:S(2)}, u32[]{:S(2)}) collective-permute-start(f32[8,128]{1,0:T(8,128)S(1)} %add.24), channel_id=1, source_target_pairs={{0,128},{4,132},{8,136},{12,140},{16,144},{20,148},{24,152},{28,15... | collective-permute-start | bytes 12296 | tf_op jit(solution)/shard_map/ppermute | solution.py:325
  114.2 4.5 %collective-permute-start.14 = (f32[8,128]{1,0:T(8,128)S(1)}, f32[8,128]{1,0:T(8,128)S(1)}, u32[]{:S(2)}, u32[]{:S(2)}) collective-permute-start(f32[8,128]{1,0:T(8,128)S(1)} %add.25), channel_id=1, source_target_pairs={{0,8},{4,12},{8,0},{12,4},{16,24},{20,28},{24,16},{28,20},{32,40},... | collective-permute-start | bytes 12296 | tf_op jit(solution)/shard_map/ppermute | solution.py:325
  118.7 4.5 %collective-permute-start.15 = (f32[8,128]{1,0:T(8,128)S(1)}, f32[8,128]{1,0:T(8,128)S(1)}, u32[]{:S(2)}, u32[]{:S(2)}) collective-permute-start(f32[8,128]{1,0:T(8,128)S(1)} %add.26), channel_id=1, source_target_pairs={{0,16},{4,20},{8,24},{12,28},{16,0},{20,4},{24,8},{28,12},{32,48},... | collective-permute-start | bytes 12296 | tf_op jit(solution)/shard_map/ppermute | solution.py:325
  123.2 8.7 %collective-permute-start.16 = (f32[8,128]{1,0:T(8,128)S(1)}, f32[8,128]{1,0:T(8,128)S(1)}, u32[]{:S(2)}, u32[]{:S(2)}) collective-permute-start(f32[8,128]{1,0:T(8,128)S(1)} %add.27.refs_5_), channel_id=1, source_target_pairs={{0,32},{4,36},{8,40},{12,44},{16,48},{20,52},{24,56},{28,60},{32,0... | collective-permute-start | bytes 12296 | tf_op jit(solution)/shard_map/ppermute | solution.py:325

commit v8 on v6

--- a/solution.py
+++ b/solution.py
@@ -167,8 +167,9 @@
     half, width = parts[0].shape
     rows = 2 * half
     columns = grads_ref.shape[1]
-    tile = 256
-    tiles = [slice(first, first + tile) for first in range(0, columns, tile)]
+    widths = (640, 384, 256) if scales else (columns,)
+    starts = [sum(widths[:i]) for i in range(len(widths))]
+    tiles = [slice(start, start + span) for start, span in zip(starts, widths)]
 
     def fetch(shift, at, out, sem):
         groups = grads_ref.shape[0] // width
@@ -205,7 +206,7 @@
 
     if scales:
         squares = squares[0][:1] + squares[1][:1]
-        scale = jnp.tile(lax.rsqrt(squares / D + epsilon), (1, tile // LANES))
+        scale = jnp.tile(lax.rsqrt(squares / D + epsilon), (1, columns // LANES))
     copies = []
     for index, at in enumerate(tiles):
         for copy in fetches[index * count:(index + 1) * count]:
@@ -217,7 +218,7 @@
         if not scales:
             out_ref[:, at] = value
             continue
-        done_ref[:, at] = value * scale
+        done_ref[:, at] = value * scale[:, at]
         copies.append(pltpu.make_async_copy(done_ref.at[:, at], out_ref.at[:, at], sems.at[index]))
         copies[-1].start()
     for copy in copies:

time: 138 us -> 136 us (0.986)
  Pallas kernels: 13.9 us -> 12 us
    pallas_call x3, Pallas kernels: 10.7 us -> 8.87 us  [product(): pl.pallas_call(functools.partial(product_kernel, shifts, total is not Non...]
  transfers between devices with their start and end apart: 15 -> 15, of which waited for: 7 -> 7; matrix products, arithmetic and copies ran while one was open for 6% -> 6% of each run, Pallas kernels for 6% -> 5%
where the time goes in v8:
time: 136 us
  waiting for transfers between devices  56.7 us (42%)
  starting transfers between devices  31.2 us (23%)
  blocking collectives  26.6 us (20%)
  Pallas kernels  12 us (9%)
  matrix products  6.59 us (5%)
    all_to_all x1, waiting for transfers between devices, exchange(): return lax.all_to_all(value, 'rows', 0, 0, tiled=True)  34.2 us
    all_to_all x1, blocking collectives, exchange(): return lax.all_to_all(value, 'rows', 0, 0, tiled=True)  26.6 us
    ppermute x8, waiting for transfers between devices, staged(): lax.ppermute(squares, axis, [(i, i ^ mask) for i in range(lax.axis_size(a...  22.4 us
    ppermute x8, starting transfers between devices, staged(): lax.ppermute(squares, axis, [(i, i ^ mask) for i in range(lax.axis_size(a...  12.8 us
    all_to_all x1, starting transfers between devices, exchange(): return lax.all_to_all(value, 'rows', 0, 0, tiled=True)  11.9 us
    pallas_call x3, Pallas kernels, product(): pl.pallas_call(functools.partial(product_kernel, shifts, total is not Non...  8.87 us
    dot_general x1, matrix products, staged(): jnp.dot(hidden_acts[0], grads, preferred_element_type=jnp.float32)  6.59 us
    ppermute x6, starting transfers between devices, col_shift(): lax.ppermute(value, 'cols', [(c, (c + shift) % cols) for c in range(cols)])  6.4 us
  transfers between devices with their start and end apart: 15, of which 7 were waited for; matrix products, arithmetic and copies ran while one was open for 6% of the time, Pallas kernels for 5%

profile of v8, /device:TPU:24, one launch (start us, length us, event | category | flops | bytes accessed | tf_op | source)
XLA Modules:
  0.0 135.6 jit_solution(12583364166732036873)
XLA Ops:
  0.0 2.6 %shard_map.55 = f32[2624,128]{1,0:T(8,128)} custom-call(s32[1]{0:T(128)} %bitcast.col_ref, bf16[256,256]{1,0:T(8,128)(2,1)} %constant.13.clone.table_ref, s32[1,432]{1,0:T(1,128)} %bitcast.18, s32[2,128]{1,0:T(2,128)} %bitcast.19, bf16[1,432,2560]{2,1,0:T(8,128)(2,1)} %acts_ref.1), custom_call_target="tpu_custom_call" | custom-call | tf_op jit(solution)/shard_map/pallas_call | solution.py:82
  2.6 11.9 %all-to-all-start = ((f32[64,1,5248]{2,1,0:T(1,128)}), f32[64,1,5248]{2,1,0:T(1,128)S(1)}, u32[]{:S(2)}, u32[]{:S(2)}) async-start(f32[64,1,5248]{2,1,0:T(1,128)} %bitcast.4), calls=%async_computation | async-start | bytes 2686976 | tf_op jit(solution)/shard_map/all_to_all | solution.py:274
  14.6 34.2 %all-to-all-done = f32[64,1,5248]{2,1,0:T(1,128)S(1)} async-done(((f32[64,1,5248]{2,1,0:T(1,128)}), f32[64,1,5248]{2,1,0:T(1,128)S(1)}, u32[]{:S(2)}, u32[]{:S(2)}) %all-to-all-start) | async-done | bytes 1343520 | tf_op jit(solution)/shard_map/all_to_all | solution.py:274
  49.3 26.6 %all_to_all.10 = f32[64,4,640]{2,1,0:T(4,128)S(1)} all-to-all(f32[64,4,640]{2,1,0:T(4,128)S(1)} %shard_map.56), channel_id=1, replica_groups=mesh['rows'=64,'cols'=4] {'rows'}, dimensions={0} | all-to-all | bytes 1310720 | tf_op jit(solution)/shard_map/all_to_all | solution.py:274
  76.6 1.8 %collective-permute-start.2 = (f32[128,640]{1,0:T(8,128)S(1)}, f32[128,640]{1,0:T(8,128)S(1)}, u32[]{:S(2)}, u32[]{:S(2)}) collective-permute-start(f32[128,640]{1,0:T(8,128)S(1)} %reshape.19.refs_1_), channel_id=1, source_target_pairs={{0,3},{1,0},{2,1},{3,2},{4,7},{5,4},{6,5},{7,6},{8,11},{9,8},{10,9... | collective-permute-start | bytes 983048 | tf_op jit(solution)/shard_map/ppermute | solution.py:270
  78.4 6.6 %fusion.1 = f32[]{:T(128)} fusion(bf16[1,432,2560]{2,1,0:T(8,128)(2,1)S(1)} %copy-done, bf16[1,2560,1280]{2,1,0:T(8,128)(2,1)} %param.6), kind=kOutput, calls=%fused_computation.2 | convolution fusion | flops 2832261120 | bytes 8765444 | tf_op jit(solution)/shard_map/dot_general | solution.py:301
  86.4 1.1 collective-permute-start.4
  87.5 1.0 collective-permute-start.5
  88.5 2.3 %collective-permute-start.1 = (f32[128,640]{1,0:T(8,128)S(1)}, f32[128,640]{1,0:T(8,128)S(1)}, u32[]{:S(2)}, u32[]{:S(2)}) collective-permute-start(f32[128,640]{1,0:T(8,128)S(1)} %collective-permute-done.refs_0_), channel_id=1, source_target_pairs={{0,1},{1,2},{2,3},{3,0},{4,5},{5,6},{6,7},{7,4},{8,9},{9,10},{10,1... | collective-permute-start | bytes 983048 | tf_op jit(solution)/shard_map/ppermute | solution.py:270
  91.4 2.0 %collective-permute-start.7 = (f32[8,128]{1,0:T(8,128)S(1)}, f32[8,128]{1,0:T(8,128)S(1)}, u32[]{:S(2)}, u32[]{:S(2)}) collective-permute-start(f32[8,128]{1,0:T(8,128)S(1)} %broadcast_add_fusion), channel_id=1, source_target_pairs={{0,2},{1,3},{2,0},{3,1},{4,6},{5,7},{6,4},{7,5},{8,10},{9,11},{10,... | collective-permute-start | bytes 12296 | tf_op jit(solution)/shard_map/ppermute | solution.py:307
  93.4 11.3 %collective-permute-done.7 = f32[8,128]{1,0:T(8,128)S(1)} collective-permute-done((f32[8,128]{1,0:T(8,128)S(1)}, f32[8,128]{1,0:T(8,128)S(1)}, u32[]{:S(2)}, u32[]{:S(2)}) %collective-permute-start.7) | collective-permute-done | bytes 4128 | tf_op jit(solution)/shard_map/ppermute | solution.py:307
  105.5 1.2 collective-permute-done.8
  106.6 1.5 %collective-permute-start.9 = (f32[8,128]{1,0:T(8,128)S(1)}, f32[8,128]{1,0:T(8,128)S(1)}, u32[]{:S(2)}, u32[]{:S(2)}) collective-permute-start(f32[8,128]{1,0:T(8,128)S(1)} %add.23), channel_id=1, source_target_pairs={{0,64},{4,68},{8,72},{12,76},{16,80},{20,84},{24,88},{28,92},{32,9... | collective-permute-start | bytes 12296 | tf_op jit(solution)/shard_map/ppermute | solution.py:307
  108.2 2.1 %collective-permute-done.9 = f32[8,128]{1,0:T(8,128)S(1)} collective-permute-done((f32[8,128]{1,0:T(8,128)S(1)}, f32[8,128]{1,0:T(8,128)S(1)}, u32[]{:S(2)}, u32[]{:S(2)}) %collective-permute-start.9) | collective-permute-done | bytes 4128 | tf_op jit(solution)/shard_map/ppermute | solution.py:307
  110.2 3.1 %collective-permute-start.10 = (f32[8,128]{1,0:T(8,128)S(1)}, f32[8,128]{1,0:T(8,128)S(1)}, u32[]{:S(2)}, u32[]{:S(2)}) collective-permute-start(f32[8,128]{1,0:T(8,128)S(1)} %add.24), channel_id=1, source_target_pairs={{0,128},{4,132},{8,136},{12,140},{16,144},{20,148},{24,152},{28,15... | collective-permute-start | bytes 12296 | tf_op jit(solution)/shard_map/ppermute | solution.py:307
  113.4 2.0 %collective-permute-done.10 = f32[8,128]{1,0:T(8,128)S(1)} collective-permute-done((f32[8,128]{1,0:T(8,128)S(1)}, f32[8,128]{1,0:T(8,128)S(1)}, u32[]{:S(2)}, u32[]{:S(2)}) %collective-permute-start.10) | collective-permute-done | bytes 4128 | tf_op jit(solution)/shard_map/ppermute | solution.py:307
  115.4 0.9 collective-permute-start.11
  116.2 2.7 %collective-permute-done.11 = f32[8,128]{1,0:T(8,128)S(1)} collective-permute-done((f32[8,128]{1,0:T(8,128)S(1)}, f32[8,128]{1,0:T(8,128)S(1)}, u32[]{:S(2)}, u32[]{:S(2)}) %collective-permute-start.11) | collective-permute-done | bytes 4128 | tf_op jit(solution)/shard_map/ppermute | solution.py:307
  119.0 1.3 collective-permute-start.12
  120.3 3.2 %collective-permute-done.12 = f32[8,128]{1,0:T(8,128)S(1)} collective-permute-done((f32[8,128]{1,0:T(8,128)S(1)}, f32[8,128]{1,0:T(8,128)S(1)}, u32[]{:S(2)}, u32[]{:S(2)}) %collective-permute-start.12) | collective-permute-done | bytes 4128 | tf_op jit(solution)/shard_map/ppermute | solution.py:307
  123.5 3.0 %collective-permute-start.13 = (f32[8,128]{1,0:T(8,128)S(1)}, f32[8,128]{1,0:T(8,128)S(1)}, u32[]{:S(2)}, u32[]{:S(2)}) collective-permute-start(f32[8,128]{1,0:T(8,128)S(1)} %add.27.refs_3_), channel_id=1, source_target_pairs={{0,32},{4,36},{8,40},{12,44},{16,48},{20,52},{24,56},{28,60},{32,0... | collective-permute-start | bytes 12296 | tf_op jit(solution)/shard_map/ppermute | solution.py:307
  126.5 2.7 %shard_map.57.refs_4_ = f32[256,1280]{1,0:T(8,128)S(1)} custom-call(s32[1]{0:T(128)} %bitcast.col_ref, f32[128,640]{1,0:T(8,128)S(1)} %reshape.18.refs_0_, f32[128,640]{1,0:T(8,128)S(1)} %reshape.19.refs_1_, bf16[2560,1280]{1,0:T(8,128)(2,1)} %bitcast.16), custom_call_target="tpu_custom_call" | custom-call | tf_op jit(solution)/shard_map/pallas_call | solution.py:258
  129.2 3.9 %shard_map.58 = (f32[256,1280]{1,0:T(8,128)S(1)}, bf16[640,1280]{1,0:T(8,128)(2,1)S(1)}) custom-call(s32[1]{0:T(128)} %bitcast.col_ref, f32[128,640]{1,0:T(8,128)S(1)} %collective-permute-done.refs_0_, f32[128,640]{1,0:T(8,128)S(1)} %collective-permute-done.4.refs_1_, f32[128,640]{1,0:T(8,128)S(1)} %collective-permute-done.5.refs_2_, ...), custom_call_target="tpu_custom_call" | custom-call | tf_op jit(solution)/shard_map/pallas_call | solution.py:258
  133.2 2.3 %shard_map.59 = f32[256,1280]{1,0:T(8,128)} custom-call(s32[1]{0:T(128)} %bitcast.col_ref, f32[128,640]{1,0:T(8,128)S(1)} %collective-permute-done.1.refs_0_, f32[128,640]{1,0:T(8,128)S(1)} %collective-permute-done.3.refs_1_, f32[256,1280]{1,0:T(8,128)S(1)} %get-tuple-element.7.refs_2_, f32[8,128]{1,0:T(8,128)S(1)} %add.27.refs_3_, ...), custom_call_target="tpu_custom_call" | custom-call | tf_op jit(solution)/shard_map/pallas_call | solution.py:258
  (26 shorter events, 4.1 us)
Async XLA Ops:
  2.6 46.1 %all-to-all-start = ((f32[64,1,5248]{2,1,0:T(1,128)}), f32[64,1,5248]{2,1,0:T(1,128)S(1)}, u32[]{:S(2)}, u32[]{:S(2)}) async-start(f32[64,1,5248]{2,1,0:T(1,128)} %bitcast.4), calls=%async_computation | async-start | bytes 2686976 | tf_op jit(solution)/shard_map/all_to_all | solution.py:274
  49.3 29.0 %copy-start = (bf16[1,432,2560]{2,1,0:T(8,128)(2,1)S(1)}, bf16[1,432,2560]{2,1,0:T(8,128)(2,1)}, u32[]{:S(2)}) copy-start(bf16[1,432,2560]{2,1,0:T(8,128)(2,1)} %acts_ref.1) | copy-start | bytes 6635524
  76.3 12.2 %collective-permute-start = (f32[128,640]{1,0:T(8,128)S(1)}, f32[128,640]{1,0:T(8,128)S(1)}, u32[]{:S(2)}, u32[]{:S(2)}) collective-permute-start(f32[128,640]{1,0:T(8,128)S(1)} %reshape.18.refs_0_), channel_id=1, source_target_pairs={{0,1},{1,2},{2,3},{3,0},{4,5},{5,6},{6,7},{7,4},{8,9},{9,10},{10,1... | collective-permute-start | bytes 983048 | tf_op jit(solution)/shard_map/ppermute | solution.py:270
  76.6 14.2 %collective-permute-start.2 = (f32[128,640]{1,0:T(8,128)S(1)}, f32[128,640]{1,0:T(8,128)S(1)}, u32[]{:S(2)}, u32[]{:S(2)}) collective-permute-start(f32[128,640]{1,0:T(8,128)S(1)} %reshape.19.refs_1_), channel_id=1, source_target_pairs={{0,3},{1,0},{2,1},{3,2},{4,7},{5,4},{6,5},{7,6},{8,11},{9,8},{10,9... | collective-permute-start | bytes 983048 | tf_op jit(solution)/shard_map/ppermute | solution.py:270
  85.6 5.1 %collective-permute-start.6 = (f32[8,128]{1,0:T(8,128)S(1)}, f32[8,128]{1,0:T(8,128)S(1)}, u32[]{:S(2)}, u32[]{:S(2)}) collective-permute-start(f32[8,128]{1,0:T(8,128)S(1)} %broadcast_in_dim.18), channel_id=1, source_target_pairs={{0,1},{1,0},{2,3},{3,2},{4,5},{5,4},{6,7},{7,6},{8,9},{9,8},{10,11... | collective-permute-start | bytes 12296 | tf_op jit(solution)/shard_map/ppermute | solution.py:307
  86.4 42.8 %collective-permute-start.4 = (f32[128,640]{1,0:T(8,128)S(1)}, f32[128,640]{1,0:T(8,128)S(1)}, u32[]{:S(2)}, u32[]{:S(2)}) collective-permute-start(f32[128,640]{1,0:T(8,128)S(1)} %reshape.19.refs_1_), channel_id=1, source_target_pairs={{0,1},{1,2},{2,3},{3,0},{4,5},{5,6},{6,7},{7,4},{8,9},{9,10},{10,1... | collective-permute-start | bytes 983048 | tf_op jit(solution)/shard_map/ppermute | solution.py:270
  87.5 41.7 %collective-permute-start.5 = (f32[128,640]{1,0:T(8,128)S(1)}, f32[128,640]{1,0:T(8,128)S(1)}, u32[]{:S(2)}, u32[]{:S(2)}) collective-permute-start(f32[128,640]{1,0:T(8,128)S(1)} %reshape.18.refs_0_), channel_id=1, source_target_pairs={{0,3},{1,0},{2,1},{3,2},{4,7},{5,4},{6,5},{7,6},{8,11},{9,8},{10,9... | collective-permute-start | bytes 983048 | tf_op jit(solution)/shard_map/ppermute | solution.py:270
  88.5 44.7 %collective-permute-start.1 = (f32[128,640]{1,0:T(8,128)S(1)}, f32[128,640]{1,0:T(8,128)S(1)}, u32[]{:S(2)}, u32[]{:S(2)}) collective-permute-start(f32[128,640]{1,0:T(8,128)S(1)} %collective-permute-done.refs_0_), channel_id=1, source_target_pairs={{0,1},{1,2},{2,3},{3,0},{4,5},{5,6},{6,7},{7,4},{8,9},{9,10},{10,1... | collective-permute-start | bytes 983048 | tf_op jit(solution)/shard_map/ppermute | solution.py:270
  90.7 42.4 %collective-permute-start.3 = (f32[128,640]{1,0:T(8,128)S(1)}, f32[128,640]{1,0:T(8,128)S(1)}, u32[]{:S(2)}, u32[]{:S(2)}) collective-permute-start(f32[128,640]{1,0:T(8,128)S(1)} %collective-permute-done.2.refs_3_), channel_id=1, source_target_pairs={{0,3},{1,0},{2,1},{3,2},{4,7},{5,4},{6,5},{7,6},{8,11},{9,8},{10,9... | collective-permute-start | bytes 983048 | tf_op jit(solution)/shard_map/ppermute | solution.py:270
  91.4 13.3 %collective-permute-start.7 = (f32[8,128]{1,0:T(8,128)S(1)}, f32[8,128]{1,0:T(8,128)S(1)}, u32[]{:S(2)}, u32[]{:S(2)}) collective-permute-start(f32[8,128]{1,0:T(8,128)S(1)} %broadcast_add_fusion), channel_id=1, source_target_pairs={{0,2},{1,3},{2,0},{3,1},{4,6},{5,7},{6,4},{7,5},{8,10},{9,11},{10,... | collective-permute-start | bytes 12296 | tf_op jit(solution)/shard_map/ppermute | solution.py:307
  105.4 1.3 collective-permute-start.8
  106.6 3.6 %collective-permute-start.9 = (f32[8,128]{1,0:T(8,128)S(1)}, f32[8,128]{1,0:T(8,128)S(1)}, u32[]{:S(2)}, u32[]{:S(2)}) collective-permute-start(f32[8,128]{1,0:T(8,128)S(1)} %add.23), channel_id=1, source_target_pairs={{0,64},{4,68},{8,72},{12,76},{16,80},{20,84},{24,88},{28,92},{32,9... | collective-permute-start | bytes 12296 | tf_op jit(solution)/shard_map/ppermute | solution.py:307
  110.2 5.1 %collective-permute-start.10 = (f32[8,128]{1,0:T(8,128)S(1)}, f32[8,128]{1,0:T(8,128)S(1)}, u32[]{:S(2)}, u32[]{:S(2)}) collective-permute-start(f32[8,128]{1,0:T(8,128)S(1)} %add.24), channel_id=1, source_target_pairs={{0,128},{4,132},{8,136},{12,140},{16,144},{20,148},{24,152},{28,15... | collective-permute-start | bytes 12296 | tf_op jit(solution)/shard_map/ppermute | solution.py:307
  115.4 3.6 %collective-permute-start.11 = (f32[8,128]{1,0:T(8,128)S(1)}, f32[8,128]{1,0:T(8,128)S(1)}, u32[]{:S(2)}, u32[]{:S(2)}) collective-permute-start(f32[8,128]{1,0:T(8,128)S(1)} %add.25), channel_id=1, source_target_pairs={{0,8},{4,12},{8,0},{12,4},{16,24},{20,28},{24,16},{28,20},{32,40},... | collective-permute-start | bytes 12296 | tf_op jit(solution)/shard_map/ppermute | solution.py:307
  119.0 4.5 %collective-permute-start.12 = (f32[8,128]{1,0:T(8,128)S(1)}, f32[8,128]{1,0:T(8,128)S(1)}, u32[]{:S(2)}, u32[]{:S(2)}) collective-permute-start(f32[8,128]{1,0:T(8,128)S(1)} %add.26), channel_id=1, source_target_pairs={{0,16},{4,20},{8,24},{12,28},{16,0},{20,4},{24,8},{28,12},{32,48},... | collective-permute-start | bytes 12296 | tf_op jit(solution)/shard_map/ppermute | solution.py:307
  123.5 9.7 %collective-permute-start.13 = (f32[8,128]{1,0:T(8,128)S(1)}, f32[8,128]{1,0:T(8,128)S(1)}, u32[]{:S(2)}, u32[]{:S(2)}) collective-permute-start(f32[8,128]{1,0:T(8,128)S(1)} %add.27.refs_3_), channel_id=1, source_target_pairs={{0,32},{4,36},{8,40},{12,44},{16,48},{20,52},{24,56},{28,60},{32,0... | collective-permute-start | bytes 12296 | tf_op jit(solution)/shard_map/ppermute | solution.py:307

commit v9 on v6

--- a/solution.py
+++ b/solution.py
@@ -48,7 +48,9 @@
     return rows
 
 
-def inner_kernel(blocks, col_ref, table_ref, signs_ref, kept_ref, acts_ref, out_ref):
+def inner_kernel(
+    blocks, col_ref, table_ref, signs_ref, kept_ref, acts_ref, out_ref, done_ref, sems
+):
     tiles = acts_ref.shape[2] // LANES
     own_rows = acts_ref.shape[1]
     stride = tiles * SUBLANES + 1
@@ -66,14 +68,24 @@
     )
     kept = kept_ref[...].astype(jnp.float32)
     share = kept.size // blocks
+    copies = []
+    run = blocks // sems.shape[0]
     for block in range(blocks):
         half, first = divmod(block * SUBLANES, size)
         for tile in range(tiles):
-            out_ref[pl.ds(block * stride + tile * SUBLANES, SUBLANES), :] = halves[half][
+            done_ref[pl.ds(block * stride + tile * SUBLANES, SUBLANES), :] = halves[half][
                 first:first + SUBLANES, tile * LANES:(tile + 1) * LANES
             ]
         row = block * share // LANES
-        out_ref[pl.ds((block + 1) * stride - 1, 1), :] = kept[row:row + 1]
+        done_ref[pl.ds((block + 1) * stride - 1, 1), :] = kept[row:row + 1]
+        if (block + 1) % run == 0:
+            part = pl.ds((block + 1 - run) * stride, run * stride)
+            copies.append(
+                pltpu.make_async_copy(done_ref.at[part], out_ref.at[part], sems.at[block // run])
+            )
+            copies[-1].start()
+    for copy in copies:
+        copy.wait()
 
 
 def inner(col, table, signs, kept, acts, blocks, width):
@@ -90,9 +102,13 @@
                 pl.BlockSpec(kept.shape, lambda i, c: (0, 0)),
                 pl.BlockSpec((1, own_rows, width), lambda i, c: (0, 0, c[0])),
             ],
-            out_specs=WHOLE,
+            out_specs=pl.BlockSpec(memory_space=pl.ANY),
+            scratch_shapes=[
+                pltpu.VMEM((rows, LANES), jnp.float32),
+                pltpu.SemaphoreType.DMA((4,)),
+            ],
         ),
-        out_shape=pltpu.VMEM((rows, LANES), jnp.float32),
+        out_shape=jax.ShapeDtypeStruct((rows, LANES), jnp.float32),
         compiler_params=PARAMS,
     )(col, *[pltpu.with_memory_space_constraint(v, pltpu.HBM) for v in (table, signs, kept, acts)])
 

time: 138 us -> 138 us (level)
  no operation moved by 1% of the time
where the time goes in v9:
time: 138 us; the launch traced here: 137 us
  waiting for transfers between devices  56.7 us (41%)
  starting transfers between devices  31.2 us (23%)
  blocking collectives  26.6 us (19%)
  Pallas kernels  13.9 us (10%)
  matrix products  6.59 us (5%)
    all_to_all x1, waiting for transfers between devices, exchange(): return lax.all_to_all(value, 'rows', 0, 0, tiled=True)  34.2 us
    all_to_all x1, blocking collectives, exchange(): return lax.all_to_all(value, 'rows', 0, 0, tiled=True)  26.6 us
    ppermute x8, waiting for transfers between devices, staged(): lax.ppermute(squares, axis, [(i, i ^ mask) for i in range(lax.axis_size(a...  22.5 us
    ppermute x8, starting transfers between devices, staged(): lax.ppermute(squares, axis, [(i, i ^ mask) for i in range(lax.axis_size(a...  12.8 us
    all_to_all x1, starting transfers between devices, exchange(): return lax.all_to_all(value, 'rows', 0, 0, tiled=True)  11.9 us
    pallas_call x3, Pallas kernels, product(): pl.pallas_call(functools.partial(product_kernel, shifts, total is not Non...  10.7 us
    dot_general x1, matrix products, staged(): jnp.dot(hidden_acts[0], grads, preferred_element_type=jnp.float32)  6.59 us
    ppermute x6, starting transfers between devices, col_shift(): lax.ppermute(value, 'cols', [(c, (c + shift) % cols) for c in range(cols)])  6.4 us
  transfers between devices with their start and end apart: 15, of which 7 were waited for; matrix products, arithmetic and copies ran while one was open for 6% of the time, Pallas kernels for 6%

profile of v9, /device:TPU:24, one launch (start us, length us, event | category | flops | bytes accessed | tf_op | source)
XLA Modules:
  0.0 137.5 jit_solution(16278329151397454428)
XLA Ops:
  0.0 2.6 %shard_map.55 = f32[2624,128]{1,0:T(8,128)} custom-call(s32[1]{0:T(128)} %bitcast.col_ref, bf16[256,256]{1,0:T(8,128)(2,1)} %constant.13.clone.table_ref, s32[1,432]{1,0:T(1,128)} %bitcast.18, s32[2,128]{1,0:T(2,128)} %bitcast.19, bf16[1,432,2560]{2,1,0:T(8,128)(2,1)} %acts_ref.1), custom_call_target="tpu_custom_call" | custom-call | tf_op jit(solution)/shard_map/pallas_call | solution.py:94
  2.6 11.9 %all-to-all-start = ((f32[64,1,5248]{2,1,0:T(1,128)}), f32[64,1,5248]{2,1,0:T(1,128)S(1)}, u32[]{:S(2)}, u32[]{:S(2)}) async-start(f32[64,1,5248]{2,1,0:T(1,128)} %bitcast.4), calls=%async_computation | async-start | bytes 2686976 | tf_op jit(solution)/shard_map/all_to_all | solution.py:289
  14.6 34.2 %all-to-all-done = f32[64,1,5248]{2,1,0:T(1,128)S(1)} async-done(((f32[64,1,5248]{2,1,0:T(1,128)}), f32[64,1,5248]{2,1,0:T(1,128)S(1)}, u32[]{:S(2)}, u32[]{:S(2)}) %all-to-all-start) | async-done | bytes 1343520 | tf_op jit(solution)/shard_map/all_to_all | solution.py:289
  49.3 26.6 %all_to_all.10 = f32[64,4,640]{2,1,0:T(4,128)S(1)} all-to-all(f32[64,4,640]{2,1,0:T(4,128)S(1)} %shard_map.56), channel_id=1, replica_groups=mesh['rows'=64,'cols'=4] {'rows'}, dimensions={0} | all-to-all | bytes 1310720 | tf_op jit(solution)/shard_map/all_to_all | solution.py:289
  76.6 1.8 %collective-permute-start.2 = (f32[128,640]{1,0:T(8,128)S(1)}, f32[128,640]{1,0:T(8,128)S(1)}, u32[]{:S(2)}, u32[]{:S(2)}) collective-permute-start(f32[128,640]{1,0:T(8,128)S(1)} %reshape.19.refs_1_), channel_id=1, source_target_pairs={{0,3},{1,0},{2,1},{3,2},{4,7},{5,4},{6,5},{7,6},{8,11},{9,8},{10,9... | collective-permute-start | bytes 983048 | tf_op jit(solution)/shard_map/ppermute | solution.py:285
  78.4 6.6 %fusion.1 = f32[]{:T(128)} fusion(bf16[1,432,2560]{2,1,0:T(8,128)(2,1)S(1)} %copy-done, bf16[1,2560,1280]{2,1,0:T(8,128)(2,1)} %param.6), kind=kOutput, calls=%fused_computation.2 | convolution fusion | flops 2832261120 | bytes 8765444 | tf_op jit(solution)/shard_map/dot_general | solution.py:316
  86.5 1.1 collective-permute-start.4
  87.5 1.0 collective-permute-start.5
  88.5 2.3 %collective-permute-start.1 = (f32[128,640]{1,0:T(8,128)S(1)}, f32[128,640]{1,0:T(8,128)S(1)}, u32[]{:S(2)}, u32[]{:S(2)}) collective-permute-start(f32[128,640]{1,0:T(8,128)S(1)} %collective-permute-done.refs_0_), channel_id=1, source_target_pairs={{0,1},{1,2},{2,3},{3,0},{4,5},{5,6},{6,7},{7,4},{8,9},{9,10},{10,1... | collective-permute-start | bytes 983048 | tf_op jit(solution)/shard_map/ppermute | solution.py:285
  91.4 2.0 %collective-permute-start.7 = (f32[8,128]{1,0:T(8,128)S(1)}, f32[8,128]{1,0:T(8,128)S(1)}, u32[]{:S(2)}, u32[]{:S(2)}) collective-permute-start(f32[8,128]{1,0:T(8,128)S(1)} %broadcast_add_fusion), channel_id=1, source_target_pairs={{0,2},{1,3},{2,0},{3,1},{4,6},{5,7},{6,4},{7,5},{8,10},{9,11},{10,... | collective-permute-start | bytes 12296 | tf_op jit(solution)/shard_map/ppermute | solution.py:322
  93.4 11.3 %collective-permute-done.7 = f32[8,128]{1,0:T(8,128)S(1)} collective-permute-done((f32[8,128]{1,0:T(8,128)S(1)}, f32[8,128]{1,0:T(8,128)S(1)}, u32[]{:S(2)}, u32[]{:S(2)}) %collective-permute-start.7) | collective-permute-done | bytes 4128 | tf_op jit(solution)/shard_map/ppermute | solution.py:322
  105.5 1.2 collective-permute-done.8
  106.7 1.5 %collective-permute-start.9 = (f32[8,128]{1,0:T(8,128)S(1)}, f32[8,128]{1,0:T(8,128)S(1)}, u32[]{:S(2)}, u32[]{:S(2)}) collective-permute-start(f32[8,128]{1,0:T(8,128)S(1)} %add.23), channel_id=1, source_target_pairs={{0,64},{4,68},{8,72},{12,76},{16,80},{20,84},{24,88},{28,92},{32,9... | collective-permute-start | bytes 12296 | tf_op jit(solution)/shard_map/ppermute | solution.py:322
  108.2 2.1 %collective-permute-done.9 = f32[8,128]{1,0:T(8,128)S(1)} collective-permute-done((f32[8,128]{1,0:T(8,128)S(1)}, f32[8,128]{1,0:T(8,128)S(1)}, u32[]{:S(2)}, u32[]{:S(2)}) %collective-permute-start.9) | collective-permute-done | bytes 4128 | tf_op jit(solution)/shard_map/ppermute | solution.py:322
  110.3 3.1 %collective-permute-start.10 = (f32[8,128]{1,0:T(8,128)S(1)}, f32[8,128]{1,0:T(8,128)S(1)}, u32[]{:S(2)}, u32[]{:S(2)}) collective-permute-start(f32[8,128]{1,0:T(8,128)S(1)} %add.24), channel_id=1, source_target_pairs={{0,128},{4,132},{8,136},{12,140},{16,144},{20,148},{24,152},{28,15... | collective-permute-start | bytes 12296 | tf_op jit(solution)/shard_map/ppermute | solution.py:322
  113.4 2.0 %collective-permute-done.10 = f32[8,128]{1,0:T(8,128)S(1)} collective-permute-done((f32[8,128]{1,0:T(8,128)S(1)}, f32[8,128]{1,0:T(8,128)S(1)}, u32[]{:S(2)}, u32[]{:S(2)}) %collective-permute-start.10) | collective-permute-done | bytes 4128 | tf_op jit(solution)/shard_map/ppermute | solution.py:322
  115.4 0.9 collective-permute-start.11
  116.3 2.7 %collective-permute-done.11 = f32[8,128]{1,0:T(8,128)S(1)} collective-permute-done((f32[8,128]{1,0:T(8,128)S(1)}, f32[8,128]{1,0:T(8,128)S(1)}, u32[]{:S(2)}, u32[]{:S(2)}) %collective-permute-start.11) | collective-permute-done | bytes 4128 | tf_op jit(solution)/shard_map/ppermute | solution.py:322
  119.0 1.3 collective-permute-start.12
  120.3 3.2 %collective-permute-done.12 = f32[8,128]{1,0:T(8,128)S(1)} collective-permute-done((f32[8,128]{1,0:T(8,128)S(1)}, f32[8,128]{1,0:T(8,128)S(1)}, u32[]{:S(2)}, u32[]{:S(2)}) %collective-permute-start.12) | collective-permute-done | bytes 4128 | tf_op jit(solution)/shard_map/ppermute | solution.py:322
  123.5 3.0 %collective-permute-start.13 = (f32[8,128]{1,0:T(8,128)S(1)}, f32[8,128]{1,0:T(8,128)S(1)}, u32[]{:S(2)}, u32[]{:S(2)}) collective-permute-start(f32[8,128]{1,0:T(8,128)S(1)} %add.27.refs_3_), channel_id=1, source_target_pairs={{0,32},{4,36},{8,40},{12,44},{16,48},{20,52},{24,56},{28,60},{32,0... | collective-permute-start | bytes 12296 | tf_op jit(solution)/shard_map/ppermute | solution.py:322
  126.5 3.6 %shard_map.57.refs_4_ = f32[256,1280]{1,0:T(8,128)S(1)} custom-call(s32[1]{0:T(128)} %bitcast.col_ref, f32[128,640]{1,0:T(8,128)S(1)} %reshape.18.refs_0_, f32[128,640]{1,0:T(8,128)S(1)} %reshape.19.refs_1_, bf16[2560,1280]{1,0:T(8,128)(2,1)} %bitcast.16), custom_call_target="tpu_custom_call" | custom-call | tf_op jit(solution)/shard_map/pallas_call | solution.py:273
  130.2 5.0 %shard_map.58 = (f32[256,1280]{1,0:T(8,128)S(1)}, bf16[640,1280]{1,0:T(8,128)(2,1)S(1)}) custom-call(s32[1]{0:T(128)} %bitcast.col_ref, f32[128,640]{1,0:T(8,128)S(1)} %collective-permute-done.refs_0_, f32[128,640]{1,0:T(8,128)S(1)} %collective-permute-done.4.refs_1_, f32[128,640]{1,0:T(8,128)S(1)} %collective-permute-done.5.refs_2_, ...), custom_call_target="tpu_custom_call" | custom-call | tf_op jit(solution)/shard_map/pallas_call | solution.py:273
  135.2 2.1 %shard_map.59 = f32[256,1280]{1,0:T(8,128)} custom-call(s32[1]{0:T(128)} %bitcast.col_ref, f32[128,640]{1,0:T(8,128)S(1)} %collective-permute-done.1.refs_0_, f32[128,640]{1,0:T(8,128)S(1)} %collective-permute-done.3.refs_1_, f32[256,1280]{1,0:T(8,128)S(1)} %get-tuple-element.7.refs_2_, f32[8,128]{1,0:T(8,128)S(1)} %add.27.refs_3_, ...), custom_call_target="tpu_custom_call" | custom-call | tf_op jit(solution)/shard_map/pallas_call | solution.py:273
  (26 shorter events, 4.0 us)
Async XLA Ops:
  2.6 46.2 %all-to-all-start = ((f32[64,1,5248]{2,1,0:T(1,128)}), f32[64,1,5248]{2,1,0:T(1,128)S(1)}, u32[]{:S(2)}, u32[]{:S(2)}) async-start(f32[64,1,5248]{2,1,0:T(1,128)} %bitcast.4), calls=%async_computation | async-start | bytes 2686976 | tf_op jit(solution)/shard_map/all_to_all | solution.py:289
  49.3 29.0 %copy-start = (bf16[1,432,2560]{2,1,0:T(8,128)(2,1)S(1)}, bf16[1,432,2560]{2,1,0:T(8,128)(2,1)}, u32[]{:S(2)}) copy-start(bf16[1,432,2560]{2,1,0:T(8,128)(2,1)} %acts_ref.1) | copy-start | bytes 6635524
  76.3 12.2 %collective-permute-start = (f32[128,640]{1,0:T(8,128)S(1)}, f32[128,640]{1,0:T(8,128)S(1)}, u32[]{:S(2)}, u32[]{:S(2)}) collective-permute-start(f32[128,640]{1,0:T(8,128)S(1)} %reshape.18.refs_0_), channel_id=1, source_target_pairs={{0,1},{1,2},{2,3},{3,0},{4,5},{5,6},{6,7},{7,4},{8,9},{9,10},{10,1... | collective-permute-start | bytes 983048 | tf_op jit(solution)/shard_map/ppermute | solution.py:285
  76.6 14.2 %collective-permute-start.2 = (f32[128,640]{1,0:T(8,128)S(1)}, f32[128,640]{1,0:T(8,128)S(1)}, u32[]{:S(2)}, u32[]{:S(2)}) collective-permute-start(f32[128,640]{1,0:T(8,128)S(1)} %reshape.19.refs_1_), channel_id=1, source_target_pairs={{0,3},{1,0},{2,1},{3,2},{4,7},{5,4},{6,5},{7,6},{8,11},{9,8},{10,9... | collective-permute-start | bytes 983048 | tf_op jit(solution)/shard_map/ppermute | solution.py:285
  85.6 5.1 %collective-permute-start.6 = (f32[8,128]{1,0:T(8,128)S(1)}, f32[8,128]{1,0:T(8,128)S(1)}, u32[]{:S(2)}, u32[]{:S(2)}) collective-permute-start(f32[8,128]{1,0:T(8,128)S(1)} %broadcast_in_dim.18), channel_id=1, source_target_pairs={{0,1},{1,0},{2,3},{3,2},{4,5},{5,4},{6,7},{7,6},{8,9},{9,8},{10,11... | collective-permute-start | bytes 12296 | tf_op jit(solution)/shard_map/ppermute | solution.py:322
  86.5 43.7 %collective-permute-start.4 = (f32[128,640]{1,0:T(8,128)S(1)}, f32[128,640]{1,0:T(8,128)S(1)}, u32[]{:S(2)}, u32[]{:S(2)}) collective-permute-start(f32[128,640]{1,0:T(8,128)S(1)} %reshape.19.refs_1_), channel_id=1, source_target_pairs={{0,1},{1,2},{2,3},{3,0},{4,5},{5,6},{6,7},{7,4},{8,9},{9,10},{10,1... | collective-permute-start | bytes 983048 | tf_op jit(solution)/shard_map/ppermute | solution.py:285
  87.5 42.7 %collective-permute-start.5 = (f32[128,640]{1,0:T(8,128)S(1)}, f32[128,640]{1,0:T(8,128)S(1)}, u32[]{:S(2)}, u32[]{:S(2)}) collective-permute-start(f32[128,640]{1,0:T(8,128)S(1)} %reshape.18.refs_0_), channel_id=1, source_target_pairs={{0,3},{1,0},{2,1},{3,2},{4,7},{5,4},{6,5},{7,6},{8,11},{9,8},{10,9... | collective-permute-start | bytes 983048 | tf_op jit(solution)/shard_map/ppermute | solution.py:285
  88.5 46.7 %collective-permute-start.1 = (f32[128,640]{1,0:T(8,128)S(1)}, f32[128,640]{1,0:T(8,128)S(1)}, u32[]{:S(2)}, u32[]{:S(2)}) collective-permute-start(f32[128,640]{1,0:T(8,128)S(1)} %collective-permute-done.refs_0_), channel_id=1, source_target_pairs={{0,1},{1,2},{2,3},{3,0},{4,5},{5,6},{6,7},{7,4},{8,9},{9,10},{10,1... | collective-permute-start | bytes 983048 | tf_op jit(solution)/shard_map/ppermute | solution.py:285
  90.8 44.5 %collective-permute-start.3 = (f32[128,640]{1,0:T(8,128)S(1)}, f32[128,640]{1,0:T(8,128)S(1)}, u32[]{:S(2)}, u32[]{:S(2)}) collective-permute-start(f32[128,640]{1,0:T(8,128)S(1)} %collective-permute-done.2.refs_3_), channel_id=1, source_target_pairs={{0,3},{1,0},{2,1},{3,2},{4,7},{5,4},{6,5},{7,6},{8,11},{9,8},{10,9... | collective-permute-start | bytes 983048 | tf_op jit(solution)/shard_map/ppermute | solution.py:285
  91.4 13.3 %collective-permute-start.7 = (f32[8,128]{1,0:T(8,128)S(1)}, f32[8,128]{1,0:T(8,128)S(1)}, u32[]{:S(2)}, u32[]{:S(2)}) collective-permute-start(f32[8,128]{1,0:T(8,128)S(1)} %broadcast_add_fusion), channel_id=1, source_target_pairs={{0,2},{1,3},{2,0},{3,1},{4,6},{5,7},{6,4},{7,5},{8,10},{9,11},{10,... | collective-permute-start | bytes 12296 | tf_op jit(solution)/shard_map/ppermute | solution.py:322
  105.4 1.3 collective-permute-start.8
  106.7 3.6 %collective-permute-start.9 = (f32[8,128]{1,0:T(8,128)S(1)}, f32[8,128]{1,0:T(8,128)S(1)}, u32[]{:S(2)}, u32[]{:S(2)}) collective-permute-start(f32[8,128]{1,0:T(8,128)S(1)} %add.23), channel_id=1, source_target_pairs={{0,64},{4,68},{8,72},{12,76},{16,80},{20,84},{24,88},{28,92},{32,9... | collective-permute-start | bytes 12296 | tf_op jit(solution)/shard_map/ppermute | solution.py:322
  110.3 5.1 %collective-permute-start.10 = (f32[8,128]{1,0:T(8,128)S(1)}, f32[8,128]{1,0:T(8,128)S(1)}, u32[]{:S(2)}, u32[]{:S(2)}) collective-permute-start(f32[8,128]{1,0:T(8,128)S(1)} %add.24), channel_id=1, source_target_pairs={{0,128},{4,132},{8,136},{12,140},{16,144},{20,148},{24,152},{28,15... | collective-permute-start | bytes 12296 | tf_op jit(solution)/shard_map/ppermute | solution.py:322
  115.4 3.6 %collective-permute-start.11 = (f32[8,128]{1,0:T(8,128)S(1)}, f32[8,128]{1,0:T(8,128)S(1)}, u32[]{:S(2)}, u32[]{:S(2)}) collective-permute-start(f32[8,128]{1,0:T(8,128)S(1)} %add.25), channel_id=1, source_target_pairs={{0,8},{4,12},{8,0},{12,4},{16,24},{20,28},{24,16},{28,20},{32,40},... | collective-permute-start | bytes 12296 | tf_op jit(solution)/shard_map/ppermute | solution.py:322
  119.0 4.5 %collective-permute-start.12 = (f32[8,128]{1,0:T(8,128)S(1)}, f32[8,128]{1,0:T(8,128)S(1)}, u32[]{:S(2)}, u32[]{:S(2)}) collective-permute-start(f32[8,128]{1,0:T(8,128)S(1)} %add.26), channel_id=1, source_target_pairs={{0,16},{4,20},{8,24},{12,28},{16,0},{20,4},{24,8},{28,12},{32,48},... | collective-permute-start | bytes 12296 | tf_op jit(solution)/shard_map/ppermute | solution.py:322
  123.5 11.7 %collective-permute-start.13 = (f32[8,128]{1,0:T(8,128)S(1)}, f32[8,128]{1,0:T(8,128)S(1)}, u32[]{:S(2)}, u32[]{:S(2)}) collective-permute-start(f32[8,128]{1,0:T(8,128)S(1)} %add.27.refs_3_), channel_id=1, source_target_pairs={{0,32},{4,36},{8,40},{12,44},{16,48},{20,52},{24,56},{28,60},{32,0... | collective-permute-start | bytes 12296 | tf_op jit(solution)/shard_map/ppermute | solution.py:322
